TPU v7x, 32 devices: a whole 2x2x4 slice. The times are simulated.
32 devices in a mesh: dp: 2 (over y), row: 4 (over z), col: 4 (over x, core).
Axes of the slice: x: 2, y: 2, z: 4, core: 2. Of those that a mesh axis runs over, the one named last changes fastest.
Arguments:
- block_input: bfloat16 [1024, 1024], P(('dp', 'row'), 'col'), may hold values from -6 to 6
- cotangent: bfloat16 [1024, 1024], P(('dp', 'row'), 'col'), may hold values from -6 to 6
- first_gain: float32 [2, 1024], P(None, 'col'), may hold values from 0.1 to 1.9
- first_shift: float32 [2, 1024], P(None, 'col'), may hold values from -1.75 to 1.75
- joined_weight: bfloat16 [2, 1024, 3072], P(None, 'col', 'row'), may hold values from -0.1875 to 0.1875
- query_bias: float32 [2, 1024], P(None, 'row'), may hold values from -3 to 3
- value_bias: float32 [2, 1024], P(None, 'row'), may hold values from -3 to 3
- output_weight: bfloat16 [2, 1024, 1024], P(None, 'row', 'col'), may hold values from -0.75 to 0.75
- output_bias: float32 [2, 1024], P(None, 'col'), may hold values from -1.75 to 1.75
- second_gain: float32 [2, 1024], P(None, 'col'), may hold values from 0.1 to 1.9
- second_shift: float32 [2, 1024], P(None, 'col'), may hold values from -1.75 to 1.75
- upward_weight: bfloat16 [2, 1024, 4096], P(None, 'col', 'row'), may hold values from -0.1875 to 0.1875
- upward_bias: float32 [2, 4096], P(None, 'row'), may hold values from -3 to 3
- downward_weight: bfloat16 [2, 4096, 1024], P(None, 'row', 'col'), may hold values from -0.09375 to 0.09375
- downward_bias: float32 [2, 1024], P(None, 'col'), may hold values from -1.75 to 1.75
Outputs:
- block_output: bfloat16 [1024, 1024], P(('dp', 'row'), 'col')
- input_gradient: float32 [1024, 1024], P(('dp', 'row'), 'col')
- first_gain_gradient: float32 [2, 1024], P(None, 'col')
- first_shift_gradient: float32 [2, 1024], P(None, 'col')
- joined_weight_gradient: float32 [2, 1024, 3072], P(None, 'col', 'row')
- query_bias_gradient: float32 [2, 1024], P(None, 'row')
- value_bias_gradient: float32 [2, 1024], P(None, 'row')
- output_weight_gradient: float32 [2, 1024, 1024], P(None, 'row', 'col')
- output_bias_gradient: float32 [2, 1024], P(None, 'col')
- second_gain_gradient: float32 [2, 1024], P(None, 'col')
- second_shift_gradient: float32 [2, 1024], P(None, 'col')
- upward_weight_gradient: float32 [2, 1024, 4096], P(None, 'col', 'row')
- upward_bias_gradient: float32 [2, 4096], P(None, 'row')
- downward_weight_gradient: float32 [2, 4096, 1024], P(None, 'row', 'col')
- downward_bias_gradient: float32 [2, 1024], P(None, 'col')
All inputs are finite; a program needn't handle non-finite values.
Results may differ from a plain program's by a relative error of at most 0.029.
Values may be sent and summed in bfloat16 or wider, within the bound.
No kernel may reach another device: no remote copies, remote signals or barrier semaphores. Data moves between devices by JAX's collectives and lax.ppermute only.
A program may use at most 64 MiB of HBM per device.

v0:
```python
import math

import jax
import jax.numpy as jnp
from jax import lax
from jax.experimental import pallas as pl
from jax.experimental.pallas import tpu as pltpu
from jax.sharding import PartitionSpec as P


H = 16
HD = 64
LAYERS = 2

VMEM_LIMIT = 16 * 1024 * 1024

norm_epsilon = 1e-05
gelu_coef = 0.044715
gelu_scale = math.sqrt(2.0 / math.pi)
masked_score = -1e30


def int_log2(value):
    return value.bit_length() - 1


def axis_swap(local, axis, step):
    size = lax.axis_size(axis)
    return lax.ppermute(local, axis, [(place, place ^ step) for place in range(size)])


def spread(local, axis):
    size = lax.axis_size(axis)
    return [local] + [axis_swap(local, axis, step) for step in range(1, size)]


def trade(blocks, axis):
    return [blocks[0]] + [axis_swap(blocks[step], axis, step) for step in range(1, len(blocks))]


def relay(sends, axis):
    size = lax.axis_size(axis)
    got = {}
    step = size // 2
    while step:
        arrived = {place ^ step: axis_swap(got[place], axis, step) for place in sorted(got)}
        arrived[step] = axis_swap(sends[step], axis, step)
        got.update(arrived)
        step //= 2
    return [got[place] for place in range(1, size)]


def sends_of(size):
    steps = []
    step = 1
    while step < size:
        steps.append(step)
        step *= 2
    return steps


def relay_all(local, axis):
    return [local] + relay({step: local for step in sends_of(lax.axis_size(axis))}, axis)


def high_bit(place):
    return 1 << int_log2(place)


def tree_sum(parts):
    parts = list(parts)
    while len(parts) > 1:
        parts = [parts[at] + parts[at + 1] for at in range(0, len(parts), 2)]
    return parts[0]


def dot(left, right):
    return lax.dot_general(left, right, (((1,), (0,)), ((), ())), preferred_element_type=jnp.float32)


def dot_right(left, right):
    return lax.dot_general(left, right, (((1,), (1,)), ((), ())), preferred_element_type=jnp.float32)


def dot_left(left, right):
    return lax.dot_general(left, right, (((0,), (0,)), ((), ())), preferred_element_type=jnp.float32)


def low(values):
    return values.astype(jnp.bfloat16)


def wide(values):
    return values.astype(jnp.float32)


def shaped(shape, dtype):
    return jax.ShapeDtypeStruct(shape, dtype)


BF = jnp.bfloat16
F32 = jnp.float32


SMEM = pl.BlockSpec(memory_space=pltpu.SMEM)
VMEM = pl.BlockSpec(memory_space=pltpu.VMEM)
ANY = pl.BlockSpec(memory_space=pl.ANY)


def run(kernel, scalars, arrays, outs, scratch=()):
    return pl.pallas_call(
        kernel,
        in_specs=[SMEM] * len(scalars) + [VMEM] * len(arrays),
        out_specs=[VMEM] * len(outs),
        out_shape=outs,
        scratch_shapes=list(scratch),
        compiler_params=pltpu.CompilerParams(vmem_limit_bytes=VMEM_LIMIT),
    )(*scalars, *arrays)


def vector_row(vecs, at):
    return jnp.concatenate([vec[at : at + 1, :] for vec in vecs], axis=1)


def norm_into(resid, gain, shift, input_ref, normed_ref, scale_ref):
    mean = jnp.mean(resid, axis=1, keepdims=True)
    spread_out = jnp.mean(resid * resid, axis=1, keepdims=True) - mean * mean
    scale = lax.rsqrt(spread_out + norm_epsilon)
    normed = (resid - mean) * scale
    normed_ref[...] = normed
    scale_ref[...] = jnp.broadcast_to(scale, scale_ref.shape)
    input_ref[...] = low(normed * gain + shift)


def start_blocks(block_input, cotangent, vectors, size):
    rows = block_input.shape[0] // size
    width = block_input.shape[1]

    def kernel(input_ref, cotangent_ref, *refs):
        vector_refs = refs[: len(vectors)]
        outs = refs[len(vectors) :]
        for step in range(size):
            outs[step][:, :width] = input_ref[step * rows : (step + 1) * rows, :]
            outs[step][:, width:] = cotangent_ref[step * rows : (step + 1) * rows, :]
        for at, ref in enumerate(vector_refs):
            outs[size][LAYERS * at : LAYERS * (at + 1), :] = ref[...]

    outs = run(
        kernel,
        [],
        [block_input, cotangent, *vectors],
        [shaped((rows, 2 * width), BF)] * size + [shaped((LAYERS * len(vectors), width), F32)],
    )
    return outs[:size], outs[size]


def turn_blocks(blocks, place):
    size = len(blocks)

    def kernel(place_ref, *refs):
        block_refs, out_refs, turn = refs[:size], refs[size : 2 * size], refs[2 * size]
        for at in range(size):
            turn[at] = block_refs[at][...]
        for at in range(size):
            out_refs[at][...] = turn[at ^ place_ref[0] ^ place_ref[1]]

    shape, dtype = blocks[0].shape, blocks[0].dtype
    return run(
        kernel,
        [place],
        list(blocks),
        [shaped(shape, dtype)] * size,
        [pltpu.VMEM((size,) + shape, dtype)],
    )


def pack_weights(joined, output, upward, downward, layer, first):
    width = joined.shape[1]
    pieces = []
    if first:
        pieces.append((0, (layer, slice(None)), joined.shape[2]))
        pieces.append((1, (layer, slice(None)), output.shape[2]))
        arrays = [joined, output]
    else:
        pieces.append((0, (layer, slice(None)), upward.shape[2]))
        for at in range(downward.shape[1] // width):
            pieces.append((1, (layer, slice(at * width, (at + 1) * width)), downward.shape[2]))
        arrays = [upward, downward]
    total = sum(piece[2] for piece in pieces)

    def kernel(one_ref, two_ref, out_ref, sems):
        copies = []
        at = 0
        for slot, (which, index, columns) in enumerate(pieces):
            ref = (one_ref, two_ref)[which]
            copies.append(
                pltpu.make_async_copy(
                    ref.at[index], out_ref.at[:, at : at + columns], sems.at[slot]
                )
            )
            at += columns
        for copy in copies:
            copy.start()
        for copy in copies:
            copy.wait()

    return pl.pallas_call(
        kernel,
        name="pack_weights",
        in_specs=[ANY] * 2,
        out_specs=ANY,
        out_shape=shaped((width, total), BF),
        scratch_shapes=[pltpu.SemaphoreType.DMA((len(pieces),))],
        compiler_params=pltpu.CompilerParams(vmem_limit_bytes=VMEM_LIMIT),
    )(*arrays)


def first_norm(got, vecs):
    size = len(got)
    rows, width = got[0].shape[0], got[0].shape[1] // 2

    def kernel(*refs):
        got_refs = refs[:size]
        vec_refs = refs[size : size + len(vecs)]
        resid_ref, cotangent_ref, input_ref, normed_ref, scale_ref = refs[size + len(vecs) :]
        whole = [ref[...] for ref in got_refs]
        resid = jnp.concatenate([wide(part[:, :width]) for part in whole], axis=1)
        cotangent_ref[...] = jnp.concatenate([part[:, width:] for part in whole], axis=1)
        resid_ref[...] = resid
        norm_into(
            resid,
            vector_row(vec_refs, GAIN_ONE * LAYERS),
            vector_row(vec_refs, SHIFT_ONE * LAYERS),
            input_ref,
            normed_ref,
            scale_ref,
        )

    full = size * width
    return run(
        kernel,
        [],
        [*got, *vecs],
        [
            shaped((rows, full), F32),
            shaped((rows, full), BF),
            shaped((rows, full), BF),
            shaped((rows, full), F32),
            shaped((rows, 128), F32),
        ],
    )


def next_norm(resid, parts, vecs, layer, bias_at, gain_at, shift_at):
    count = len(parts)
    next_layer = layer + 1 if gain_at == GAIN_ONE else layer

    def kernel(resid_ref, *refs):
        part_refs = refs[:count]
        vec_refs = refs[count : count + len(vecs)]
        out_ref, input_ref, normed_ref, scale_ref = refs[count + len(vecs) :]
        total = tree_sum([wide(ref[...]) for ref in part_refs])
        resid = resid_ref[...] + total + vector_row(vec_refs, bias_at * LAYERS + layer)
        out_ref[...] = resid
        norm_into(
            resid,
            vector_row(vec_refs, gain_at * LAYERS + next_layer),
            vector_row(vec_refs, shift_at * LAYERS + next_layer),
            input_ref,
            normed_ref,
            scale_ref,
        )

    rows, full = resid.shape
    return run(
        kernel,
        [],
        [resid, *parts, *vecs],
        [
            shaped((rows, full), F32),
            shaped((rows, full), BF),
            shaped((rows, full), F32),
            shaped((rows, 128), F32),
        ],
    )


def cut_rows(value, refs):
    rows = refs[0].shape[0]
    for at, ref in enumerate(refs):
        ref[...] = value[at * rows : (at + 1) * rows]


def cut_columns(value, refs):
    width = refs[0].shape[1]
    for at, ref in enumerate(refs):
        ref[...] = value[:, at * width : (at + 1) * width]


def gathered(refs):
    return jnp.concatenate([ref[...] for ref in refs], axis=0)


def attention_forward(blocks, packs, query_bias, value_bias, slopes, place, layer):
    size, cols = len(blocks), len(packs)
    rows, full = blocks[0].shape
    length = size * rows
    width = full // cols
    across = query_bias.shape[1]
    heads = across // HD
    shift = int_log2(rows)

    def kernel(place_ref, slopes_ref, *refs):
        block_refs = refs[:size]
        pack_refs = refs[size : size + cols]
        query_bias_ref, value_bias_ref = refs[size + cols : size + cols + 2]
        all_ref, qkv_ref, probs_ref, mixed_ref = refs[size + cols + 2 : size + cols + 6]
        part_refs = refs[size + cols + 6 :]
        full_first = gathered(block_refs)
        all_ref[...] = full_first
        joined = tree_sum(
            [
                dot(full_first[:, at * width : (at + 1) * width], pack_refs[at][:, : 3 * across])
                for at in range(cols)
            ]
        )
        turn = place_ref[0] ^ place_ref[1]

        def where_is(axis):
            index = lax.broadcasted_iota(jnp.int32, (length, length), axis)
            return ((lax.shift_right_logical(index, shift) ^ turn) << shift) + (index & (rows - 1))

        offset = wide(where_is(1) - where_is(0))
        allowed = offset <= 0.0
        for head in range(heads):
            at = head * 3 * HD
            here = slice(head * HD, (head + 1) * HD)
            query = low(joined[:, at : at + HD] + query_bias_ref[layer : layer + 1, here])
            keys = low(joined[:, at + HD : at + 2 * HD])
            values = low(
                joined[:, at + 2 * HD : at + 3 * HD] + value_bias_ref[layer : layer + 1, here]
            )
            qkv_ref[:, at : at + HD] = query
            qkv_ref[:, at + HD : at + 2 * HD] = keys
            qkv_ref[:, at + 2 * HD : at + 3 * HD] = values
            scores = dot_right(query, keys) * (1.0 / math.sqrt(HD)) + slopes_ref[head] * offset
            scores = jnp.where(allowed, scores, masked_score)
            top = jnp.max(scores, axis=1, keepdims=True)
            log_total = top + jnp.log(jnp.sum(jnp.exp(scores - top), axis=1, keepdims=True))
            probs = jnp.exp(scores - log_total)
            probs_ref[head] = probs
            mixed_ref[:, here] = low(dot(low(probs), values))
        mixed = mixed_ref[...]
        partial = jnp.concatenate(
            [low(dot(mixed, pack_ref[:, 3 * across : 3 * across + width])) for pack_ref in pack_refs],
            axis=1,
        )
        cut_rows(partial, part_refs)

    outs = run(
        kernel,
        [place, slopes],
        [*blocks, *packs, query_bias, value_bias],
        [
            shaped((length, full), BF),
            shaped((length, 3 * across), BF),
            shaped((heads, length, length), F32),
            shaped((length, across), BF),
        ]
        + [shaped((rows, full), BF)] * size,
    )
    return outs[:4], outs[4:]


def bundle_into(refs, steps, shared, addressed, width):
    for at, ref in enumerate(refs):
        first = steps[at - 1] if at else 0
        count = first if at else 1
        column = 0
        for value in shared:
            ref[:, column : column + value.shape[1]] = value
            column += value.shape[1]
        for place in range(first, first + count):
            for value in addressed:
                ref[:, column : column + width] = value[:, place * width : (place + 1) * width]
                column += width


def bundle_shapes(length, steps, shared, addressed, width):
    counts = [1] + list(steps)
    return [shaped((length, shared + count * addressed * width), BF) for count in counts]


def feed_forward(blocks, packs, upward_bias, first_all, mixed, layer):
    size, cols = len(blocks), len(packs)
    rows, full = blocks[0].shape
    length = size * rows
    width = full // cols
    units = upward_bias.shape[1]
    across = mixed.shape[1]
    steps = sends_of(cols)

    def kernel(*refs):
        block_refs = refs[:size]
        pack_refs = refs[size : size + cols]
        bias_ref, first_ref, mixed_ref, slope_ref = refs[size + cols : size + cols + 4]
        part_refs = refs[size + cols + 4 : 2 * size + cols + 4]
        send_refs = refs[2 * size + cols + 4 :]
        full_second = gathered(block_refs)
        pre_act = tree_sum(
            [
                dot(full_second[:, at * width : (at + 1) * width], pack_refs[at][:, :units])
                for at in range(cols)
            ]
        )
        pre_act = pre_act + bias_ref[layer : layer + 1, :]
        inner = gelu_scale * (pre_act + gelu_coef * pre_act * pre_act * pre_act)
        tangent = jnp.tanh(inner)
        hidden = low(0.5 * pre_act * (1.0 + tangent))
        slope_ref[...] = 0.5 * (1.0 + tangent) + 0.5 * pre_act * (
            1.0 - tangent * tangent
        ) * gelu_scale * (1.0 + 3.0 * gelu_coef * pre_act * pre_act)
        partial = jnp.concatenate(
            [
                low(
                    tree_sum(
                        [
                            dot(
                                hidden[:, at : at + width],
                                pack_ref[:, units + at : units + at + width],
                            )
                            for at in range(0, units, width)
                        ]
                    )
                )
                for pack_ref in pack_refs
            ],
            axis=1,
        )
        cut_rows(partial, part_refs)
        bundle_into(
            send_refs, steps, [mixed_ref[...], hidden], [first_ref[...], full_second], width
        )

    outs = run(
        kernel,
        [],
        [*blocks, *packs, upward_bias, first_all, mixed],
        [shaped((length, units), F32)]
        + [shaped((rows, full), BF)] * size
        + bundle_shapes(length, steps, across + units, 2, width),
    )
    return outs[0], outs[1 : 1 + size], outs[1 + size :]


def feed_backward(blocks, packs, slope):
    size, cols = len(blocks), len(packs)
    rows, full = blocks[0].shape
    length = size * rows
    width = full // cols
    units = slope.shape[1]
    steps = sends_of(cols)

    def kernel(*refs):
        block_refs = refs[:size]
        pack_refs = refs[size : size + cols]
        slope_ref = refs[size + cols]
        part_refs = refs[size + cols + 1 : 2 * size + cols + 1]
        send_refs = refs[2 * size + cols + 1 :]
        full_grad = gathered(block_refs)
        grad_hidden = jnp.concatenate(
            [
                tree_sum(
                    [
                        dot_right(
                            full_grad[:, place * width : (place + 1) * width],
                            pack_refs[place][:, units + at : units + at + width],
                        )
                        for place in range(cols)
                    ]
                )
                for at in range(0, units, width)
            ],
            axis=1,
        )
        grad_pre = low(grad_hidden * slope_ref[...])
        partial = jnp.concatenate(
            [low(dot_right(grad_pre, pack_ref[:, :units])) for pack_ref in pack_refs], axis=1
        )
        cut_rows(partial, part_refs)
        bundle_into(send_refs, steps, [grad_pre], [full_grad], width)

    outs = run(
        kernel,
        [],
        [*blocks, *packs, slope],
        [shaped((rows, full), BF)] * size + bundle_shapes(length, steps, units, 1, width),
    )
    return outs[:size], outs[size:]


def norm_backward(grad_resid, parts, normed, scale, vecs, layer, gain_at, extra):
    count = len(parts)
    rows, full = grad_resid.shape

    def kernel(grad_ref, normed_ref, scale_ref, *refs):
        part_refs = refs[:count]
        vec_refs = refs[count : count + len(vecs)]
        out_ref, low_ref, sums_ref = refs[count + len(vecs) :]
        grad_in = wide(grad_ref[...])
        grad_out = tree_sum([wide(ref[...]) for ref in part_refs])
        normed = normed_ref[...]
        grad_normed = grad_out * vector_row(vec_refs, gain_at * LAYERS + layer)
        first = jnp.mean(grad_normed, axis=1, keepdims=True)
        second = jnp.mean(grad_normed * normed, axis=1, keepdims=True)
        total = grad_in + scale_ref[:, :1] * (grad_normed - first - normed * second)
        out_ref[...] = total
        low_ref[...] = low(total)
        sums_ref[0:1, :] = jnp.sum(grad_out * normed, axis=0, keepdims=True)
        sums_ref[1:2, :] = jnp.sum(grad_out, axis=0, keepdims=True)
        if extra:
            sums_ref[2:3, :] = jnp.sum(total, axis=0, keepdims=True)
            sums_ref[3:4, :] = jnp.sum(grad_in, axis=0, keepdims=True)

    return run(
        kernel,
        [],
        [grad_resid, normed, scale, *parts, *vecs],
        [
            shaped((rows, full), F32),
            shaped((rows, full), BF),
            shaped((4 if extra else 2, full), F32),
        ],
    )


def attention_backward(blocks, packs, qkv, probs, mixed):
    size, cols = len(blocks), len(packs)
    rows, full = blocks[0].shape
    length = size * rows
    width = full // cols
    across = mixed.shape[1]
    heads = across // HD
    steps = sends_of(cols)
    factor = 1.0 / math.sqrt(HD)

    def kernel(*refs):
        block_refs = refs[:size]
        pack_refs = refs[size : size + cols]
        qkv_ref, probs_ref, mixed_ref = refs[size + cols : size + cols + 3]
        part_refs = refs[size + cols + 3 : 2 * size + cols + 3]
        send_refs = refs[2 * size + cols + 3 :]
        joined_ref = send_refs[0]
        full_middle = gathered(block_refs)
        grad_mixed = low(
            tree_sum(
                [
                    dot_right(
                        full_middle[:, at * width : (at + 1) * width],
                        pack_refs[at][:, 3 * across : 3 * across + width],
                    )
                    for at in range(cols)
                ]
            )
        )
        for head in range(heads):
            at = head * 3 * HD
            here = slice(head * HD, (head + 1) * HD)
            query = qkv_ref[:, at : at + HD]
            keys = qkv_ref[:, at + HD : at + 2 * HD]
            values = qkv_ref[:, at + 2 * HD : at + 3 * HD]
            grad_here = grad_mixed[:, here]
            probs = probs_ref[head]
            value_sum = dot_left(low(probs), grad_here)
            grad_probs = dot_right(grad_here, values)
            delta = jnp.sum(wide(grad_here) * wide(mixed_ref[:, here]), axis=1, keepdims=True)
            grad_scores = low(probs * (grad_probs - delta))
            joined_ref[:, at : at + HD] = low(dot(grad_scores, keys) * factor)
            joined_ref[:, at + HD : at + 2 * HD] = low(dot_left(grad_scores, query) * factor)
            joined_ref[:, at + 2 * HD : at + 3 * HD] = low(value_sum)
        grad_joined = joined_ref[:, : 3 * across]
        partial = jnp.concatenate(
            [low(dot_right(grad_joined, pack_ref[:, : 3 * across])) for pack_ref in pack_refs],
            axis=1,
        )
        cut_rows(partial, part_refs)
        bundle_into(send_refs, steps, [grad_joined], [full_middle], width)

    outs = run(
        kernel,
        [],
        [*blocks, *packs, qkv, probs, mixed],
        [shaped((rows, full), BF)] * size + bundle_shapes(length, steps, 3 * across, 1, width),
    )
    return outs[:size], outs[size:]


def columns_of(place, slot, shared, addressed, width):
    index = place - high_bit(place) if place else 0
    start = shared + (index * addressed + slot) * width
    return slice(start, start + width)


def feed_changes(ahead, behind, across, units, width):
    cols = len(ahead)
    shared = across + units

    def kernel(*refs):
        ahead_refs = refs[:cols]
        behind_refs = refs[cols : 2 * cols]
        out_ref, sum_ref = refs[2 * cols :]

        def rows_of(some, pick):
            return jnp.concatenate([ref[:, pick(at)] for at, ref in enumerate(some)], axis=0)

        grad_all = rows_of(behind_refs, lambda at: columns_of(at, 0, units, 1, width))
        pre_all = rows_of(behind_refs, lambda at: slice(0, units))
        second_all = rows_of(ahead_refs, lambda at: columns_of(at, 1, shared, 2, width))
        out_ref[:, :units] = low(dot_left(second_all, pre_all))
        for at in range(0, units, width):
            hidden_all = rows_of(ahead_refs, lambda _: slice(across + at, across + at + width))
            out_ref[:, units + at : units + at + width] = low(dot_left(hidden_all, grad_all))
        sum_ref[...] = jnp.sum(wide(pre_all), axis=0, keepdims=True)

    return run(
        kernel, [], [*ahead, *behind], [shaped((width, 2 * units), BF), shaped((1, units), F32)]
    )


def attention_changes(ahead, behind, across, units, width):
    cols = len(ahead)
    shared = across + units

    def kernel(*refs):
        ahead_refs = refs[:cols]
        behind_refs = refs[cols : 2 * cols]
        out_ref, sum_ref = refs[2 * cols :]

        def rows_of(some, pick):
            return jnp.concatenate([ref[:, pick(at)] for at, ref in enumerate(some)], axis=0)

        first_all = rows_of(ahead_refs, lambda at: columns_of(at, 0, shared, 2, width))
        joined_all = rows_of(behind_refs, lambda at: slice(0, 3 * across))
        middle_all = rows_of(behind_refs, lambda at: columns_of(at, 0, 3 * across, 1, width))
        mixed_all = rows_of(ahead_refs, lambda at: slice(0, across))
        out_ref[:, : 3 * across] = low(dot_left(first_all, joined_all))
        out_ref[:, 3 * across :] = low(dot_left(mixed_all, middle_all))
        sum_ref[...] = jnp.sum(wide(joined_all), axis=0, keepdims=True)

    return run(
        kernel,
        [],
        [*ahead, *behind],
        [shaped((width, 3 * across + width), BF), shaped((1, 3 * across), F32)],
    )


def finish(own, other, layer, cuts, shapes, kept):
    def kernel(own_ref, other_ref, *refs):
        out_refs = refs[len(kept or ()) :]
        for out_ref, pieces in zip(out_refs, cuts):
            row = 0
            for start, stop in pieces:
                out_ref[0, row : row + own_ref.shape[0], :] = wide(own_ref[:, start:stop]) + wide(
                    other_ref[:, start:stop]
                )
                row += own_ref.shape[0]

    def whole(array):
        return pl.BlockSpec(array.shape, lambda at: (0, 0))

    return pl.pallas_call(
        kernel,
        name="finish",
        grid=(1,),
        in_specs=[whole(own), whole(other)] + [ANY] * len(kept or ()),
        out_specs=[pl.BlockSpec((1,) + shape[1:], lambda at: (layer, 0, 0)) for shape in shapes],
        out_shape=[shaped(shape, F32) for shape in shapes],
        input_output_aliases={2 + at: at for at in range(len(kept or ()))},
        compiler_params=pltpu.CompilerParams(vmem_limit_bytes=VMEM_LIMIT),
    )(own, other, *(kept or ()))


def end_blocks(values, size):
    rows, full = values.shape
    width = full // size

    def kernel(value_ref, *out_refs):
        for at in range(size):
            out_refs[at][...] = value_ref[:, at * width : (at + 1) * width]

    return run(kernel, [], [values], [shaped((rows, width), values.dtype)] * size)


def end_place(got):
    size = len(got)
    rows, width = got[0].shape

    def kernel(*refs):
        cut = refs[size]
        for at in range(size):
            cut[at * rows : (at + 1) * rows, :] = refs[at][...]

    return run(kernel, [], list(got), [shaped((rows * size, width), got[0].dtype)])[0]


def turn_in(blocks, place):
    got = turn_blocks(trade(blocks, "row"), place)
    return trade(got, "col")


def turn_out(blocks, place):
    got = turn_blocks(trade(blocks, "col"), place)
    return end_place(trade(got, "row"))


def width_total(vectors):
    size = lax.axis_size("col")
    share = vectors.shape[1] // size
    step = size // 2
    while step:
        mine, theirs = vectors[:, : step * share], vectors[:, step * share :]
        vectors = mine + axis_swap(theirs, "col", step)
        step //= 2
    return over_dp(tree_sum(spread(vectors, "row")))


def over_dp(total):
    step = lax.axis_size("dp") // 2
    while step:
        total = total + axis_swap(total, "dp", step)
        step //= 2
    return total


def last_resid(resid, parts, vecs, layer):
    count = len(parts)

    def kernel(resid_ref, *refs):
        part_refs = refs[:count]
        vec_refs = refs[count : count + len(vecs)]
        total = tree_sum([wide(ref[...]) for ref in part_refs])
        bias = vector_row(vec_refs, BIAS_DOWN * LAYERS + layer)
        cut_columns(low(resid_ref[...] + total + bias), refs[count + len(vecs) :])

    rows, full = resid.shape
    width = full // len(vecs)
    return run(kernel, [], [resid, *parts, *vecs], [shaped((rows, width), BF)] * len(vecs))


GAIN_ONE, SHIFT_ONE, BIAS_OUT, GAIN_TWO, SHIFT_TWO, BIAS_DOWN = range(6)


def shards(
    block_input,
    cotangent,
    first_gain,
    first_shift,
    joined_weight,
    query_bias,
    value_bias,
    output_weight,
    output_bias,
    second_gain,
    second_shift,
    upward_weight,
    upward_bias,
    downward_weight,
    downward_bias,
):
    row = lax.axis_index("row")
    col = lax.axis_index("col")
    place = jnp.stack([row, col]).astype(jnp.int32)
    across = query_bias.shape[1]
    heads_here = across // HD
    units = upward_bias.shape[1]
    width = block_input.shape[1]
    size = lax.axis_size("row")
    steps = sends_of(lax.axis_size("col"))
    head_index = (row * heads_here).astype(jnp.float32) + jnp.arange(heads_here).astype(jnp.float32)
    slopes = 2.0 ** (-8.0 * (head_index + 1.0) / H)

    blocks, vectors = start_blocks(
        block_input,
        cotangent,
        [first_gain, first_shift, output_bias, second_gain, second_shift, downward_bias],
        size,
    )
    got = turn_in(blocks, place)
    vecs = relay_all(vectors, "col")
    weights = []
    for layer in range(LAYERS):
        weights.append([])
        for first in (True, False):
            pack = pack_weights(
                joined_weight, output_weight, upward_weight, downward_weight, layer, first
            )
            weights[layer].append(relay_all(pack, "col"))
    resid, grad_resid, norm_input, normed, scale = first_norm(got, vecs)
    saved = []
    for layer in range(LAYERS):
        attention_packs, feed_packs = weights[layer]
        first_kept = (normed, scale)
        (first_all, qkv, probs, mixed), parts = attention_forward(
            spread(norm_input, "row"), attention_packs, query_bias, value_bias, slopes, place, layer
        )
        middle, norm_input, normed, scale = next_norm(
            resid, trade(parts, "row"), vecs, layer, BIAS_OUT, GAIN_TWO, SHIFT_TWO
        )
        slope, parts, sends = feed_forward(
            spread(norm_input, "row"), feed_packs, upward_bias, first_all, mixed, layer
        )
        ahead = [sends[0]] + relay(dict(zip(steps, sends[1:])), "col")
        saved.append((first_kept, (normed, scale), qkv, probs, mixed, slope, ahead))
        parts = trade(parts, "row")
        if layer + 1 < LAYERS:
            resid, norm_input, normed, scale = next_norm(
                middle, parts, vecs, layer, BIAS_DOWN, GAIN_ONE, SHIFT_ONE
            )
        else:
            block_output = turn_out(last_resid(middle, parts, vecs, layer), place)

    grad_low = grad_resid
    sums = [None] * LAYERS
    lines = [None] * LAYERS
    feed_outs = attention_outs = None
    for layer in reversed(range(LAYERS)):
        attention_packs, feed_packs = weights[layer]
        first_kept, second_kept, qkv, probs, mixed, slope, ahead = saved[layer]
        parts, sends = feed_backward(spread(grad_low, "row"), feed_packs, slope)
        feed_behind = [sends[0]] + relay(dict(zip(steps, sends[1:])), "col")
        grad_middle, middle_low, second_sums = norm_backward(
            grad_resid, trade(parts, "row"), *second_kept, vecs, layer, GAIN_TWO, True
        )
        parts, sends = attention_backward(
            spread(middle_low, "row"), attention_packs, qkv, probs, mixed
        )
        attention_behind = [sends[0]] + relay(dict(zip(steps, sends[1:])), "col")
        grad_resid, grad_low, first_sums = norm_backward(
            grad_middle, trade(parts, "row"), *first_kept, vecs, layer, GAIN_ONE, False
        )
        change, pre_sum = feed_changes(ahead, feed_behind, across, units, width)
        feed_outs = finish(
            change,
            axis_swap(change, "dp", 1),
            layer,
            [[(0, units)], [(at, at + width) for at in range(units, 2 * units, width)]],
            [upward_weight.shape, downward_weight.shape],
            feed_outs,
        )
        change, joined_sum = attention_changes(ahead, attention_behind, across, units, width)
        attention_outs = finish(
            change,
            axis_swap(change, "dp", 1),
            layer,
            [[(0, 3 * across)], [(3 * across, 3 * across + width)]],
            [joined_weight.shape, output_weight.shape],
            attention_outs,
        )
        sums[layer] = (first_sums, second_sums)
        lines[layer] = (pre_sum, joined_sum)
    input_gradient = turn_out(end_blocks(grad_resid, size), place)
    vector_sums = width_total(
        jnp.concatenate([part for pair in sums for part in pair], axis=0)
    ).reshape(LAYERS, 6, width)
    line = over_dp(jnp.concatenate([part for pair in lines for part in pair], axis=1))
    line = line.reshape(LAYERS, units + 3 * across)
    per_head = line[:, units:].reshape(LAYERS, heads_here, 3, HD)
    return (
        block_output,
        input_gradient,
        vector_sums[:, 0],
        vector_sums[:, 1],
        attention_outs[0],
        per_head[:, :, 0].reshape(LAYERS, across),
        per_head[:, :, 2].reshape(LAYERS, across),
        attention_outs[1],
        vector_sums[:, 4],
        vector_sums[:, 2],
        vector_sums[:, 3],
        feed_outs[0],
        line[:, :units],
        feed_outs[1],
        vector_sums[:, 5],
    )


def solution(mesh):
    return jax.shard_map(
        shards,
        mesh=mesh,
        in_specs=(
            P(("dp", "row"), "col"),
            P(("dp", "row"), "col"),
            P(None, "col"),
            P(None, "col"),
            P(None, "col", "row"),
            P(None, "row"),
            P(None, "row"),
            P(None, "row", "col"),
            P(None, "col"),
            P(None, "col"),
            P(None, "col"),
            P(None, "col", "row"),
            P(None, "row"),
            P(None, "row", "col"),
            P(None, "col"),
        ),
        out_specs=(
            P(("dp", "row"), "col"),
            P(("dp", "row"), "col"),
            P(None, "col"),
            P(None, "col"),
            P(None, "col", "row"),
            P(None, "row"),
            P(None, "row"),
            P(None, "row", "col"),
            P(None, "col"),
            P(None, "col"),
            P(None, "col"),
            P(None, "col", "row"),
            P(None, "row"),
            P(None, "row", "col"),
            P(None, "col"),
        ),
        check_vma=False,
    )
```

profile of v0, /device:TPU:0, one launch (start us, length us, event | category | flops | bytes accessed | tf_op | source)
XLA Modules:
  0.0 399.5 jit_solution(6346557682696911529)
XLA Ops:
  3.4 3.0 collective-permute-start.22
  9.1 2.6 collective-permute-start.1
  15.2 3.7 collective-permute-done.2.refs_3_
  20.4 43.2 %collective-permute-done.7.refs_6_ = f32[12,256]{1,0:T(8,128)S(1)} collective-permute-done((f32[12,256]{1,0:T(8,128)S(1)}, f32[12,256]{1,0:T(8,128)S(1)}, u32[]{:S(2)}, u32[]{:S(2)}) %collective-permute-start.7) | collective-permute-done | bytes 12320 | tf_op jit(solution)/shard_map/ppermute | solution.py:29
  73.8 2.6 collective-permute-start.10
  77.1 4.3 %collective-permute-start.11 = (bf16[32,1024]{1,0:T(8,128)(2,1)S(1)}, bf16[32,1024]{1,0:T(8,128)(2,1)S(1)}, u32[]{:S(2)}, u32[]{:S(2)}) collective-permute-start(bf16[32,1024]{1,0:T(8,128)(2,1)S(1)} %get-tuple-element.154.refs_0_), channel_id=1, source_target_pairs={{0,12},{4,8},{8,4},{12,0},{1,13},{5,9},{9,5},{13,1},{2,14},{6,10},... | collective-permute-start | bytes 196616 | tf_op jit(solution)/shard_map/ppermute | solution.py:29
  92.9 3.2 shard_map.265
  96.2 4.4 %collective-permute-start.16 = (bf16[32,1024]{1,0:T(8,128)(2,1)S(1)}, bf16[32,1024]{1,0:T(8,128)(2,1)S(1)}, u32[]{:S(2)}, u32[]{:S(2)}) collective-permute-start(bf16[32,1024]{1,0:T(8,128)(2,1)S(1)} %get-tuple-element.157), channel_id=1, source_target_pairs={{0,8},{4,12},{8,0},{12,4},{1,9},{5,13},{9,1},{13,5},{2,10},{6,14},... | collective-permute-start | bytes 196616 | tf_op jit(solution)/shard_map/ppermute | solution.py:29
  100.6 4.8 %collective-permute-start.17 = (bf16[32,1024]{1,0:T(8,128)(2,1)S(1)}, bf16[32,1024]{1,0:T(8,128)(2,1)S(1)}, u32[]{:S(2)}, u32[]{:S(2)}) collective-permute-start(bf16[32,1024]{1,0:T(8,128)(2,1)S(1)} %get-tuple-element.158), channel_id=1, source_target_pairs={{0,12},{4,8},{8,4},{12,0},{1,13},{5,9},{9,5},{13,1},{2,14},{6,10},... | collective-permute-start | bytes 196616 | tf_op jit(solution)/shard_map/ppermute | solution.py:29
  107.9 4.4 %collective-permute-start.19 = (bf16[32,1024]{1,0:T(8,128)(2,1)S(1)}, bf16[32,1024]{1,0:T(8,128)(2,1)S(1)}, u32[]{:S(2)}, u32[]{:S(2)}) collective-permute-start(bf16[32,1024]{1,0:T(8,128)(2,1)S(1)} %get-tuple-element.160.refs_0_), channel_id=1, source_target_pairs={{0,8},{4,12},{8,0},{12,4},{1,9},{5,13},{9,1},{13,5},{2,10},{6,14},... | collective-permute-start | bytes 196616 | tf_op jit(solution)/shard_map/ppermute | solution.py:29
  112.4 5.0 %collective-permute-start.20 = (bf16[32,1024]{1,0:T(8,128)(2,1)S(1)}, bf16[32,1024]{1,0:T(8,128)(2,1)S(1)}, u32[]{:S(2)}, u32[]{:S(2)}) collective-permute-start(bf16[32,1024]{1,0:T(8,128)(2,1)S(1)} %get-tuple-element.160.refs_0_), channel_id=1, source_target_pairs={{0,12},{4,8},{8,4},{12,0},{1,13},{5,9},{9,5},{13,1},{2,14},{6,10},... | collective-permute-start | bytes 196616 | tf_op jit(solution)/shard_map/ppermute | solution.py:29
  119.6 3.0 shard_map.267
  122.7 4.5 %collective-permute-done.24.refs_1_ = bf16[32,1024]{1,0:T(8,128)(2,1)S(1)} collective-permute-done((bf16[32,1024]{1,0:T(8,128)(2,1)S(1)}, bf16[32,1024]{1,0:T(8,128)(2,1)S(1)}, u32[]{:S(2)}, u32[]{:S(2)}) %collective-permute-start.24) | collective-permute-done | bytes 65568 | tf_op jit(solution)/shard_map/ppermute | solution.py:29
  127.2 2.6 collective-permute-start.25
  129.8 3.8 collective-permute-done.25.refs_2_
  133.6 3.3 collective-permute-start.26
  136.9 2.7 collective-permute-done.26.refs_3_
  139.9 3.9 collective-permute-start.28
  144.3 3.2 collective-permute-done.28.refs_2_
  147.4 2.4 collective-permute-done.29.refs_3_
  149.9 3.1 shard_map.269
  154.3 3.0 collective-permute-start.35
  160.7 3.6 collective-permute-start.37
  165.1 3.6 collective-permute-start.52
  170.5 2.4 shard_map.271
  174.9 2.7 shard_map.275
  179.1 3.0 collective-permute-start.56
  182.3 3.8 collective-permute-done.55.refs_2_
  190.7 3.0 collective-permute-done.58.refs_2_
  195.8 2.9 shard_map.277
  207.9 2.8 collective-permute-start.64
  212.3 3.7 collective-permute-done.64.refs_2_
  217.5 3.5 shard_map.279
  226.4 2.3 collective-permute-start.43
  231.6 3.0 collective-permute-start.70
  238.2 2.4 collective-permute-done.71.refs_3_
  240.6 3.6 shard_map.281
  246.2 2.4 collective-permute-start.74
  250.4 2.7 collective-permute-done.73.refs_2_
  259.7 2.9 collective-permute-done.50.refs_3_
  266.5 8.1 %collective-permute-done.105.refs_6_ = bf16[128,1536]{1,0:T(8,128)(2,1)S(1)} collective-permute-done((bf16[128,1536]{1,0:T(8,128)(2,1)S(1)}, bf16[128,1536]{1,0:T(8,128)(2,1)S(1)}, u32[]{:S(2)}, u32[]{:S(2)}) %collective-permute-start.105) | collective-permute-done | bytes 393248 | tf_op jit(solution)/shard_map/ppermute | solution.py:29
  281.0 15.3 %collective-permute-done.76.refs_2_ = f32[32,256]{1,0:T(8,128)S(1)} collective-permute-done((f32[32,256]{1,0:T(8,128)S(1)}, f32[32,256]{1,0:T(8,128)S(1)}, u32[]{:S(2)}, u32[]{:S(2)}) %collective-permute-start.76) | collective-permute-done | bytes 32800 | tf_op jit(solution)/shard_map/ppermute | solution.py:29
  303.8 6.9 %collective-permute-done.91.refs_6_ = bf16[128,1280]{1,0:T(8,128)(2,1)} collective-permute-done((bf16[128,1280]{1,0:T(8,128)(2,1)}, bf16[128,1280]{1,0:T(8,128)(2,1)}, u32[]{:S(2)}, u32[]{:S(2)}) %collective-permute-start.91) | collective-permute-done | bytes 327712 | tf_op jit(solution)/shard_map/ppermute | solution.py:29
  314.1 3.1 shard_map.288
  326.2 2.6 collective-permute-start.80
  334.6 53.6 %collective-permute-done.107 = f32[1,3584]{1,0:T(1,128)S(1)} collective-permute-done((f32[1,3584]{1,0:T(1,128)S(1)}, f32[1,3584]{1,0:T(1,128)S(1)}, u32[]{:S(2)}, u32[]{:S(2)}) %collective-permute-start.107) | collective-permute-done | bytes 14368 | tf_op jit(solution)/shard_map/ppermute | solution.py:29
  393.6 3.0 finish.6
  396.5 3.0 finish.7
  (352 shorter events, 131.6 us)
Async XLA Ops:
  3.4 81.4 %collective-permute-start.22 = (bf16[256,2048]{1,0:T(8,128)(2,1)S(1)}, bf16[256,2048]{1,0:T(8,128)(2,1)}, u32[]{:S(2)}, u32[]{:S(2)}) collective-permute-start(bf16[256,2048]{1,0:T(8,128)(2,1)S(1)} %pack_weights.5.refs_4_), channel_id=1, source_target_pairs={{0,2},{1,3},{2,0},{3,1},{4,6},{5,7},{6,4},{7,5},{8,10},{9,11},{10,... | collective-permute-start | bytes 3145736 | tf_op jit(solution)/shard_map/ppermute | solution.py:29
  6.5 77.8 %collective-permute-start.13 = (bf16[256,1024]{1,0:T(8,128)(2,1)S(1)}, bf16[256,1024]{1,0:T(8,128)(2,1)}, u32[]{:S(2)}, u32[]{:S(2)}) collective-permute-start(bf16[256,1024]{1,0:T(8,128)(2,1)S(1)} %pack_weights.4.refs_4_), channel_id=1, source_target_pairs={{0,2},{1,3},{2,0},{3,1},{4,6},{5,7},{6,4},{7,5},{8,10},{9,11},{10,... | collective-permute-start | bytes 1572872 | tf_op jit(solution)/shard_map/ppermute | solution.py:29
  11.9 84.3 %collective-permute-start.40 = (bf16[256,2048]{1,0:T(8,128)(2,1)S(1)}, bf16[256,2048]{1,0:T(8,128)(2,1)}, u32[]{:S(2)}, u32[]{:S(2)}) collective-permute-start(bf16[256,2048]{1,0:T(8,128)(2,1)S(1)} %pack_weights.7.refs_4_), channel_id=1, source_target_pairs={{0,2},{1,3},{2,0},{3,1},{4,6},{5,7},{6,4},{7,5},{8,10},{9,11},{10,... | collective-permute-start | bytes 3145736 | tf_op jit(solution)/shard_map/ppermute | solution.py:29
  19.4 47.1 %collective-permute-start.3 = (bf16[32,512]{1,0:T(8,128)(2,1)S(1)}, bf16[32,512]{1,0:T(8,128)(2,1)S(1)}, u32[]{:S(2)}, u32[]{:S(2)}) collective-permute-start(bf16[32,512]{1,0:T(8,128)(2,1)S(1)} %get-tuple-element.149), channel_id=1, source_target_pairs={{0,1},{1,0},{2,3},{3,2},{4,5},{5,4},{6,7},{7,6},{8,9},{9,8},{10,11... | collective-permute-start | bytes 98312 | tf_op jit(solution)/shard_map/ppermute | solution.py:29
  19.5 44.1 %collective-permute-start.7 = (f32[12,256]{1,0:T(8,128)S(1)}, f32[12,256]{1,0:T(8,128)S(1)}, u32[]{:S(2)}, u32[]{:S(2)}) collective-permute-start(f32[12,256]{1,0:T(8,128)S(1)} %get-tuple-element.152.refs_4_), channel_id=1, source_target_pairs={{0,2},{1,3},{2,0},{3,1},{4,6},{5,7},{6,4},{7,5},{8,10},{9,11},{10,... | collective-permute-start | bytes 36872 | tf_op jit(solution)/shard_map/ppermute | solution.py:29
  73.8 8.3 %collective-permute-start.10 = (bf16[32,1024]{1,0:T(8,128)(2,1)S(1)}, bf16[32,1024]{1,0:T(8,128)(2,1)S(1)}, u32[]{:S(2)}, u32[]{:S(2)}) collective-permute-start(bf16[32,1024]{1,0:T(8,128)(2,1)S(1)} %get-tuple-element.154.refs_0_), channel_id=1, source_target_pairs={{0,8},{4,12},{8,0},{12,4},{1,9},{5,13},{9,1},{13,5},{2,10},{6,14},... | collective-permute-start | bytes 196616 | tf_op jit(solution)/shard_map/ppermute | solution.py:29
  84.3 23.6 %collective-permute-start.21 = (bf16[256,2048]{1,0:T(8,128)(2,1)S(1)}, bf16[256,2048]{1,0:T(8,128)(2,1)}, u32[]{:S(2)}, u32[]{:S(2)}) collective-permute-start(bf16[256,2048]{1,0:T(8,128)(2,1)S(1)} %pack_weights.5.refs_4_), channel_id=1, source_target_pairs={{0,1},{1,0},{2,3},{3,2},{4,5},{5,4},{6,7},{7,6},{8,9},{9,8},{10,11... | collective-permute-start | bytes 3145736 | tf_op jit(solution)/shard_map/ppermute | solution.py:29
  84.8 34.8 %collective-permute-start.23 = (bf16[256,2048]{1,0:T(8,128)(2,1)}, bf16[256,2048]{1,0:T(8,128)(2,1)}, u32[]{:S(2)}, u32[]{:S(2)}) collective-permute-start(bf16[256,2048]{1,0:T(8,128)(2,1)} %collective-permute-done.22.refs_6_), channel_id=1, source_target_pairs={{0,1},{1,0},{2,3},{3,2},{4,5},{5,4},{6,7},{7,6},{8,9},{9,8},{10,11... | collective-permute-start | bytes 3145736 | tf_op jit(solution)/shard_map/ppermute | solution.py:29
  86.9 20.9 %collective-permute-start.31 = (bf16[256,1024]{1,0:T(8,128)(2,1)S(1)}, bf16[256,1024]{1,0:T(8,128)(2,1)}, u32[]{:S(2)}, u32[]{:S(2)}) collective-permute-start(bf16[256,1024]{1,0:T(8,128)(2,1)S(1)} %pack_weights.6.refs_4_), channel_id=1, source_target_pairs={{0,2},{1,3},{2,0},{3,1},{4,6},{5,7},{6,4},{7,5},{8,10},{9,11},{10,... | collective-permute-start | bytes 1572872 | tf_op jit(solution)/shard_map/ppermute | solution.py:29
  96.2 9.1 %collective-permute-start.16 = (bf16[32,1024]{1,0:T(8,128)(2,1)S(1)}, bf16[32,1024]{1,0:T(8,128)(2,1)S(1)}, u32[]{:S(2)}, u32[]{:S(2)}) collective-permute-start(bf16[32,1024]{1,0:T(8,128)(2,1)S(1)} %get-tuple-element.157), channel_id=1, source_target_pairs={{0,8},{4,12},{8,0},{12,4},{1,9},{5,13},{9,1},{13,5},{2,10},{6,14},... | collective-permute-start | bytes 196616 | tf_op jit(solution)/shard_map/ppermute | solution.py:29
  105.4 59.8 %collective-permute-start.39 = (bf16[256,2048]{1,0:T(8,128)(2,1)S(1)}, bf16[256,2048]{1,0:T(8,128)(2,1)S(1)}, u32[]{:S(2)}, u32[]{:S(2)}) collective-permute-start(bf16[256,2048]{1,0:T(8,128)(2,1)S(1)} %pack_weights.7.refs_4_), channel_id=1, source_target_pairs={{0,1},{1,0},{2,3},{3,2},{4,5},{5,4},{6,7},{7,6},{8,9},{9,8},{10,11... | collective-permute-start | bytes 3145736 | tf_op jit(solution)/shard_map/ppermute | solution.py:29
  107.6 57.5 %collective-permute-start.41 = (bf16[256,2048]{1,0:T(8,128)(2,1)}, bf16[256,2048]{1,0:T(8,128)(2,1)S(1)}, u32[]{:S(2)}, u32[]{:S(2)}) collective-permute-start(bf16[256,2048]{1,0:T(8,128)(2,1)} %collective-permute-done.40.refs_6_), channel_id=1, source_target_pairs={{0,1},{1,0},{2,3},{3,2},{4,5},{5,4},{6,7},{7,6},{8,9},{9,8},{10,11... | collective-permute-start | bytes 3145736 | tf_op jit(solution)/shard_map/ppermute | solution.py:29
  107.9 9.5 %collective-permute-start.19 = (bf16[32,1024]{1,0:T(8,128)(2,1)S(1)}, bf16[32,1024]{1,0:T(8,128)(2,1)S(1)}, u32[]{:S(2)}, u32[]{:S(2)}) collective-permute-start(bf16[32,1024]{1,0:T(8,128)(2,1)S(1)} %get-tuple-element.160.refs_0_), channel_id=1, source_target_pairs={{0,8},{4,12},{8,0},{12,4},{1,9},{5,13},{9,1},{13,5},{2,10},{6,14},... | collective-permute-start | bytes 196616 | tf_op jit(solution)/shard_map/ppermute | solution.py:29
  117.3 22.6 %collective-permute-start.30 = (bf16[256,1024]{1,0:T(8,128)(2,1)S(1)}, bf16[256,1024]{1,0:T(8,128)(2,1)S(1)}, u32[]{:S(2)}, u32[]{:S(2)}) collective-permute-start(bf16[256,1024]{1,0:T(8,128)(2,1)S(1)} %pack_weights.6.refs_4_), channel_id=1, source_target_pairs={{0,1},{1,0},{2,3},{3,2},{4,5},{5,4},{6,7},{7,6},{8,9},{9,8},{10,11... | collective-permute-start | bytes 1572872 | tf_op jit(solution)/shard_map/ppermute | solution.py:29
  119.6 24.2 %collective-permute-start.32 = (bf16[256,1024]{1,0:T(8,128)(2,1)}, bf16[256,1024]{1,0:T(8,128)(2,1)S(1)}, u32[]{:S(2)}, u32[]{:S(2)}) collective-permute-start(bf16[256,1024]{1,0:T(8,128)(2,1)} %collective-permute-done.31.refs_6_), channel_id=1, source_target_pairs={{0,1},{1,0},{2,3},{3,2},{4,5},{5,4},{6,7},{7,6},{8,9},{9,8},{10,11... | collective-permute-start | bytes 1572872 | tf_op jit(solution)/shard_map/ppermute | solution.py:29
  139.9 7.5 %collective-permute-start.28 = (bf16[32,1024]{1,0:T(8,128)(2,1)S(1)}, bf16[32,1024]{1,0:T(8,128)(2,1)S(1)}, u32[]{:S(2)}, u32[]{:S(2)}) collective-permute-start(bf16[32,1024]{1,0:T(8,128)(2,1)S(1)} %get-tuple-element.168.refs_0_), channel_id=1, source_target_pairs={{0,8},{4,12},{8,0},{12,4},{1,9},{5,13},{9,1},{13,5},{2,10},{6,14},... | collective-permute-start | bytes 196616 | tf_op jit(solution)/shard_map/ppermute | solution.py:29
  160.7 8.1 %collective-permute-start.36 = (bf16[32,1024]{1,0:T(8,128)(2,1)S(1)}, bf16[32,1024]{1,0:T(8,128)(2,1)S(1)}, u32[]{:S(2)}, u32[]{:S(2)}) collective-permute-start(bf16[32,1024]{1,0:T(8,128)(2,1)S(1)} %get-tuple-element.174.refs_0_), channel_id=1, source_target_pairs={{0,4},{4,0},{8,12},{12,8},{1,5},{5,1},{9,13},{13,9},{2,6},{6,2},{1... | collective-permute-start | bytes 196616 | tf_op jit(solution)/shard_map/ppermute | solution.py:29
  160.7 8.8 %collective-permute-start.37 = (bf16[32,1024]{1,0:T(8,128)(2,1)S(1)}, bf16[32,1024]{1,0:T(8,128)(2,1)S(1)}, u32[]{:S(2)}, u32[]{:S(2)}) collective-permute-start(bf16[32,1024]{1,0:T(8,128)(2,1)S(1)} %get-tuple-element.174.refs_0_), channel_id=1, source_target_pairs={{0,8},{4,12},{8,0},{12,4},{1,9},{5,13},{9,1},{13,5},{2,10},{6,14},... | collective-permute-start | bytes 196616 | tf_op jit(solution)/shard_map/ppermute | solution.py:29
  165.1 8.5 %collective-permute-start.51 = (bf16[32,1024]{1,0:T(8,128)(2,1)S(1)}, bf16[32,1024]{1,0:T(8,128)(2,1)S(1)}, u32[]{:S(2)}, u32[]{:S(2)}) collective-permute-start(bf16[32,1024]{1,0:T(8,128)(2,1)S(1)} %get-tuple-element.189.refs_0_.grad_ref), channel_id=1, source_target_pairs={{0,4},{4,0},{8,12},{12,8},{1,5},{5,1},{9,13},{13,9},{2,6},{6,2},{1... | collective-permute-start | bytes 196616 | tf_op jit(solution)/shard_map/ppermute | solution.py:29
  165.1 8.5 %collective-permute-start.52 = (bf16[32,1024]{1,0:T(8,128)(2,1)S(1)}, bf16[32,1024]{1,0:T(8,128)(2,1)S(1)}, u32[]{:S(2)}, u32[]{:S(2)}) collective-permute-start(bf16[32,1024]{1,0:T(8,128)(2,1)S(1)} %get-tuple-element.189.refs_0_.grad_ref), channel_id=1, source_target_pairs={{0,8},{4,12},{8,0},{12,4},{1,9},{5,13},{9,1},{13,5},{2,10},{6,14},... | collective-permute-start | bytes 196616 | tf_op jit(solution)/shard_map/ppermute | solution.py:29
  177.7 8.4 %collective-permute-start.55 = (bf16[32,1024]{1,0:T(8,128)(2,1)S(1)}, bf16[32,1024]{1,0:T(8,128)(2,1)S(1)}, u32[]{:S(2)}, u32[]{:S(2)}) collective-permute-start(bf16[32,1024]{1,0:T(8,128)(2,1)S(1)} %get-tuple-element.195), channel_id=1, source_target_pairs={{0,8},{4,12},{8,0},{12,4},{1,9},{5,13},{9,1},{13,5},{2,10},{6,14},... | collective-permute-start | bytes 196616 | tf_op jit(solution)/shard_map/ppermute | solution.py:29
  207.9 8.1 %collective-permute-start.64 = (bf16[32,1024]{1,0:T(8,128)(2,1)S(1)}, bf16[32,1024]{1,0:T(8,128)(2,1)S(1)}, u32[]{:S(2)}, u32[]{:S(2)}) collective-permute-start(bf16[32,1024]{1,0:T(8,128)(2,1)S(1)} %get-tuple-element.210.refs_0_), channel_id=1, source_target_pairs={{0,8},{4,12},{8,0},{12,4},{1,9},{5,13},{9,1},{13,5},{2,10},{6,14},... | collective-permute-start | bytes 196616 | tf_op jit(solution)/shard_map/ppermute | solution.py:29
  221.0 7.7 %collective-permute-start.66 = (bf16[32,1024]{1,0:T(8,128)(2,1)S(1)}, bf16[32,1024]{1,0:T(8,128)(2,1)S(1)}, u32[]{:S(2)}, u32[]{:S(2)}) collective-permute-start(bf16[32,1024]{1,0:T(8,128)(2,1)S(1)} %get-tuple-element.213), channel_id=1, source_target_pairs={{0,4},{4,0},{8,12},{12,8},{1,5},{5,1},{9,13},{13,9},{2,6},{6,2},{1... | collective-permute-start | bytes 196616 | tf_op jit(solution)/shard_map/ppermute | solution.py:29
  226.4 8.1 %collective-permute-start.43 = (bf16[32,1024]{1,0:T(8,128)(2,1)S(1)}, bf16[32,1024]{1,0:T(8,128)(2,1)S(1)}, u32[]{:S(2)}, u32[]{:S(2)}) collective-permute-start(bf16[32,1024]{1,0:T(8,128)(2,1)S(1)} %get-tuple-element.179), channel_id=1, source_target_pairs={{0,8},{4,12},{8,0},{12,4},{1,9},{5,13},{9,1},{13,5},{2,10},{6,14},... | collective-permute-start | bytes 196616 | tf_op jit(solution)/shard_map/ppermute | solution.py:29
  228.7 35.8 %collective-permute-start.88 = (bf16[128,2304]{1,0:T(8,128)(2,1)S(1)}, bf16[128,2304]{1,0:T(8,128)(2,1)S(1)}, u32[]{:S(2)}, u32[]{:S(2)}) collective-permute-start(bf16[128,2304]{1,0:T(8,128)(2,1)S(1)} %get-tuple-element.241), channel_id=1, source_target_pairs={{0,2},{1,3},{2,0},{3,1},{4,6},{5,7},{6,4},{7,5},{8,10},{9,11},{10,... | collective-permute-start | bytes 1769480 | tf_op jit(solution)/shard_map/ppermute | solution.py:29
  236.1 27.4 %collective-permute-start.87 = (bf16[128,1792]{1,0:T(8,128)(2,1)S(1)}, bf16[128,1792]{1,0:T(8,128)(2,1)S(1)}, u32[]{:S(2)}, u32[]{:S(2)}) collective-permute-start(bf16[128,1792]{1,0:T(8,128)(2,1)S(1)} %get-tuple-element.240), channel_id=1, source_target_pairs={{0,1},{1,0},{2,3},{3,2},{4,5},{5,4},{6,7},{7,6},{8,9},{9,8},{10,11... | collective-permute-start | bytes 1376264 | tf_op jit(solution)/shard_map/ppermute | solution.py:29
  244.3 8.8 %collective-permute-start.73 = (bf16[32,1024]{1,0:T(8,128)(2,1)S(1)}, bf16[32,1024]{1,0:T(8,128)(2,1)S(1)}, u32[]{:S(2)}, u32[]{:S(2)}) collective-permute-start(bf16[32,1024]{1,0:T(8,128)(2,1)S(1)} %get-tuple-element.224), channel_id=1, source_target_pairs={{0,8},{4,12},{8,0},{12,4},{1,9},{5,13},{9,1},{13,5},{2,10},{6,14},... | collective-permute-start | bytes 196616 | tf_op jit(solution)/shard_map/ppermute | solution.py:29
  253.9 8.7 %collective-permute-start.81 = (f32[12,512]{1,0:T(8,128)S(1)}, f32[12,512]{1,0:T(8,128)S(1)}, u32[]{:S(2)}, u32[]{:S(2)}) collective-permute-start(f32[12,512]{1,0:T(8,128)S(1)} %slice.57), channel_id=1, source_target_pairs={{0,2},{1,3},{2,0},{3,1},{4,6},{5,7},{6,4},{7,5},{8,10},{9,11},{10,... | collective-permute-start | bytes 73736 | tf_op jit(solution)/shard_map/ppermute | solution.py:29
  259.7 16.8 %collective-permute-start.94 = (bf16[128,1792]{1,0:T(8,128)(2,1)S(1)}, bf16[128,1792]{1,0:T(8,128)(2,1)S(1)}, u32[]{:S(2)}, u32[]{:S(2)}) collective-permute-start(bf16[128,1792]{1,0:T(8,128)(2,1)S(1)} %get-tuple-element.247), channel_id=1, source_target_pairs={{0,1},{1,0},{2,3},{3,2},{4,5},{5,4},{6,7},{7,6},{8,9},{9,8},{10,11... | collective-permute-start | bytes 1376264 | tf_op jit(solution)/shard_map/ppermute | solution.py:29
  262.6 12.0 %collective-permute-start.105 = (bf16[128,1536]{1,0:T(8,128)(2,1)S(1)}, bf16[128,1536]{1,0:T(8,128)(2,1)S(1)}, u32[]{:S(2)}, u32[]{:S(2)}) collective-permute-start(bf16[128,1536]{1,0:T(8,128)(2,1)S(1)} %get-tuple-element.263), channel_id=1, source_target_pairs={{0,2},{1,3},{2,0},{3,1},{4,6},{5,7},{6,4},{7,5},{8,10},{9,11},{10,... | collective-permute-start | bytes 1179656 | tf_op jit(solution)/shard_map/ppermute | solution.py:29
  264.5 36.4 %collective-permute-start.95 = (bf16[128,2304]{1,0:T(8,128)(2,1)S(1)}, bf16[128,2304]{1,0:T(8,128)(2,1)S(1)}, u32[]{:S(2)}, u32[]{:S(2)}) collective-permute-start(bf16[128,2304]{1,0:T(8,128)(2,1)S(1)} %get-tuple-element.248), channel_id=1, source_target_pairs={{0,2},{1,3},{2,0},{3,1},{4,6},{5,7},{6,4},{7,5},{8,10},{9,11},{10,... | collective-permute-start | bytes 1769480 | tf_op jit(solution)/shard_map/ppermute | solution.py:29
  265.7 11.5 %collective-permute-start.75 = (f32[32,256]{1,0:T(8,128)S(1)}, f32[32,256]{1,0:T(8,128)S(1)}, u32[]{:S(2)}, u32[]{:S(2)}) collective-permute-start(f32[32,256]{1,0:T(8,128)S(1)} %get-tuple-element.228), channel_id=1, source_target_pairs={{0,1},{1,0},{2,3},{3,2},{4,5},{5,4},{6,7},{7,6},{8,9},{9,8},{10,11... | collective-permute-start | bytes 98312 | tf_op jit(solution)/shard_map/ppermute | solution.py:29
  266.5 12.2 %collective-permute-start.84 = (f32[12,256]{1,0:T(8,128)S(1)}, f32[12,256]{1,0:T(8,128)S(1)}, u32[]{:S(2)}, u32[]{:S(2)}) collective-permute-start(f32[12,256]{1,0:T(8,128)S(1)} %slice_add_fusion.1), channel_id=1, source_target_pairs={{0,8},{4,12},{8,0},{12,4},{1,9},{5,13},{9,1},{13,5},{2,10},{6,14},... | collective-permute-start | bytes 36872 | tf_op jit(solution)/shard_map/ppermute | solution.py:29
  277.2 23.6 %collective-permute-start.102 = (bf16[128,1536]{1,0:T(8,128)(2,1)S(1)}, bf16[128,1536]{1,0:T(8,128)(2,1)}, u32[]{:S(2)}, u32[]{:S(2)}) collective-permute-start(bf16[128,1536]{1,0:T(8,128)(2,1)S(1)} %get-tuple-element.258), channel_id=1, source_target_pairs={{0,2},{1,3},{2,0},{3,1},{4,6},{5,7},{6,4},{7,5},{8,10},{9,11},{10,... | collective-permute-start | bytes 1179656 | tf_op jit(solution)/shard_map/ppermute | solution.py:29
  278.7 32.1 %collective-permute-start.89 = (bf16[128,2304]{1,0:T(8,128)(2,1)S(1)}, bf16[128,2304]{1,0:T(8,128)(2,1)S(1)}, u32[]{:S(2)}, u32[]{:S(2)}) collective-permute-start(bf16[128,2304]{1,0:T(8,128)(2,1)S(1)} %collective-permute-done.88.refs_2_), channel_id=1, source_target_pairs={{0,1},{1,0},{2,3},{3,2},{4,5},{5,4},{6,7},{7,6},{8,9},{9,8},{10,11... | collective-permute-start | bytes 1769480 | tf_op jit(solution)/shard_map/ppermute | solution.py:29
  280.1 16.1 %collective-permute-start.76 = (f32[32,256]{1,0:T(8,128)S(1)}, f32[32,256]{1,0:T(8,128)S(1)}, u32[]{:S(2)}, u32[]{:S(2)}) collective-permute-start(f32[32,256]{1,0:T(8,128)S(1)} %get-tuple-element.229), channel_id=1, source_target_pairs={{0,2},{1,3},{2,0},{3,1},{4,6},{5,7},{6,4},{7,5},{8,10},{9,11},{10,... | collective-permute-start | bytes 98312 | tf_op jit(solution)/shard_map/ppermute | solution.py:29
  281.0 16.8 %collective-permute-start.77 = (f32[32,256]{1,0:T(8,128)S(1)}, f32[32,256]{1,0:T(8,128)S(1)}, u32[]{:S(2)}, u32[]{:S(2)}) collective-permute-start(f32[32,256]{1,0:T(8,128)S(1)} %get-tuple-element.230), channel_id=1, source_target_pairs={{0,3},{1,2},{2,1},{3,0},{4,7},{5,6},{6,5},{7,4},{8,11},{9,10},{10,... | collective-permute-start | bytes 98312 | tf_op jit(solution)/shard_map/ppermute | solution.py:29
  300.0 10.8 %collective-permute-start.91 = (bf16[128,1280]{1,0:T(8,128)(2,1)}, bf16[128,1280]{1,0:T(8,128)(2,1)}, u32[]{:S(2)}, u32[]{:S(2)}) collective-permute-start(bf16[128,1280]{1,0:T(8,128)(2,1)} %get-tuple-element.244), channel_id=1, source_target_pairs={{0,2},{1,3},{2,0},{3,1},{4,6},{5,7},{6,4},{7,5},{8,10},{9,11},{10,... | collective-permute-start | bytes 983048 | tf_op jit(solution)/shard_map/ppermute | solution.py:29
  300.8 10.6 %collective-permute-start.103 = (bf16[128,1536]{1,0:T(8,128)(2,1)}, bf16[128,1536]{1,0:T(8,128)(2,1)}, u32[]{:S(2)}, u32[]{:S(2)}) collective-permute-start(bf16[128,1536]{1,0:T(8,128)(2,1)} %collective-permute-done.102.refs_6_), channel_id=1, source_target_pairs={{0,1},{1,0},{2,3},{3,2},{4,5},{5,4},{6,7},{7,6},{8,9},{9,8},{10,11... | collective-permute-start | bytes 1179656 | tf_op jit(solution)/shard_map/ppermute | solution.py:29
  300.8 16.8 %collective-permute-start.96 = (bf16[128,2304]{1,0:T(8,128)(2,1)S(1)}, bf16[128,2304]{1,0:T(8,128)(2,1)S(1)}, u32[]{:S(2)}, u32[]{:S(2)}) collective-permute-start(bf16[128,2304]{1,0:T(8,128)(2,1)S(1)} %collective-permute-done.95.refs_2_), channel_id=1, source_target_pairs={{0,1},{1,0},{2,3},{3,2},{4,5},{5,4},{6,7},{7,6},{8,9},{9,8},{10,11... | collective-permute-start | bytes 1769480 | tf_op jit(solution)/shard_map/ppermute | solution.py:29
  302.6 18.3 %collective-permute-start.98 = (bf16[128,1280]{1,0:T(8,128)(2,1)}, bf16[128,1280]{1,0:T(8,128)(2,1)S(1)}, u32[]{:S(2)}, u32[]{:S(2)}) collective-permute-start(bf16[128,1280]{1,0:T(8,128)(2,1)} %copy-done.55), channel_id=1, source_target_pairs={{0,2},{1,3},{2,0},{3,1},{4,6},{5,7},{6,4},{7,5},{8,10},{9,11},{10,... | collective-permute-start | bytes 983048 | tf_op jit(solution)/shard_map/ppermute | solution.py:29
  310.8 11.2 %collective-permute-start.90 = (bf16[128,1024]{1,0:T(8,128)(2,1)}, bf16[128,1024]{1,0:T(8,128)(2,1)S(1)}, u32[]{:S(2)}, u32[]{:S(2)}) collective-permute-start(bf16[128,1024]{1,0:T(8,128)(2,1)} %copy-done.58), channel_id=1, source_target_pairs={{0,1},{1,0},{2,3},{3,2},{4,5},{5,4},{6,7},{7,6},{8,9},{9,8},{10,11... | collective-permute-start | bytes 786440 | tf_op jit(solution)/shard_map/ppermute | solution.py:29
  311.4 10.7 %collective-permute-start.92 = (bf16[128,1280]{1,0:T(8,128)(2,1)}, bf16[128,1280]{1,0:T(8,128)(2,1)S(1)}, u32[]{:S(2)}, u32[]{:S(2)}) collective-permute-start(bf16[128,1280]{1,0:T(8,128)(2,1)} %collective-permute-done.91.refs_6_), channel_id=1, source_target_pairs={{0,1},{1,0},{2,3},{3,2},{4,5},{5,4},{6,7},{7,6},{8,9},{9,8},{10,11... | collective-permute-start | bytes 983048 | tf_op jit(solution)/shard_map/ppermute | solution.py:29
  317.7 78.9 %collective-permute-start.108 = (bf16[256,2048]{1,0:T(8,128)(2,1)}, bf16[256,2048]{1,0:T(8,128)(2,1)}, u32[]{:S(2)}, u32[]{:S(2)}) collective-permute-start(bf16[256,2048]{1,0:T(8,128)(2,1)} %get-tuple-element.267.own_ref), channel_id=1, source_target_pairs={{0,16},{16,0},{1,17},{17,1},{2,18},{18,2},{3,19},{19,3},{4,20},{20... | collective-permute-start | bytes 3145736 | tf_op jit(solution)/shard_map/ppermute | solution.py:29
  320.9 72.7 %collective-permute-start.109 = (bf16[256,2048]{1,0:T(8,128)(2,1)}, bf16[256,2048]{1,0:T(8,128)(2,1)}, u32[]{:S(2)}, u32[]{:S(2)}) collective-permute-start(bf16[256,2048]{1,0:T(8,128)(2,1)} %get-tuple-element.268.own_ref), channel_id=1, source_target_pairs={{0,16},{16,0},{1,17},{17,1},{2,18},{18,2},{3,19},{19,3},{4,20},{20... | collective-permute-start | bytes 3145736 | tf_op jit(solution)/shard_map/ppermute | solution.py:29
  329.3 62.1 %collective-permute-start.93 = (bf16[256,1024]{1,0:T(8,128)(2,1)}, bf16[256,1024]{1,0:T(8,128)(2,1)S(1)}, u32[]{:S(2)}, u32[]{:S(2)}) collective-permute-start(bf16[256,1024]{1,0:T(8,128)(2,1)} %get-tuple-element.245.own_ref), channel_id=1, source_target_pairs={{0,16},{16,0},{1,17},{17,1},{2,18},{18,2},{3,19},{19,3},{4,20},{20... | collective-permute-start | bytes 1572872 | tf_op jit(solution)/shard_map/ppermute | solution.py:29
  330.8 59.6 %collective-permute-start.100 = (bf16[256,1024]{1,0:T(8,128)(2,1)S(1)}, bf16[256,1024]{1,0:T(8,128)(2,1)S(1)}, u32[]{:S(2)}, u32[]{:S(2)}) collective-permute-start(bf16[256,1024]{1,0:T(8,128)(2,1)S(1)} %get-tuple-element.252.own_ref), channel_id=1, source_target_pairs={{0,16},{16,0},{1,17},{17,1},{2,18},{18,2},{3,19},{19,3},{4,20},{20... | collective-permute-start | bytes 1572872 | tf_op jit(solution)/shard_map/ppermute | solution.py:29
  331.9 56.3 %collective-permute-start.107 = (f32[1,3584]{1,0:T(1,128)S(1)}, f32[1,3584]{1,0:T(1,128)S(1)}, u32[]{:S(2)}, u32[]{:S(2)}) collective-permute-start(f32[1,3584]{1,0:T(1,128)S(1)} %constant_dynamic-update-slice_fusion), channel_id=1, source_target_pairs={{0,16},{16,0},{1,17},{17,1},{2,18},{18,2},{3,19},{19,3},{4,20},{20... | collective-permute-start | bytes 43016 | tf_op jit(solution)/shard_map/ppermute | solution.py:29
  (121 other events, 1126.8 us)
where the time goes:
time: 400 us; the launch traced here: 399 us
  waiting for transfers between devices  197 us (49%)
  starting transfers between devices  131 us (33%)
  Pallas kernels  46.4 us (12%)
  local copies, waits for them, and re-layouts  23.5 us (6%)
    ppermute x110, waiting for transfers between devices, axis_swap(): lax.ppermute(local, axis, [(place, place ^ step) for place in range(size)])  197 us
    ppermute x110, starting transfers between devices, axis_swap(): lax.ppermute(local, axis, [(place, place ^ step) for place in range(size)])  131 us
    pallas_call x28, Pallas kernels, run(): pl.pallas_call(kernel, in_specs=[SMEM] * len(scalars) + [VMEM] * len(arra...  36.8 us
    unnamed x124, local copies, waits for them, and re-layouts  21.5 us
    pallas_call x4, Pallas kernels, finish(): pl.pallas_call(kernel, name='finish', grid=(1,), in_specs=[whole(own), wh...  9.07 us
  transfers between devices with their start and end apart: 110, of which 43 were waited for; matrix products, arithmetic and copies ran while one was open for 1% of the time, Pallas kernels for 8%

commit v1 on v0

v1 whole, which is shorter than its diff:
```python
import math

import jax
import jax.numpy as jnp
from jax import lax
from jax.experimental import pallas as pl
from jax.experimental.pallas import tpu as pltpu
from jax.sharding import PartitionSpec as P


H = 16
HD = 64
LAYERS = 2

VMEM_LIMIT = 16 * 1024 * 1024
DP, ROW, COL = "dp", "row", "col"
GAIN_ONE, SHIFT_ONE, BIAS_OUT, GAIN_TWO, SHIFT_TWO, BIAS_DOWN = range(6)

norm_epsilon = 1e-05
gelu_coef = 0.044715
gelu_scale = math.sqrt(2.0 / math.pi)
masked_score = -1e30


def int_log2(value):
    return value.bit_length() - 1


def axis_swap(local, axis, step):
    size = lax.axis_size(axis)
    return lax.ppermute(local, axis, [(place, place ^ step) for place in range(size)])


def spread(local, axis):
    size = lax.axis_size(axis)
    return [local] + [axis_swap(local, axis, step) for step in range(1, size)]


def trade(blocks, axis):
    return [blocks[0]] + [axis_swap(blocks[step], axis, step) for step in range(1, len(blocks))]


def relay(sends, axis):
    size = lax.axis_size(axis)
    got = {}
    step = size // 2
    while step:
        arrived = {place ^ step: axis_swap(got[place], axis, step) for place in sorted(got)}
        arrived[step] = axis_swap(sends[step], axis, step)
        got.update(arrived)
        step //= 2
    return [got[place] for place in range(1, size)]


def sends_of(size):
    steps = []
    step = 1
    while step < size:
        steps.append(step)
        step *= 2
    return steps


def relay_all(local, axis):
    return [local] + relay({step: local for step in sends_of(lax.axis_size(axis))}, axis)


def high_bit(place):
    return 1 << int_log2(place)


def tree_sum(parts):
    parts = list(parts)
    while len(parts) > 1:
        parts = [parts[at] + parts[at + 1] for at in range(0, len(parts), 2)]
    return parts[0]


def dot(left, right):
    return lax.dot_general(left, right, (((1,), (0,)), ((), ())), preferred_element_type=jnp.float32)


def dot_right(left, right):
    return lax.dot_general(left, right, (((1,), (1,)), ((), ())), preferred_element_type=jnp.float32)


def dot_left(left, right):
    return lax.dot_general(left, right, (((0,), (0,)), ((), ())), preferred_element_type=jnp.float32)


def low(values):
    return values.astype(jnp.bfloat16)


def wide(values):
    return values.astype(jnp.float32)


def shaped(shape, dtype):
    return jax.ShapeDtypeStruct(shape, dtype)


BF = jnp.bfloat16
F32 = jnp.float32


VMEM = pl.BlockSpec(memory_space=pltpu.VMEM)
ANY = pl.BlockSpec(memory_space=pl.ANY)
HBM = pl.BlockSpec(memory_space=pltpu.HBM)


def run(kernel, arrays, outs, scratch=(), spec=None):
    return pl.pallas_call(
        kernel,
        in_specs=[spec or VMEM] * len(arrays),
        out_specs=[VMEM] * len(outs),
        out_shape=outs,
        scratch_shapes=list(scratch),
        compiler_params=pltpu.CompilerParams(vmem_limit_bytes=VMEM_LIMIT),
    )(*arrays)


def vector_row(vecs, at):
    return jnp.concatenate([vec[at : at + 1, :] for vec in vecs], axis=1)


def norm_into(resid, gain, shift, input_ref, stats_ref):
    mean = jnp.mean(resid, axis=1, keepdims=True)
    spread_out = jnp.mean(resid * resid, axis=1, keepdims=True) - mean * mean
    scale = lax.rsqrt(spread_out + norm_epsilon)
    half = stats_ref.shape[1] // 2
    stats_ref[:, :half] = jnp.broadcast_to(mean, (resid.shape[0], half))
    stats_ref[:, half:] = jnp.broadcast_to(scale, (resid.shape[0], half))
    input_ref[...] = low((resid - mean) * scale * gain + shift)


def start_copies(copies):
    for copy in copies:
        copy.start()
    for copy in copies:
        copy.wait()


def in_hbm(array):
    return pltpu.with_memory_space_constraint(array, pltpu.HBM)


def weight_pieces(upward, downward, layer, width, first):
    if first:
        return [(0, (layer,), upward), (1, (layer,), downward)]
    chunks = downward[1] // width
    pieces = [(0, (layer,), upward[2])]
    for at in range(chunks):
        pieces.append((1, (layer, slice(at * width, (at + 1) * width)), downward[2]))
    return pieces


def pack_copies(refs, out_ref, sems, pieces):
    copies = []
    at = 0
    for slot, (which, index, columns) in enumerate(pieces):
        copies.append(
            pltpu.make_async_copy(
                refs[which].at[index], out_ref.at[:, at : at + columns], sems.at[slot]
            )
        )
        at += columns
    return copies


def start_blocks(block_input, cotangent, joined, output, size):
    rows = block_input.shape[0] // size
    width = block_input.shape[1]
    pieces = weight_pieces(joined.shape[2], output.shape[2], 0, joined.shape[1], True)
    total = sum(piece[2] for piece in pieces)

    def kernel(input_ref, cotangent_ref, joined_ref, output_ref, *refs):
        outs, pack_ref, sems, pack_sems = refs[:size], *refs[size:]
        copies = []
        for step in range(size):
            here = slice(step * rows, (step + 1) * rows)
            copies.append(
                pltpu.make_async_copy(
                    input_ref.at[here], outs[step].at[:, :width], sems.at[2 * step]
                )
            )
            copies.append(
                pltpu.make_async_copy(
                    cotangent_ref.at[here], outs[step].at[:, width:], sems.at[2 * step + 1]
                )
            )
        copies += pack_copies((joined_ref, output_ref), pack_ref, pack_sems, pieces)
        start_copies(copies)

    outs = run(
        kernel,
        [in_hbm(array) for array in (block_input, cotangent, joined, output)],
        [shaped((rows, 2 * width), BF)] * size + [shaped((joined.shape[1], total), BF)],
        [pltpu.SemaphoreType.DMA((2 * size,)), pltpu.SemaphoreType.DMA((len(pieces),))],
        HBM,
    )
    return outs[:size], outs[size]


def start_vectors(vectors, biases):
    count, width = len(vectors), vectors[0].shape[1]

    def kernel(*refs):
        vector_refs = refs[:count]
        bias_refs = refs[count : count + len(biases)]
        out_ref = refs[count + len(biases)]
        bias_outs = refs[count + len(biases) + 1 : count + 2 * len(biases) + 1]
        landing = refs[count + 2 * len(biases) + 1 : -1]
        sems = refs[-1]
        pairs = list(zip(vector_refs, landing)) + list(zip(bias_refs, bias_outs))
        start_copies(
            [
                pltpu.make_async_copy(source, target, sems.at[at])
                for at, (source, target) in enumerate(pairs)
            ]
        )
        for at, ref in enumerate(landing):
            out_ref[LAYERS * at : LAYERS * (at + 1), :] = ref[...]

    outs = run(
        kernel,
        [in_hbm(array) for array in (*vectors, *biases)],
        [shaped((LAYERS * count, width), F32)] + [shaped(bias.shape, F32) for bias in biases],
        [pltpu.VMEM(vector.shape, F32) for vector in vectors]
        + [pltpu.SemaphoreType.DMA((count + len(biases),))],
        HBM,
    )
    return outs[0], outs[1:]


def turn_blocks(blocks, extra=0):
    size = len(blocks)
    rows = blocks[0].shape[0] - extra

    def kernel(*refs):
        block_refs, out_refs, turn = refs[:size], refs[size : 2 * size], refs[2 * size]
        shift = lax.axis_index(ROW) ^ lax.axis_index(COL)
        for at in range(size):
            turn[at] = block_refs[at][:rows, :]
        if extra:
            total = tree_sum([ref[rows:, :] for ref in block_refs])
        for at in range(size):
            out_refs[at][:rows, :] = turn[at ^ shift]
            if extra:
                out_refs[at][rows:, :] = total

    shape, dtype = blocks[0].shape, blocks[0].dtype
    return run(
        kernel,
        list(blocks),
        [shaped(shape, dtype)] * size,
        [pltpu.VMEM((size, rows, shape[1]), dtype)],
    )


def pack_weights(one, two, layer, width, first):
    last = two.shape[2] if first else two.shape
    pieces = weight_pieces(one.shape[2] if first else one.shape, last, layer, width, first)
    total = sum(piece[2] for piece in pieces)

    def kernel(one_ref, two_ref, out_ref, sems):
        start_copies(pack_copies((one_ref, two_ref), out_ref, sems, pieces))

    return pl.pallas_call(
        kernel,
        in_specs=[HBM] * 2,
        out_specs=VMEM,
        out_shape=shaped((width, total), BF),
        scratch_shapes=[pltpu.SemaphoreType.DMA((len(pieces),))],
        compiler_params=pltpu.CompilerParams(vmem_limit_bytes=VMEM_LIMIT),
    )(in_hbm(one), in_hbm(two))


def first_norm(got, vecs):
    size = len(got)
    rows, width = got[0].shape[0], got[0].shape[1] // 2

    def kernel(*refs):
        got_refs = refs[:size]
        vec_refs = refs[size : size + len(vecs)]
        resid_ref, cotangent_ref, input_ref, stats_ref = refs[size + len(vecs) :]
        whole = [ref[...] for ref in got_refs]
        resid = jnp.concatenate([wide(part[:, :width]) for part in whole], axis=1)
        cotangent_ref[...] = jnp.concatenate([part[:, width:] for part in whole], axis=1)
        resid_ref[...] = resid
        norm_into(
            resid,
            vector_row(vec_refs, GAIN_ONE * LAYERS),
            vector_row(vec_refs, SHIFT_ONE * LAYERS),
            input_ref,
            stats_ref,
        )

    full = size * width
    return run(
        kernel,
        [*got, *vecs],
        [
            shaped((rows, full), F32),
            shaped((rows, full), BF),
            shaped((rows, full), BF),
            shaped((rows, 256), F32),
        ],
    )


def next_norm(resid, parts, vecs, layer, bias_at, gain_at, shift_at):
    count = len(parts)
    next_layer = layer + 1 if gain_at == GAIN_ONE else layer

    def kernel(resid_ref, *refs):
        part_refs = refs[:count]
        vec_refs = refs[count : count + len(vecs)]
        out_ref, input_ref, stats_ref = refs[count + len(vecs) :]
        total = tree_sum([wide(ref[...]) for ref in part_refs])
        resid = resid_ref[...] + total + vector_row(vec_refs, bias_at * LAYERS + layer)
        out_ref[...] = resid
        norm_into(
            resid,
            vector_row(vec_refs, gain_at * LAYERS + next_layer),
            vector_row(vec_refs, shift_at * LAYERS + next_layer),
            input_ref,
            stats_ref,
        )

    rows, full = resid.shape
    return run(
        kernel,
        [resid, *parts, *vecs],
        [shaped((rows, full), F32), shaped((rows, full), BF), shaped((rows, 256), F32)],
    )


def cut_rows(value, refs):
    rows = refs[0].shape[0]
    for at, ref in enumerate(refs):
        ref[...] = value[at * rows : (at + 1) * rows]


def gathered(refs):
    return jnp.concatenate([ref[...] for ref in refs], axis=0)


def attention_forward(blocks, packs, query_bias, value_bias, layer):
    size, cols = len(blocks), len(packs)
    rows, full = blocks[0].shape
    length = size * rows
    width = full // cols
    across = query_bias.shape[1]
    heads = across // HD
    shift = int_log2(rows)
    steps = sends_of(cols)

    def kernel(*refs):
        block_refs = refs[:size]
        pack_refs = refs[size : size + cols]
        query_bias_ref, value_bias_ref = refs[size + cols : size + cols + 2]
        qkv_ref, probs_ref = refs[size + cols + 2 : size + cols + 4]
        part_refs = refs[size + cols + 4 : 2 * size + cols + 4]
        send_refs = refs[2 * size + cols + 4 :]
        mixed_ref = send_refs[0]
        full_first = gathered(block_refs)
        joined = tree_sum(
            [
                dot(full_first[:, at * width : (at + 1) * width], pack_refs[at][:, : 3 * across])
                for at in range(cols)
            ]
        )
        row = lax.axis_index(ROW)
        turn = row ^ lax.axis_index(COL)

        def where_is(axis):
            index = lax.broadcasted_iota(jnp.int32, (length, length), axis)
            return ((lax.shift_right_logical(index, shift) ^ turn) << shift) + (index & (rows - 1))

        offset = wide(where_is(1) - where_is(0))
        allowed = offset <= 0.0
        for head in range(heads):
            at = head * 3 * HD
            here = slice(head * HD, (head + 1) * HD)
            query = low(joined[:, at : at + HD] + query_bias_ref[layer : layer + 1, here])
            keys = low(joined[:, at + HD : at + 2 * HD])
            values = low(
                joined[:, at + 2 * HD : at + 3 * HD] + value_bias_ref[layer : layer + 1, here]
            )
            qkv_ref[:, at : at + HD] = query
            qkv_ref[:, at + HD : at + 2 * HD] = keys
            qkv_ref[:, at + 2 * HD : at + 3 * HD] = values
            index = jnp.full((1, length), row * heads + head + 1, jnp.int32)
            slope = jnp.exp2(wide(index) * (-8.0 / H))
            scores = dot_right(query, keys) * (1.0 / math.sqrt(HD)) + slope * offset
            scores = jnp.where(allowed, scores, masked_score)
            top = jnp.max(scores, axis=1, keepdims=True)
            log_total = top + jnp.log(jnp.sum(jnp.exp(scores - top), axis=1, keepdims=True))
            probs = jnp.exp(scores - log_total)
            probs_ref[head] = probs
            mixed_ref[:, here] = low(dot(low(probs), values))
        mixed = mixed_ref[:, :across]
        partial = jnp.concatenate(
            [low(dot(mixed, pack_ref[:, 3 * across : 3 * across + width])) for pack_ref in pack_refs],
            axis=1,
        )
        cut_rows(partial, part_refs)
        bundle_into(send_refs, steps, [mixed], [full_first], width)

    outs = run(
        kernel,
        [*blocks, *packs, query_bias, value_bias],
        [shaped((length, 3 * across), BF), shaped((heads, length, length), F32)]
        + [shaped((rows, full), BF)] * size
        + bundle_shapes(length, steps, across, 1, width),
    )
    return outs[:2], outs[2 : 2 + size], outs[2 + size :]


def bundle_into(refs, steps, shared, addressed, width):
    for at, ref in enumerate(refs):
        first = steps[at - 1] if at else 0
        count = first if at else 1
        column = 0
        for value in shared:
            ref[:, column : column + value.shape[1]] = value
            column += value.shape[1]
        for place in range(first, first + count):
            for value in addressed:
                ref[:, column : column + width] = value[:, place * width : (place + 1) * width]
                column += width


def bundle_shapes(length, steps, shared, addressed, width):
    counts = [1] + list(steps)
    return [shaped((length, shared + count * addressed * width), BF) for count in counts]


def feed_forward(blocks, packs, upward_bias, layer, middle=None, vecs=()):
    size, cols = len(blocks), len(packs)
    rows, full = blocks[0].shape
    length = size * rows
    width = full // cols
    units = upward_bias.shape[1]
    steps = sends_of(cols)
    extra = [middle, *vecs] if vecs else []
    parts = [shaped((length, width), BF)] * cols if vecs else [shaped((rows, full), BF)] * size

    def kernel(*refs):
        block_refs = refs[:size]
        pack_refs = refs[size : size + cols]
        bias_ref = refs[size + cols]
        more = refs[size + cols + 1 : size + cols + 1 + len(extra)]
        slope_ref = refs[size + cols + 1 + len(extra)]
        part_refs = refs[size + cols + 2 + len(extra) :][: len(parts)]
        send_refs = refs[size + cols + 2 + len(extra) + len(parts) :]
        full_second = gathered(block_refs)
        pre_act = tree_sum(
            [
                dot(full_second[:, at * width : (at + 1) * width], pack_refs[at][:, :units])
                for at in range(cols)
            ]
        )
        pre_act = pre_act + bias_ref[layer : layer + 1, :]
        inner = gelu_scale * (pre_act + gelu_coef * pre_act * pre_act * pre_act)
        tangent = jnp.tanh(inner)
        hidden = low(0.5 * pre_act * (1.0 + tangent))
        slope_ref[...] = 0.5 * (1.0 + tangent) + 0.5 * pre_act * (
            1.0 - tangent * tangent
        ) * gelu_scale * (1.0 + 3.0 * gelu_coef * pre_act * pre_act)
        partial = jnp.concatenate(
            [
                tree_sum(
                    [
                        dot(
                            hidden[:, at : at + width],
                            pack_ref[:, units + at : units + at + width],
                        )
                        for at in range(0, units, width)
                    ]
                )
                for pack_ref in pack_refs
            ],
            axis=1,
        )
        if vecs:
            bias = vector_row(more[1:], BIAS_DOWN * LAYERS + layer)
            shift = lax.axis_index(ROW) ^ lax.axis_index(COL)
            for step in range(size):
                block = partial[step * rows : (step + 1) * rows]
                if not step:
                    block = block + more[0][...] + bias
                at = pl.multiple_of((step ^ shift) * rows, rows)
                for place, ref in enumerate(part_refs):
                    ref[pl.ds(at, rows), :] = low(block[:, place * width : (place + 1) * width])
        else:
            cut_rows(low(partial), part_refs)
        bundle_into(send_refs, steps, [hidden], [full_second], width)

    outs = run(
        kernel,
        [*blocks, *packs, upward_bias, *extra],
        [shaped((length, units), F32)]
        + parts
        + bundle_shapes(length, steps, units, 1, width),
    )
    return outs[0], outs[1 : 1 + len(parts)], outs[1 + len(parts) :]


def feed_backward(blocks, packs, slope):
    size, cols = len(blocks), len(packs)
    rows, full = blocks[0].shape
    length = size * rows
    width = full // cols
    units = slope.shape[1]
    steps = sends_of(cols)

    def kernel(*refs):
        block_refs = refs[:size]
        pack_refs = refs[size : size + cols]
        slope_ref = refs[size + cols]
        part_refs = refs[size + cols + 1 : 2 * size + cols + 1]
        pre_ref = refs[2 * size + cols + 1]
        send_refs = refs[2 * size + cols + 2 :]
        full_grad = gathered(block_refs)
        grad_hidden = jnp.concatenate(
            [
                tree_sum(
                    [
                        dot_right(
                            full_grad[:, place * width : (place + 1) * width],
                            pack_refs[place][:, units + at : units + at + width],
                        )
                        for place in range(cols)
                    ]
                )
                for at in range(0, units, width)
            ],
            axis=1,
        )
        grad_pre = low(grad_hidden * slope_ref[...])
        pre_ref[...] = grad_pre
        partial = jnp.concatenate(
            [low(dot_right(grad_pre, pack_ref[:, :units])) for pack_ref in pack_refs], axis=1
        )
        cut_rows(partial, part_refs)
        bundle_into(send_refs, steps, [], [full_grad], width)

    outs = run(
        kernel,
        [*blocks, *packs, slope],
        [shaped((rows, full), BF)] * size
        + [shaped((length, units), BF)]
        + bundle_shapes(length, steps, 0, 1, width),
    )
    return outs[:size], outs[size], outs[size + 1 :]


def norm_back_math(grad_in, part_refs, resid_ref, stats_ref, gain):
    grad_out = tree_sum([wide(ref[...]) for ref in part_refs])
    half = stats_ref.shape[1] // 2
    scale = stats_ref[:, half : half + 1]
    normed = (resid_ref[...] - stats_ref[:, :1]) * scale
    grad_normed = grad_out * gain
    first = jnp.mean(grad_normed, axis=1, keepdims=True)
    second = jnp.mean(grad_normed * normed, axis=1, keepdims=True)
    total = grad_in + scale * (grad_normed - first - normed * second)
    sums = [
        jnp.sum(grad_out * normed, axis=0, keepdims=True),
        jnp.sum(grad_out, axis=0, keepdims=True),
    ]
    return total, sums


def norm_backward(grad_resid, parts, resid, stats, vecs, layer, gain_at, extra):
    count = len(parts)
    rows, full = grad_resid.shape

    def kernel(grad_ref, resid_ref, stats_ref, *refs):
        part_refs = refs[:count]
        vec_refs = refs[count : count + len(vecs)]
        out_ref, low_ref, sums_ref = refs[count + len(vecs) :]
        grad_in = wide(grad_ref[...])
        total, sums = norm_back_math(
            grad_in, part_refs, resid_ref, stats_ref, vector_row(vec_refs, gain_at * LAYERS + layer)
        )
        out_ref[...] = total
        low_ref[...] = low(total)
        if extra:
            sums.append(jnp.sum(total, axis=0, keepdims=True))
            sums.append(jnp.sum(grad_in, axis=0, keepdims=True))
        for at, value in enumerate(sums):
            sums_ref[at : at + 1, :] = value

    return run(
        kernel,
        [grad_resid, resid, stats, *parts, *vecs],
        [
            shaped((rows, full), F32),
            shaped((rows, full), BF),
            shaped((4 if extra else 2, full), F32),
        ],
    )


def last_backward(grad_resid, parts, resid, stats, vecs, other_sums, extra):
    count = len(parts)
    rows, full = grad_resid.shape
    cols = len(vecs)
    width = full // cols

    def kernel(grad_ref, resid_ref, stats_ref, *refs):
        part_refs = refs[:count]
        vec_refs = refs[count : count + cols]
        sums_refs = refs[count + cols : count + cols + len(other_sums)]
        out_refs = refs[count + cols + len(other_sums) :]
        total, sums = norm_back_math(
            grad_ref[...], part_refs, resid_ref, stats_ref, vector_row(vec_refs, GAIN_ONE * LAYERS)
        )
        lines = list(sums)
        for ref in sums_refs:
            lines += [ref[at : at + 1, :] for at in range(ref.shape[0])]
        for place in range(cols):
            here = slice(place * width, (place + 1) * width)
            out_refs[place][:rows, :] = total[:, here]
            out_refs[place][rows:, :] = jnp.zeros((extra, width), F32)
            for at, line in enumerate(lines):
                out_refs[place][rows + at : rows + at + 1, :] = line[:, here]

    return run(
        kernel,
        [grad_resid, resid, stats, *parts, *vecs, *other_sums],
        [shaped((rows + extra, width), F32)] * cols,
    )


def attention_backward(blocks, packs, qkv, probs, mixed, across):
    size, cols = len(blocks), len(packs)
    rows, full = blocks[0].shape
    length = size * rows
    width = full // cols
    heads = across // HD
    factor = 1.0 / math.sqrt(HD)

    def kernel(*refs):
        block_refs = refs[:size]
        pack_refs = refs[size : size + cols]
        qkv_ref, probs_ref, mixed_ref = refs[size + cols : size + cols + 3]
        part_refs = refs[size + cols + 3 : 2 * size + cols + 3]
        send_refs = refs[2 * size + cols + 3 :]
        joined_ref = send_refs[0]
        full_middle = gathered(block_refs)
        grad_mixed = low(
            tree_sum(
                [
                    dot_right(
                        full_middle[:, at * width : (at + 1) * width],
                        pack_refs[at][:, 3 * across : 3 * across + width],
                    )
                    for at in range(cols)
                ]
            )
        )
        for head in range(heads):
            at = head * 3 * HD
            here = slice(head * HD, (head + 1) * HD)
            query = qkv_ref[:, at : at + HD]
            keys = qkv_ref[:, at + HD : at + 2 * HD]
            values = qkv_ref[:, at + 2 * HD : at + 3 * HD]
            grad_here = grad_mixed[:, here]
            probs = probs_ref[head]
            value_sum = dot_left(low(probs), grad_here)
            grad_probs = dot_right(grad_here, values)
            delta = jnp.sum(wide(grad_here) * wide(mixed_ref[:, here]), axis=1, keepdims=True)
            grad_scores = low(probs * (grad_probs - delta))
            joined_ref[:, at : at + HD] = low(dot(grad_scores, keys) * factor)
            joined_ref[:, at + HD : at + 2 * HD] = low(dot_left(grad_scores, query) * factor)
            joined_ref[:, at + 2 * HD : at + 3 * HD] = low(value_sum)
        grad_joined = joined_ref[:, : 3 * across]
        partial = jnp.concatenate(
            [low(dot_right(grad_joined, pack_ref[:, : 3 * across])) for pack_ref in pack_refs],
            axis=1,
        )
        cut_rows(partial, part_refs)
        bundle_into(send_refs, sends_of(cols), [grad_joined], [full_middle], width)

    outs = run(
        kernel,
        [*blocks, *packs, qkv, probs, mixed],
        [shaped((rows, full), BF)] * size
        + bundle_shapes(length, sends_of(cols), 3 * across, 1, width),
    )
    return outs[:size], outs[size:]


def rows_of(refs, pick):
    return jnp.concatenate([ref[:, pick(at)] for at, ref in enumerate(refs)], axis=0)


def slices_of(refs, shared, width):
    def pick(place):
        start = shared + (place - high_bit(place) if place else 0) * width
        return slice(start, start + width)

    return rows_of(refs, pick)


def down_changes(ahead, grads, units, width):
    cols = len(ahead)

    def kernel(*refs):
        ahead_refs, grad_refs, out_ref = refs[:cols], refs[cols : 2 * cols], refs[2 * cols]
        grad_all = slices_of(grad_refs, 0, width)
        for at in range(0, units, width):
            hidden_all = rows_of(ahead_refs, lambda _: slice(at, at + width))
            out_ref[:, at : at + width] = low(dot_left(hidden_all, grad_all))

    return run(kernel, [*ahead, *grads], [shaped((width, units), BF)])[0]


def up_changes(ahead, pres, units, width):
    cols = len(ahead)

    def kernel(*refs):
        ahead_refs, pre_refs, out_ref = refs[:cols], refs[cols : 2 * cols], refs[2 * cols]
        pre_all = gathered(pre_refs)
        out_ref[:width, :] = low(dot_left(slices_of(ahead_refs, units, width), pre_all))
        total = jnp.sum(wide(pre_all), axis=0, keepdims=True)
        out_ref[width:, :] = low(jnp.broadcast_to(total, (16, units)))

    return run(kernel, [*ahead, *pres], [shaped((width + 16, units), BF)])[0]


def attention_changes(ahead, joined, across, width):
    cols = len(ahead)

    def kernel(*refs):
        ahead_refs, joined_refs, out_ref = refs[:cols], refs[cols : 2 * cols], refs[2 * cols]
        joined_all = rows_of(joined_refs, lambda _: slice(0, 3 * across))
        out_ref[:width, : 3 * across] = low(
            dot_left(slices_of(ahead_refs, across, width), joined_all)
        )
        total = jnp.sum(wide(joined_all), axis=0, keepdims=True)
        out_ref[width:, : 3 * across] = low(jnp.broadcast_to(total, (16, 3 * across)))
        mixed_all = rows_of(ahead_refs, lambda _: slice(0, across))
        change = low(dot_left(mixed_all, slices_of(joined_refs, 3 * across, width)))
        for at in range(0, across, width):
            column = 3 * across + at // width * width
            out_ref[:width, column : column + width] = change[at : at + width]
        out_ref[width:, 3 * across :] = jnp.zeros((16, out_ref.shape[1] - 3 * across), BF)

    return run(
        kernel,
        [*ahead, *joined],
        [shaped((width + 16, 4 * across), BF)],
    )[0]


def finish(own, other, layer, cuts, shapes, kept, line):
    width = own.shape[0] - (16 if line else 0)

    def kernel(own_ref, other_ref, *refs):
        out_refs = refs[len(kept or ()) :]
        for out_ref, pieces in zip(out_refs, cuts):
            row = 0
            for start, stop in pieces:
                out_ref[0, row : row + width, :] = wide(own_ref[:width, start:stop]) + wide(
                    other_ref[:width, start:stop]
                )
                row += width
        if line:
            out_refs[-1][...] = wide(own_ref[width : width + 8, :]) + wide(
                other_ref[width : width + 8, :]
            )

    def whole(array):
        return pl.BlockSpec(array.shape, lambda at: (0, 0))

    lines = [shaped((8, own.shape[1]), F32)] if line else []
    return pl.pallas_call(
        kernel,
        grid=(1,),
        in_specs=[whole(own), whole(other)] + [ANY] * len(kept or ()),
        out_specs=[pl.BlockSpec((1,) + shape[1:], lambda at: (layer, 0, 0)) for shape in shapes]
        + [whole(array) for array in lines],
        out_shape=[shaped(shape, F32) for shape in shapes] + lines,
        input_output_aliases={2 + at: at for at in range(len(kept or ()))},
        compiler_params=pltpu.CompilerParams(vmem_limit_bytes=VMEM_LIMIT),
    )(own, other, *(kept or ()))


def finish_vectors(own, other, up_lines, joined_lines, across):
    width = own.shape[1]
    units = up_lines[0].shape[1]
    heads = across // HD

    def kernel(*refs):
        own_ref, other_ref = refs[:2]
        up_refs = refs[2 : 2 + LAYERS]
        joined_refs = refs[2 + LAYERS : 2 + 2 * LAYERS]
        outs = refs[2 + 2 * LAYERS :]
        total = own_ref[...] + other_ref[...]
        for layer in range(LAYERS):
            here = slice(layer, layer + 1)
            for slot in range(6):
                outs[slot][here, :] = total[6 * layer + slot : 6 * layer + slot + 1, :]
            outs[6][here, :] = up_refs[layer][:1, :]
            for head in range(heads):
                at = head * 3 * HD
                there = slice(head * HD, (head + 1) * HD)
                outs[7][here, there] = joined_refs[layer][:1, at : at + HD]
                outs[8][here, there] = joined_refs[layer][:1, at + 2 * HD : at + 3 * HD]

    return run(
        kernel,
        [own, other, *up_lines, *joined_lines],
        [shaped((LAYERS, width), F32)] * 6
        + [shaped((LAYERS, units), F32)]
        + [shaped((LAYERS, across), F32)] * 2,
    )


def end_place(got, extra=0):
    size = len(got)
    rows, width = got[0].shape[0] - extra, got[0].shape[1]

    def kernel(*refs):
        for at in range(size):
            refs[size][at * rows : (at + 1) * rows, :] = refs[at][:rows, :]
        if extra:
            refs[size + 1][...] = tree_sum([ref[rows:, :] for ref in refs[:size]])

    outs = [shaped((rows * size, width), got[0].dtype)]
    if extra:
        outs.append(shaped((extra, width), got[0].dtype))
    return run(kernel, list(got), outs)


def turn_in(blocks):
    got = turn_blocks(trade(blocks, ROW))
    return trade(got, COL)


def turn_out(blocks, extra=0):
    got = turn_blocks(trade(blocks, COL), extra)
    return end_place(trade(got, ROW), extra)


def turn_sum(blocks):
    got = turn_blocks(trade(blocks, COL))
    return sum_blocks(trade(got, ROW))


def sum_blocks(got):
    def kernel(*refs):
        refs[-1][...] = low(tree_sum([wide(ref[...]) for ref in refs[:-1]]))

    return run(kernel, list(got), [shaped(got[0].shape, BF)])[0]


def shards(
    block_input,
    cotangent,
    first_gain,
    first_shift,
    joined_weight,
    query_bias,
    value_bias,
    output_weight,
    output_bias,
    second_gain,
    second_shift,
    upward_weight,
    upward_bias,
    downward_weight,
    downward_bias,
):
    across = query_bias.shape[1]
    units = upward_bias.shape[1]
    width = block_input.shape[1]
    size, cols = lax.axis_size(ROW), lax.axis_size(COL)
    steps = sends_of(cols)
    extra = -(-6 * LAYERS // 8) * 8

    def exchange(sends):
        return [sends[0]] + relay(dict(zip(steps, sends[1:])), COL)

    blocks, first_pack = start_blocks(block_input, cotangent, joined_weight, output_weight, size)
    vectors, (query_bias, value_bias, upward_bias) = start_vectors(
        [first_gain, first_shift, output_bias, second_gain, second_shift, downward_bias],
        [query_bias, value_bias, upward_bias],
    )
    got = turn_in(blocks)
    vecs = relay_all(vectors, COL)
    weights = []
    for layer in range(LAYERS):
        weights.append([])
        for first in (True, False):
            if layer or not first:
                pair = (joined_weight, output_weight) if first else (upward_weight, downward_weight)
                pack = pack_weights(*pair, layer, width, first)
            else:
                pack = first_pack
            weights[layer].append(relay_all(pack, COL))
    resid, grad_resid, norm_input, stats = first_norm(got, vecs)
    saved = []
    for layer in range(LAYERS):
        attention_packs, feed_packs = weights[layer]
        first_kept = (resid, stats)
        (qkv, probs), parts, sends = attention_forward(
            spread(norm_input, ROW), attention_packs, query_bias, value_bias, layer
        )
        attention_ahead = exchange(sends)
        middle, norm_input, stats = next_norm(
            resid, trade(parts, ROW), vecs, layer, BIAS_OUT, GAIN_TWO, SHIFT_TWO
        )
        second_kept = (middle, stats)
        slope, parts, sends = feed_forward(
            spread(norm_input, ROW),
            feed_packs,
            upward_bias,
            layer,
            *((middle, vecs) if layer + 1 == LAYERS else ()),
        )
        feed_ahead = exchange(sends)
        saved.append((first_kept, second_kept, qkv, probs, slope, attention_ahead, feed_ahead))
        if layer + 1 < LAYERS:
            resid, norm_input, stats = next_norm(
                middle, trade(parts, ROW), vecs, layer, BIAS_DOWN, GAIN_ONE, SHIFT_ONE
            )
        else:
            block_output = turn_sum(parts)

    grad_low = grad_resid
    sums = []
    down_outs = up_outs = attention_outs = None
    up_lines, joined_lines = [None] * LAYERS, [None] * LAYERS
    for layer in reversed(range(LAYERS)):
        attention_packs, feed_packs = weights[layer]
        first_kept, second_kept, qkv, probs, slope, attention_ahead, feed_ahead = saved[layer]
        parts, grad_pre, sends = feed_backward(spread(grad_low, ROW), feed_packs, slope)
        grads = exchange(sends)
        pres = relay_all(grad_pre, COL)
        grad_middle, middle_low, second_sums = norm_backward(
            grad_resid, trade(parts, ROW), *second_kept, vecs, layer, GAIN_TWO, True
        )
        parts, sends = attention_backward(
            spread(middle_low, ROW), attention_packs, qkv, probs, attention_ahead[0], across
        )
        joined = exchange(sends)
        parts = trade(parts, ROW)
        if layer:
            grad_resid, grad_low, first_sums = norm_backward(
                grad_middle, parts, *first_kept, vecs, layer, GAIN_ONE, False
            )
            sums = [first_sums, second_sums] + sums
        else:
            blocks = last_backward(
                grad_middle, parts, *first_kept, vecs, [second_sums] + sums, extra
            )
        change = down_changes(feed_ahead, grads, units, width)
        down_outs = finish(
            change,
            axis_swap(change, DP, 1),
            layer,
            [[(at, at + width) for at in range(0, units, width)]],
            [downward_weight.shape],
            down_outs,
            False,
        )
        change = up_changes(feed_ahead, pres, units, width)
        *up_outs, up_lines[layer] = finish(
            change,
            axis_swap(change, DP, 1),
            layer,
            [[(0, units)]],
            [upward_weight.shape],
            up_outs,
            True,
        )
        change = attention_changes(attention_ahead, joined, across, width)
        chunk = range(3 * across, 3 * across + across // width * width, width)
        *attention_outs, joined_lines[layer] = finish(
            change,
            axis_swap(change, DP, 1),
            layer,
            [[(0, 3 * across)], [(at, at + width) for at in chunk]],
            [joined_weight.shape, output_weight.shape],
            attention_outs,
            True,
        )
    input_gradient, totals = turn_out(blocks, extra)
    vector_sums = finish_vectors(totals, axis_swap(totals, DP, 1), up_lines, joined_lines, across)
    return (
        block_output,
        input_gradient,
        vector_sums[0],
        vector_sums[1],
        attention_outs[0],
        vector_sums[7],
        vector_sums[8],
        attention_outs[1],
        vector_sums[4],
        vector_sums[2],
        vector_sums[3],
        up_outs[0],
        vector_sums[6],
        down_outs[0],
        vector_sums[5],
    )


def solution(mesh):
    return jax.shard_map(
        shards,
        mesh=mesh,
        in_specs=(
            P((DP, ROW), COL),
            P((DP, ROW), COL),
            P(None, COL),
            P(None, COL),
            P(None, COL, ROW),
            P(None, ROW),
            P(None, ROW),
            P(None, ROW, COL),
            P(None, COL),
            P(None, COL),
            P(None, COL),
            P(None, COL, ROW),
            P(None, ROW),
            P(None, ROW, COL),
            P(None, COL),
        ),
        out_specs=(
            P((DP, ROW), COL),
            P((DP, ROW), COL),
            P(None, COL),
            P(None, COL),
            P(None, COL, ROW),
            P(None, ROW),
            P(None, ROW),
            P(None, ROW, COL),
            P(None, COL),
            P(None, COL),
            P(None, COL),
            P(None, COL, ROW),
            P(None, ROW),
            P(None, ROW, COL),
            P(None, COL),
        ),
        check_vma=False,
    )
```

time: 400 us -> 354 us (0.89)
  local copies, waits for them, and re-layouts: 23.5 us -> 0 us
  Pallas kernels: 46.4 us -> 31.3 us
  starting transfers between devices: 131 us -> 119 us
  waiting for transfers between devices: 197 us -> 202 us
    unnamed x124 -> x0, local copies, waits for them, and re-layouts: 21.5 us -> none
    pallas_call x36 -> x39, Pallas kernels: 46.4 us -> 31.3 us  [the longest x30 21.4 us: run(): pl.pallas_call(kernel, in_specs=[spec or VMEM] * len(arrays), out_specs=[...]
    ppermute x110 -> x115, starting transfers between devices: 131 us -> 119 us  [axis_swap(): lax.ppermute(local, axis, [(place, place ^ step) for place in range(size)])]
    ppermute x110 -> x115, waiting for transfers between devices: 197 us -> 202 us  [axis_swap(): lax.ppermute(local, axis, [(place, place ^ step) for place in range(size)])]
  transfers between devices with their start and end apart: 110 -> 115, of which waited for: 43 -> 48; matrix products, arithmetic and copies ran while one was open for 1% -> 0% of each run, Pallas kernels for 8% -> 8%
where the time goes in v1:
time: 354 us
  waiting for transfers between devices  202 us (57%)
  starting transfers between devices  119 us (34%)
  Pallas kernels  31.3 us (9%)
    ppermute x115, waiting for transfers between devices, axis_swap(): lax.ppermute(local, axis, [(place, place ^ step) for place in range(size)])  202 us
    ppermute x115, starting transfers between devices, axis_swap(): lax.ppermute(local, axis, [(place, place ^ step) for place in range(size)])  119 us
    pallas_call x30, Pallas kernels, run(): pl.pallas_call(kernel, in_specs=[spec or VMEM] * len(arrays), out_specs=[...  21.4 us
  transfers between devices with their start and end apart: 115, of which 48 were waited for; matrix products, arithmetic and copies ran while one was open for 0% of the time, Pallas kernels for 8%

profile of v1, /device:TPU:0, one launch (start us, length us, event | category | flops | bytes accessed | tf_op | source)
XLA Modules:
  0.0 353.8 jit_solution(11618704370243608264)
XLA Ops:
  1.9 3.0 collective-permute-start.22
  7.5 2.1 collective-permute-start.40
  11.1 2.6 collective-permute-start.1
  13.7 3.3 collective-permute-start.2
  20.1 42.0 %collective-permute-done.7.refs_6_.refs_12_ = f32[12,256]{1,0:T(8,128)S(1)} collective-permute-done((f32[12,256]{1,0:T(8,128)S(1)}, f32[12,256]{1,0:T(8,128)S(1)}, u32[]{:S(2)}, u32[]{:S(2)}) %collective-permute-start.7) | collective-permute-done | bytes 12320 | tf_op jit(solution)/shard_map/ppermute | solution.py:31
  65.1 2.2 collective-permute-done.4.refs_2_
  70.4 2.6 collective-permute-start.10
  73.1 4.3 %collective-permute-start.11 = (bf16[32,1024]{1,0:T(8,128)(2,1)S(1)}, bf16[32,1024]{1,0:T(8,128)(2,1)S(1)}, u32[]{:S(2)}, u32[]{:S(2)}) collective-permute-start(bf16[32,1024]{1,0:T(8,128)(2,1)S(1)} %get-tuple-element.157.refs_0_), channel_id=1, source_target_pairs={{0,12},{4,8},{8,4},{12,0},{1,13},{5,9},{9,5},{13,1},{2,14},{6,10},... | collective-permute-start | bytes 196616 | tf_op jit(solution)/shard_map/ppermute | solution.py:31
  77.4 2.2 collective-permute-done.11.refs_3_
  83.1 2.0 shard_map.266
  85.2 4.4 %collective-permute-start.16 = (bf16[32,1024]{1,0:T(8,128)(2,1)S(1)}, bf16[32,1024]{1,0:T(8,128)(2,1)S(1)}, u32[]{:S(2)}, u32[]{:S(2)}) collective-permute-start(bf16[32,1024]{1,0:T(8,128)(2,1)S(1)} %get-tuple-element.163), channel_id=1, source_target_pairs={{0,8},{4,12},{8,0},{12,4},{1,9},{5,13},{9,1},{13,5},{2,10},{6,14},... | collective-permute-start | bytes 196616 | tf_op jit(solution)/shard_map/ppermute | solution.py:31
  89.6 4.8 %collective-permute-start.17 = (bf16[32,1024]{1,0:T(8,128)(2,1)S(1)}, bf16[32,1024]{1,0:T(8,128)(2,1)S(1)}, u32[]{:S(2)}, u32[]{:S(2)}) collective-permute-start(bf16[32,1024]{1,0:T(8,128)(2,1)S(1)} %get-tuple-element.164), channel_id=1, source_target_pairs={{0,12},{4,8},{8,4},{12,0},{1,13},{5,9},{9,5},{13,1},{2,14},{6,10},... | collective-permute-start | bytes 196616 | tf_op jit(solution)/shard_map/ppermute | solution.py:31
  94.3 2.2 collective-permute-done.17.refs_3_
  96.8 4.4 %collective-permute-start.19 = (bf16[32,1024]{1,0:T(8,128)(2,1)S(1)}, bf16[32,1024]{1,0:T(8,128)(2,1)S(1)}, u32[]{:S(2)}, u32[]{:S(2)}) collective-permute-start(bf16[32,1024]{1,0:T(8,128)(2,1)S(1)} %get-tuple-element.166.refs_0_), channel_id=1, source_target_pairs={{0,8},{4,12},{8,0},{12,4},{1,9},{5,13},{9,1},{13,5},{2,10},{6,14},... | collective-permute-start | bytes 196616 | tf_op jit(solution)/shard_map/ppermute | solution.py:31
  101.3 5.0 %collective-permute-start.20 = (bf16[32,1024]{1,0:T(8,128)(2,1)S(1)}, bf16[32,1024]{1,0:T(8,128)(2,1)S(1)}, u32[]{:S(2)}, u32[]{:S(2)}) collective-permute-start(bf16[32,1024]{1,0:T(8,128)(2,1)S(1)} %get-tuple-element.166.refs_0_), channel_id=1, source_target_pairs={{0,12},{4,8},{8,4},{12,0},{1,13},{5,9},{9,5},{13,1},{2,14},{6,10},... | collective-permute-start | bytes 196616 | tf_op jit(solution)/shard_map/ppermute | solution.py:31
  106.3 2.2 collective-permute-done.20.refs_3_
  109.7 4.5 %collective-permute-done.24.refs_1_ = bf16[32,1024]{1,0:T(8,128)(2,1)S(1)} collective-permute-done((bf16[32,1024]{1,0:T(8,128)(2,1)S(1)}, bf16[32,1024]{1,0:T(8,128)(2,1)S(1)}, u32[]{:S(2)}, u32[]{:S(2)}) %collective-permute-start.24) | collective-permute-done | bytes 65568 | tf_op jit(solution)/shard_map/ppermute | solution.py:31
  114.2 2.6 collective-permute-start.25
  116.9 3.8 %collective-permute-done.25.refs_2_ = bf16[32,1024]{1,0:T(8,128)(2,1)S(1)} collective-permute-done((bf16[32,1024]{1,0:T(8,128)(2,1)S(1)}, bf16[32,1024]{1,0:T(8,128)(2,1)S(1)}, u32[]{:S(2)}, u32[]{:S(2)}) %collective-permute-start.25) | collective-permute-done | bytes 65568 | tf_op jit(solution)/shard_map/ppermute | solution.py:31
  120.6 3.3 collective-permute-start.26
  124.0 2.7 collective-permute-done.26.refs_3_
  126.9 3.9 %collective-permute-start.28 = (bf16[32,1024]{1,0:T(8,128)(2,1)S(1)}, bf16[32,1024]{1,0:T(8,128)(2,1)S(1)}, u32[]{:S(2)}, u32[]{:S(2)}) collective-permute-start(bf16[32,1024]{1,0:T(8,128)(2,1)S(1)} %get-tuple-element.173.refs_0_), channel_id=1, source_target_pairs={{0,8},{4,12},{8,0},{12,4},{1,9},{5,13},{9,1},{13,5},{2,10},{6,14},... | collective-permute-start | bytes 196616 | tf_op jit(solution)/shard_map/ppermute | solution.py:31
  132.0 2.5 collective-permute-done.28.refs_2_
  134.5 2.4 collective-permute-done.29.refs_3_
  136.9 2.0 shard_map.272
  140.3 3.2 collective-permute-done.33.refs_1_
  146.4 3.5 collective-permute-done.35.refs_3_
  151.7 2.9 collective-permute-start.38
  154.8 5.9 %collective-permute-done.37.refs_2_ = bf16[32,1024]{1,0:T(8,128)(2,1)S(1)} collective-permute-done((bf16[32,1024]{1,0:T(8,128)(2,1)S(1)}, bf16[32,1024]{1,0:T(8,128)(2,1)S(1)}, u32[]{:S(2)}, u32[]{:S(2)}) %collective-permute-start.37) | collective-permute-done | bytes 65568 | tf_op jit(solution)/shard_map/ppermute | solution.py:31
  163.4 3.4 collective-permute-done.50.refs_3_
  169.6 3.0 collective-permute-done.51.refs_1_
  173.6 2.1 collective-permute-start.53
  175.7 4.1 %collective-permute-done.53.refs_3_ = bf16[32,1024]{1,0:T(8,128)(2,1)S(1)} collective-permute-done((bf16[32,1024]{1,0:T(8,128)(2,1)S(1)}, bf16[32,1024]{1,0:T(8,128)(2,1)S(1)}, u32[]{:S(2)}, u32[]{:S(2)}) %collective-permute-start.53) | collective-permute-done | bytes 65568 | tf_op jit(solution)/shard_map/ppermute | solution.py:31
  191.3 2.3 collective-permute-start.58
  194.6 2.0 collective-permute-start.59
  204.3 2.4 collective-permute-start.61
  209.1 2.0 collective-permute-start.47
  215.9 2.2 collective-permute-start.63
  221.1 2.6 collective-permute-done.64.refs_2_
  225.6 4.2 %collective-permute-done.65.refs_3_ = bf16[32,1024]{1,0:T(8,128)(2,1)S(1)} collective-permute-done((bf16[32,1024]{1,0:T(8,128)(2,1)S(1)}, bf16[32,1024]{1,0:T(8,128)(2,1)S(1)}, u32[]{:S(2)}, u32[]{:S(2)}) %collective-permute-start.65) | collective-permute-done | bytes 65568 | tf_op jit(solution)/shard_map/ppermute | solution.py:31
  230.1 2.4 collective-permute-start.67
  236.1 2.7 collective-permute-done.67.refs_2_
  252.4 3.1 collective-permute-done.108.refs_6_
  256.3 4.2 %collective-permute-done.73.refs_2_ = f32[48,256]{1,0:T(8,128)S(1)} collective-permute-done((f32[48,256]{1,0:T(8,128)S(1)}, f32[48,256]{1,0:T(8,128)S(1)}, u32[]{:S(2)}, u32[]{:S(2)}) %collective-permute-start.73) | collective-permute-done | bytes 49184 | tf_op jit(solution)/shard_map/ppermute | solution.py:31
  263.2 8.1 %collective-permute-done.74.refs_3_ = f32[48,256]{1,0:T(8,128)S(1)} collective-permute-done((f32[48,256]{1,0:T(8,128)S(1)}, f32[48,256]{1,0:T(8,128)S(1)}, u32[]{:S(2)}, u32[]{:S(2)}) %collective-permute-start.74) | collective-permute-done | bytes 49184 | tf_op jit(solution)/shard_map/ppermute | solution.py:31
  273.0 4.1 %collective-permute-done.75.refs_1_ = f32[48,256]{1,0:T(8,128)S(1)} collective-permute-done((f32[48,256]{1,0:T(8,128)S(1)}, f32[48,256]{1,0:T(8,128)S(1)}, u32[]{:S(2)}, u32[]{:S(2)}) %collective-permute-start.75) | collective-permute-done | bytes 49184 | tf_op jit(solution)/shard_map/ppermute | solution.py:31
  281.9 2.1 collective-permute-done.76.refs_2_
  290.3 55.3 %collective-permute-done.114.other_ref = bf16[256,1024]{1,0:T(8,128)(2,1)S(1)} collective-permute-done((bf16[256,1024]{1,0:T(8,128)(2,1)S(1)}, bf16[256,1024]{1,0:T(8,128)(2,1)S(1)}, u32[]{:S(2)}, u32[]{:S(2)}) %collective-permute-start.114) | collective-permute-done | bytes 524320 | tf_op jit(solution)/shard_map/ppermute | solution.py:31
  (221 shorter events, 107.6 us)
Async XLA Ops:
  1.9 78.3 %collective-permute-start.22 = (bf16[256,2048]{1,0:T(8,128)(2,1)S(1)}, bf16[256,2048]{1,0:T(8,128)(2,1)S(1)}, u32[]{:S(2)}, u32[]{:S(2)}) collective-permute-start(bf16[256,2048]{1,0:T(8,128)(2,1)S(1)} %shard_map.268.refs_4_), channel_id=1, source_target_pairs={{0,2},{1,3},{2,0},{3,1},{4,6},{5,7},{6,4},{7,5},{8,10},{9,11},{10,... | collective-permute-start | bytes 3145736 | tf_op jit(solution)/shard_map/ppermute | solution.py:31
  6.2 73.5 %collective-permute-start.13 = (bf16[256,1024]{1,0:T(8,128)(2,1)S(1)}, bf16[256,1024]{1,0:T(8,128)(2,1)S(1)}, u32[]{:S(2)}, u32[]{:S(2)}) collective-permute-start(bf16[256,1024]{1,0:T(8,128)(2,1)S(1)} %get-tuple-element.158.refs_4_), channel_id=1, source_target_pairs={{0,2},{1,3},{2,0},{3,1},{4,6},{5,7},{6,4},{7,5},{8,10},{9,11},{10,... | collective-permute-start | bytes 1572872 | tf_op jit(solution)/shard_map/ppermute | solution.py:31
  7.5 77.7 %collective-permute-start.40 = (bf16[256,2048]{1,0:T(8,128)(2,1)S(1)}, bf16[256,2048]{1,0:T(8,128)(2,1)S(1)}, u32[]{:S(2)}, u32[]{:S(2)}) collective-permute-start(bf16[256,2048]{1,0:T(8,128)(2,1)S(1)} %shard_map.274.refs_4_), channel_id=1, source_target_pairs={{0,2},{1,3},{2,0},{3,1},{4,6},{5,7},{6,4},{7,5},{8,10},{9,11},{10,... | collective-permute-start | bytes 3145736 | tf_op jit(solution)/shard_map/ppermute | solution.py:31
  19.5 45.6 %collective-permute-start.3 = (bf16[32,512]{1,0:T(8,128)(2,1)S(1)}, bf16[32,512]{1,0:T(8,128)(2,1)S(1)}, u32[]{:S(2)}, u32[]{:S(2)}) collective-permute-start(bf16[32,512]{1,0:T(8,128)(2,1)S(1)} %get-tuple-element.152), channel_id=1, source_target_pairs={{0,1},{1,0},{2,3},{3,2},{4,5},{5,4},{6,7},{7,6},{8,9},{9,8},{10,11... | collective-permute-start | bytes 98312 | tf_op jit(solution)/shard_map/ppermute | solution.py:31
  19.6 42.6 %collective-permute-start.7 = (f32[12,256]{1,0:T(8,128)S(1)}, f32[12,256]{1,0:T(8,128)S(1)}, u32[]{:S(2)}, u32[]{:S(2)}) collective-permute-start(f32[12,256]{1,0:T(8,128)S(1)} %get-tuple-element.155.refs_4_.refs_10_), channel_id=1, source_target_pairs={{0,2},{1,3},{2,0},{3,1},{4,6},{5,7},{6,4},{7,5},{8,10},{9,11},{10,... | collective-permute-start | bytes 36872 | tf_op jit(solution)/shard_map/ppermute | solution.py:31
  79.7 17.1 %collective-permute-start.21 = (bf16[256,2048]{1,0:T(8,128)(2,1)S(1)}, bf16[256,2048]{1,0:T(8,128)(2,1)S(1)}, u32[]{:S(2)}, u32[]{:S(2)}) collective-permute-start(bf16[256,2048]{1,0:T(8,128)(2,1)S(1)} %shard_map.268.refs_4_), channel_id=1, source_target_pairs={{0,1},{1,0},{2,3},{3,2},{4,5},{5,4},{6,7},{7,6},{8,9},{9,8},{10,11... | collective-permute-start | bytes 3145736 | tf_op jit(solution)/shard_map/ppermute | solution.py:31
  80.2 28.3 %collective-permute-start.23 = (bf16[256,2048]{1,0:T(8,128)(2,1)S(1)}, bf16[256,2048]{1,0:T(8,128)(2,1)S(1)}, u32[]{:S(2)}, u32[]{:S(2)}) collective-permute-start(bf16[256,2048]{1,0:T(8,128)(2,1)S(1)} %collective-permute-done.22.refs_6_), channel_id=1, source_target_pairs={{0,1},{1,0},{2,3},{3,2},{4,5},{5,4},{6,7},{7,6},{8,9},{9,8},{10,11... | collective-permute-start | bytes 3145736 | tf_op jit(solution)/shard_map/ppermute | solution.py:31
  81.3 15.4 %collective-permute-start.31 = (bf16[256,1024]{1,0:T(8,128)(2,1)S(1)}, bf16[256,1024]{1,0:T(8,128)(2,1)S(1)}, u32[]{:S(2)}, u32[]{:S(2)}) collective-permute-start(bf16[256,1024]{1,0:T(8,128)(2,1)S(1)} %shard_map.271.refs_4_), channel_id=1, source_target_pairs={{0,2},{1,3},{2,0},{3,1},{4,6},{5,7},{6,4},{7,5},{8,10},{9,11},{10,... | collective-permute-start | bytes 1572872 | tf_op jit(solution)/shard_map/ppermute | solution.py:31
  85.2 9.1 %collective-permute-start.16 = (bf16[32,1024]{1,0:T(8,128)(2,1)S(1)}, bf16[32,1024]{1,0:T(8,128)(2,1)S(1)}, u32[]{:S(2)}, u32[]{:S(2)}) collective-permute-start(bf16[32,1024]{1,0:T(8,128)(2,1)S(1)} %get-tuple-element.163), channel_id=1, source_target_pairs={{0,8},{4,12},{8,0},{12,4},{1,9},{5,13},{9,1},{13,5},{2,10},{6,14},... | collective-permute-start | bytes 196616 | tf_op jit(solution)/shard_map/ppermute | solution.py:31
  94.3 57.4 %collective-permute-start.39 = (bf16[256,2048]{1,0:T(8,128)(2,1)S(1)}, bf16[256,2048]{1,0:T(8,128)(2,1)S(1)}, u32[]{:S(2)}, u32[]{:S(2)}) collective-permute-start(bf16[256,2048]{1,0:T(8,128)(2,1)S(1)} %shard_map.274.refs_4_), channel_id=1, source_target_pairs={{0,1},{1,0},{2,3},{3,2},{4,5},{5,4},{6,7},{7,6},{8,9},{9,8},{10,11... | collective-permute-start | bytes 3145736 | tf_op jit(solution)/shard_map/ppermute | solution.py:31
  96.6 58.1 %collective-permute-start.41 = (bf16[256,2048]{1,0:T(8,128)(2,1)S(1)}, bf16[256,2048]{1,0:T(8,128)(2,1)S(1)}, u32[]{:S(2)}, u32[]{:S(2)}) collective-permute-start(bf16[256,2048]{1,0:T(8,128)(2,1)S(1)} %collective-permute-done.40.refs_6_), channel_id=1, source_target_pairs={{0,1},{1,0},{2,3},{3,2},{4,5},{5,4},{6,7},{7,6},{8,9},{9,8},{10,11... | collective-permute-start | bytes 3145736 | tf_op jit(solution)/shard_map/ppermute | solution.py:31
  96.8 9.5 %collective-permute-start.19 = (bf16[32,1024]{1,0:T(8,128)(2,1)S(1)}, bf16[32,1024]{1,0:T(8,128)(2,1)S(1)}, u32[]{:S(2)}, u32[]{:S(2)}) collective-permute-start(bf16[32,1024]{1,0:T(8,128)(2,1)S(1)} %get-tuple-element.166.refs_0_), channel_id=1, source_target_pairs={{0,8},{4,12},{8,0},{12,4},{1,9},{5,13},{9,1},{13,5},{2,10},{6,14},... | collective-permute-start | bytes 196616 | tf_op jit(solution)/shard_map/ppermute | solution.py:31
  106.3 20.6 %collective-permute-start.30 = (bf16[256,1024]{1,0:T(8,128)(2,1)S(1)}, bf16[256,1024]{1,0:T(8,128)(2,1)S(1)}, u32[]{:S(2)}, u32[]{:S(2)}) collective-permute-start(bf16[256,1024]{1,0:T(8,128)(2,1)S(1)} %shard_map.271.refs_4_), channel_id=1, source_target_pairs={{0,1},{1,0},{2,3},{3,2},{4,5},{5,4},{6,7},{7,6},{8,9},{9,8},{10,11... | collective-permute-start | bytes 1572872 | tf_op jit(solution)/shard_map/ppermute | solution.py:31
  108.5 22.3 %collective-permute-start.32 = (bf16[256,1024]{1,0:T(8,128)(2,1)S(1)}, bf16[256,1024]{1,0:T(8,128)(2,1)S(1)}, u32[]{:S(2)}, u32[]{:S(2)}) collective-permute-start(bf16[256,1024]{1,0:T(8,128)(2,1)S(1)} %collective-permute-done.31.refs_6_), channel_id=1, source_target_pairs={{0,1},{1,0},{2,3},{3,2},{4,5},{5,4},{6,7},{7,6},{8,9},{9,8},{10,11... | collective-permute-start | bytes 1572872 | tf_op jit(solution)/shard_map/ppermute | solution.py:31
  131.3 20.4 %collective-permute-start.94 = (bf16[128,768]{1,0:T(8,128)(2,1)S(1)}, bf16[128,768]{1,0:T(8,128)(2,1)S(1)}, u32[]{:S(2)}, u32[]{:S(2)}) collective-permute-start(bf16[128,768]{1,0:T(8,128)(2,1)S(1)} %get-tuple-element.248), channel_id=1, source_target_pairs={{0,2},{1,3},{2,0},{3,1},{4,6},{5,7},{6,4},{7,5},{8,10},{9,11},{10,... | collective-permute-start | bytes 589832 | tf_op jit(solution)/shard_map/ppermute | solution.py:31
  150.7 10.1 %collective-permute-start.37 = (bf16[32,1024]{1,0:T(8,128)(2,1)S(1)}, bf16[32,1024]{1,0:T(8,128)(2,1)S(1)}, u32[]{:S(2)}, u32[]{:S(2)}) collective-permute-start(bf16[32,1024]{1,0:T(8,128)(2,1)S(1)} %get-tuple-element.178.refs_0_), channel_id=1, source_target_pairs={{0,8},{4,12},{8,0},{12,4},{1,9},{5,13},{9,1},{13,5},{2,10},{6,14},... | collective-permute-start | bytes 196616 | tf_op jit(solution)/shard_map/ppermute | solution.py:31
  151.7 31.5 %collective-permute-start.79 = (bf16[128,1280]{1,0:T(8,128)(2,1)S(1)}, bf16[128,1280]{1,0:T(8,128)(2,1)S(1)}, u32[]{:S(2)}, u32[]{:S(2)}) collective-permute-start(bf16[128,1280]{1,0:T(8,128)(2,1)S(1)} %get-tuple-element.237), channel_id=1, source_target_pairs={{0,1},{1,0},{2,3},{3,2},{4,5},{5,4},{6,7},{7,6},{8,9},{9,8},{10,11... | collective-permute-start | bytes 983048 | tf_op jit(solution)/shard_map/ppermute | solution.py:31
  151.7 9.0 %collective-permute-start.38 = (bf16[32,1024]{1,0:T(8,128)(2,1)S(1)}, bf16[32,1024]{1,0:T(8,128)(2,1)S(1)}, u32[]{:S(2)}, u32[]{:S(2)}) collective-permute-start(bf16[32,1024]{1,0:T(8,128)(2,1)S(1)} %get-tuple-element.178.refs_0_), channel_id=1, source_target_pairs={{0,12},{4,8},{8,4},{12,0},{1,13},{5,9},{9,5},{13,1},{2,14},{6,10},... | collective-permute-start | bytes 196616 | tf_op jit(solution)/shard_map/ppermute | solution.py:31
  154.7 14.3 %collective-permute-start.93 = (bf16[128,512]{1,0:T(8,128)(2,1)S(1)}, bf16[128,512]{1,0:T(8,128)(2,1)S(1)}, u32[]{:S(2)}, u32[]{:S(2)}) collective-permute-start(bf16[128,512]{1,0:T(8,128)(2,1)S(1)} %get-tuple-element.247), channel_id=1, source_target_pairs={{0,1},{1,0},{2,3},{3,2},{4,5},{5,4},{6,7},{7,6},{8,9},{9,8},{10,11... | collective-permute-start | bytes 393224 | tf_op jit(solution)/shard_map/ppermute | solution.py:31
  154.8 8.6 %collective-permute-start.49 = (bf16[32,1024]{1,0:T(8,128)(2,1)S(1)}, bf16[32,1024]{1,0:T(8,128)(2,1)S(1)}, u32[]{:S(2)}, u32[]{:S(2)}) collective-permute-start(bf16[32,1024]{1,0:T(8,128)(2,1)S(1)} %get-tuple-element.188.refs_0_.grad_ref), channel_id=1, source_target_pairs={{0,8},{4,12},{8,0},{12,4},{1,9},{5,13},{9,1},{13,5},{2,10},{6,14},... | collective-permute-start | bytes 196616 | tf_op jit(solution)/shard_map/ppermute | solution.py:31
  160.7 19.9 %collective-permute-start.95 = (bf16[128,768]{1,0:T(8,128)(2,1)S(1)}, bf16[128,768]{1,0:T(8,128)(2,1)S(1)}, u32[]{:S(2)}, u32[]{:S(2)}) collective-permute-start(bf16[128,768]{1,0:T(8,128)(2,1)S(1)} %collective-permute-done.94.refs_2_), channel_id=1, source_target_pairs={{0,1},{1,0},{2,3},{3,2},{4,5},{5,4},{6,7},{7,6},{8,9},{9,8},{10,11... | collective-permute-start | bytes 589832 | tf_op jit(solution)/shard_map/ppermute | solution.py:31
  168.9 34.6 %collective-permute-start.80 = (bf16[128,1536]{1,0:T(8,128)(2,1)S(1)}, bf16[128,1536]{1,0:T(8,128)(2,1)S(1)}, u32[]{:S(2)}, u32[]{:S(2)}) collective-permute-start(bf16[128,1536]{1,0:T(8,128)(2,1)S(1)} %get-tuple-element.238), channel_id=1, source_target_pairs={{0,2},{1,3},{2,0},{3,1},{4,6},{5,7},{6,4},{7,5},{8,10},{9,11},{10,... | collective-permute-start | bytes 1179656 | tf_op jit(solution)/shard_map/ppermute | solution.py:31
  172.6 8.8 %collective-permute-start.100 = (bf16[128,512]{1,0:T(8,128)(2,1)S(1)}, bf16[128,512]{1,0:T(8,128)(2,1)S(1)}, u32[]{:S(2)}, u32[]{:S(2)}) collective-permute-start(bf16[128,512]{1,0:T(8,128)(2,1)S(1)} %get-tuple-element.252), channel_id=1, source_target_pairs={{0,1},{1,0},{2,3},{3,2},{4,5},{5,4},{6,7},{7,6},{8,9},{9,8},{10,11... | collective-permute-start | bytes 393224 | tf_op jit(solution)/shard_map/ppermute | solution.py:31
  179.8 14.8 %collective-permute-start.101 = (bf16[128,768]{1,0:T(8,128)(2,1)S(1)}, bf16[128,768]{1,0:T(8,128)(2,1)S(1)}, u32[]{:S(2)}, u32[]{:S(2)}) collective-permute-start(bf16[128,768]{1,0:T(8,128)(2,1)S(1)} %get-tuple-element.253), channel_id=1, source_target_pairs={{0,2},{1,3},{2,0},{3,1},{4,6},{5,7},{6,4},{7,5},{8,10},{9,11},{10,... | collective-permute-start | bytes 589832 | tf_op jit(solution)/shard_map/ppermute | solution.py:31
  193.7 25.0 %collective-permute-start.89 = (bf16[128,1024]{1,0:T(8,128)(2,1)S(1)}, bf16[128,1024]{1,0:T(8,128)(2,1)S(1)}, u32[]{:S(2)}, u32[]{:S(2)}) collective-permute-start(bf16[128,1024]{1,0:T(8,128)(2,1)S(1)} %get-tuple-element.243.refs_4_), channel_id=1, source_target_pairs={{0,1},{1,0},{2,3},{3,2},{4,5},{5,4},{6,7},{7,6},{8,9},{9,8},{10,11... | collective-permute-start | bytes 786440 | tf_op jit(solution)/shard_map/ppermute | solution.py:31
  203.5 14.6 %collective-permute-start.112 = (bf16[128,512]{1,0:T(8,128)(2,1)S(1)}, bf16[128,512]{1,0:T(8,128)(2,1)S(1)}, u32[]{:S(2)}, u32[]{:S(2)}) collective-permute-start(bf16[128,512]{1,0:T(8,128)(2,1)S(1)} %get-tuple-element.277), channel_id=1, source_target_pairs={{0,2},{1,3},{2,0},{3,1},{4,6},{5,7},{6,4},{7,5},{8,10},{9,11},{10,... | collective-permute-start | bytes 393224 | tf_op jit(solution)/shard_map/ppermute | solution.py:31
  212.3 22.2 %collective-permute-start.86 = (bf16[128,1280]{1,0:T(8,128)(2,1)S(1)}, bf16[128,1280]{1,0:T(8,128)(2,1)S(1)}, u32[]{:S(2)}, u32[]{:S(2)}) collective-permute-start(bf16[128,1280]{1,0:T(8,128)(2,1)S(1)} %get-tuple-element.241), channel_id=1, source_target_pairs={{0,1},{1,0},{2,3},{3,2},{4,5},{5,4},{6,7},{7,6},{8,9},{9,8},{10,11... | collective-permute-start | bytes 983048 | tf_op jit(solution)/shard_map/ppermute | solution.py:31
  213.4 16.6 %collective-permute-start.90 = (bf16[128,1024]{1,0:T(8,128)(2,1)S(1)}, bf16[128,1024]{1,0:T(8,128)(2,1)S(1)}, u32[]{:S(2)}, u32[]{:S(2)}) collective-permute-start(bf16[128,1024]{1,0:T(8,128)(2,1)S(1)} %get-tuple-element.243.refs_4_), channel_id=1, source_target_pairs={{0,2},{1,3},{2,0},{3,1},{4,6},{5,7},{6,4},{7,5},{8,10},{9,11},{10,... | collective-permute-start | bytes 786440 | tf_op jit(solution)/shard_map/ppermute | solution.py:31
  218.7 23.6 %collective-permute-start.87 = (bf16[128,1536]{1,0:T(8,128)(2,1)S(1)}, bf16[128,1536]{1,0:T(8,128)(2,1)S(1)}, u32[]{:S(2)}, u32[]{:S(2)}) collective-permute-start(bf16[128,1536]{1,0:T(8,128)(2,1)S(1)} %get-tuple-element.242), channel_id=1, source_target_pairs={{0,2},{1,3},{2,0},{3,1},{4,6},{5,7},{6,4},{7,5},{8,10},{9,11},{10,... | collective-permute-start | bytes 1179656 | tf_op jit(solution)/shard_map/ppermute | solution.py:31
  221.1 9.0 %collective-permute-start.102 = (bf16[128,768]{1,0:T(8,128)(2,1)S(1)}, bf16[128,768]{1,0:T(8,128)(2,1)S(1)}, u32[]{:S(2)}, u32[]{:S(2)}) collective-permute-start(bf16[128,768]{1,0:T(8,128)(2,1)S(1)} %collective-permute-done.101.refs_2_), channel_id=1, source_target_pairs={{0,1},{1,0},{2,3},{3,2},{4,5},{5,4},{6,7},{7,6},{8,9},{9,8},{10,11... | collective-permute-start | bytes 589832 | tf_op jit(solution)/shard_map/ppermute | solution.py:31
  230.1 8.8 %collective-permute-start.67 = (bf16[32,1024]{1,0:T(8,128)(2,1)S(1)}, bf16[32,1024]{1,0:T(8,128)(2,1)S(1)}, u32[]{:S(2)}, u32[]{:S(2)}) collective-permute-start(bf16[32,1024]{1,0:T(8,128)(2,1)S(1)} %get-tuple-element.215.refs_0_), channel_id=1, source_target_pairs={{0,8},{4,12},{8,0},{12,4},{1,9},{5,13},{9,1},{13,5},{2,10},{6,14},... | collective-permute-start | bytes 196616 | tf_op jit(solution)/shard_map/ppermute | solution.py:31
  234.4 26.1 %collective-permute-start.81 = (bf16[128,1536]{1,0:T(8,128)(2,1)S(1)}, bf16[128,1536]{1,0:T(8,128)(2,1)S(1)}, u32[]{:S(2)}, u32[]{:S(2)}) collective-permute-start(bf16[128,1536]{1,0:T(8,128)(2,1)S(1)} %collective-permute-done.80.refs_2_), channel_id=1, source_target_pairs={{0,1},{1,0},{2,3},{3,2},{4,5},{5,4},{6,7},{7,6},{8,9},{9,8},{10,11... | collective-permute-start | bytes 1179656 | tf_op jit(solution)/shard_map/ppermute | solution.py:31
  235.6 19.9 %collective-permute-start.104 = (bf16[128,1280]{1,0:T(8,128)(2,1)S(1)}, bf16[128,1280]{1,0:T(8,128)(2,1)S(1)}, u32[]{:S(2)}, u32[]{:S(2)}) collective-permute-start(bf16[128,1280]{1,0:T(8,128)(2,1)S(1)} %get-tuple-element.256), channel_id=1, source_target_pairs={{0,2},{1,3},{2,0},{3,1},{4,6},{5,7},{6,4},{7,5},{8,10},{9,11},{10,... | collective-permute-start | bytes 983048 | tf_op jit(solution)/shard_map/ppermute | solution.py:31
  238.8 13.5 %collective-permute-start.103 = (bf16[128,1024]{1,0:T(8,128)(2,1)S(1)}, bf16[128,1024]{1,0:T(8,128)(2,1)S(1)}, u32[]{:S(2)}, u32[]{:S(2)}) collective-permute-start(bf16[128,1024]{1,0:T(8,128)(2,1)S(1)} %get-tuple-element.255), channel_id=1, source_target_pairs={{0,1},{1,0},{2,3},{3,2},{4,5},{5,4},{6,7},{7,6},{8,9},{9,8},{10,11... | collective-permute-start | bytes 786440 | tf_op jit(solution)/shard_map/ppermute | solution.py:31
  251.7 9.4 %collective-permute-start.83 = (bf16[128,1024]{1,0:T(8,128)(2,1)S(1)}, bf16[128,1024]{1,0:T(8,128)(2,1)S(1)}, u32[]{:S(2)}, u32[]{:S(2)}) collective-permute-start(bf16[128,1024]{1,0:T(8,128)(2,1)S(1)} %get-tuple-element.239.refs_4_), channel_id=1, source_target_pairs={{0,2},{1,3},{2,0},{3,1},{4,6},{5,7},{6,4},{7,5},{8,10},{9,11},{10,... | collective-permute-start | bytes 786440 | tf_op jit(solution)/shard_map/ppermute | solution.py:31
  255.5 17.3 %collective-permute-start.91 = (bf16[128,1024]{1,0:T(8,128)(2,1)S(1)}, bf16[128,1024]{1,0:T(8,128)(2,1)S(1)}, u32[]{:S(2)}, u32[]{:S(2)}) collective-permute-start(bf16[128,1024]{1,0:T(8,128)(2,1)S(1)} %collective-permute-done.90.refs_6_), channel_id=1, source_target_pairs={{0,1},{1,0},{2,3},{3,2},{4,5},{5,4},{6,7},{7,6},{8,9},{9,8},{10,11... | collective-permute-start | bytes 786440 | tf_op jit(solution)/shard_map/ppermute | solution.py:31
  256.1 16.8 %collective-permute-start.82 = (bf16[128,1024]{1,0:T(8,128)(2,1)S(1)}, bf16[128,1024]{1,0:T(8,128)(2,1)S(1)}, u32[]{:S(2)}, u32[]{:S(2)}) collective-permute-start(bf16[128,1024]{1,0:T(8,128)(2,1)S(1)} %get-tuple-element.239.refs_4_), channel_id=1, source_target_pairs={{0,1},{1,0},{2,3},{3,2},{4,5},{5,4},{6,7},{7,6},{8,9},{9,8},{10,11... | collective-permute-start | bytes 786440 | tf_op jit(solution)/shard_map/ppermute | solution.py:31
  260.5 16.6 %collective-permute-start.97 = (bf16[128,1280]{1,0:T(8,128)(2,1)S(1)}, bf16[128,1280]{1,0:T(8,128)(2,1)S(1)}, u32[]{:S(2)}, u32[]{:S(2)}) collective-permute-start(bf16[128,1280]{1,0:T(8,128)(2,1)S(1)} %get-tuple-element.251), channel_id=1, source_target_pairs={{0,2},{1,3},{2,0},{3,1},{4,6},{5,7},{6,4},{7,5},{8,10},{9,11},{10,... | collective-permute-start | bytes 983048 | tf_op jit(solution)/shard_map/ppermute | solution.py:31
  261.0 10.2 %collective-permute-start.74 = (f32[48,256]{1,0:T(8,128)S(1)}, f32[48,256]{1,0:T(8,128)S(1)}, u32[]{:S(2)}, u32[]{:S(2)}) collective-permute-start(f32[48,256]{1,0:T(8,128)S(1)} %get-tuple-element.229), channel_id=1, source_target_pairs={{0,3},{1,2},{2,1},{3,0},{4,7},{5,6},{6,5},{7,4},{8,11},{9,10},{10,... | collective-permute-start | bytes 147464 | tf_op jit(solution)/shard_map/ppermute | solution.py:31
  262.4 15.2 %collective-permute-start.84 = (bf16[128,1024]{1,0:T(8,128)(2,1)S(1)}, bf16[128,1024]{1,0:T(8,128)(2,1)S(1)}, u32[]{:S(2)}, u32[]{:S(2)}) collective-permute-start(bf16[128,1024]{1,0:T(8,128)(2,1)S(1)} %collective-permute-done.83.refs_6_), channel_id=1, source_target_pairs={{0,1},{1,0},{2,3},{3,2},{4,5},{5,4},{6,7},{7,6},{8,9},{9,8},{10,11... | collective-permute-start | bytes 786440 | tf_op jit(solution)/shard_map/ppermute | solution.py:31
  271.3 17.9 %collective-permute-start.110 = (bf16[256,1024]{1,0:T(8,128)(2,1)S(1)}, bf16[256,1024]{1,0:T(8,128)(2,1)S(1)}, u32[]{:S(2)}, u32[]{:S(2)}) collective-permute-start(bf16[256,1024]{1,0:T(8,128)(2,1)S(1)} %shard_map.297.own_ref), channel_id=1, source_target_pairs={{0,16},{16,0},{1,17},{17,1},{2,18},{18,2},{3,19},{19,3},{4,20},{20... | collective-permute-start | bytes 1572872 | tf_op jit(solution)/shard_map/ppermute | solution.py:31
  277.1 9.0 %collective-permute-start.98 = (bf16[128,1280]{1,0:T(8,128)(2,1)S(1)}, bf16[128,1280]{1,0:T(8,128)(2,1)S(1)}, u32[]{:S(2)}, u32[]{:S(2)}) collective-permute-start(bf16[128,1280]{1,0:T(8,128)(2,1)S(1)} %collective-permute-done.97.refs_6_), channel_id=1, source_target_pairs={{0,1},{1,0},{2,3},{3,2},{4,5},{5,4},{6,7},{7,6},{8,9},{9,8},{10,11... | collective-permute-start | bytes 983048 | tf_op jit(solution)/shard_map/ppermute | solution.py:31
  278.7 8.3 %collective-permute-start.77 = (f32[48,256]{1,0:T(8,128)S(1)}, f32[48,256]{1,0:T(8,128)S(1)}, u32[]{:S(2)}, u32[]{:S(2)}) collective-permute-start(f32[48,256]{1,0:T(8,128)S(1)} %get-tuple-element.233), channel_id=1, source_target_pairs={{0,12},{4,8},{8,4},{12,0},{1,13},{5,9},{9,5},{13,1},{2,14},{6,10},... | collective-permute-start | bytes 147464 | tf_op jit(solution)/shard_map/ppermute | solution.py:31
  284.0 64.9 %collective-permute-start.92 = (bf16[272,1024]{1,0:T(8,128)(2,1)S(1)}, bf16[272,1024]{1,0:T(8,128)(2,1)S(1)}, u32[]{:S(2)}, u32[]{:S(2)}) collective-permute-start(bf16[272,1024]{1,0:T(8,128)(2,1)S(1)} %shard_map.289.own_ref), channel_id=1, source_target_pairs={{0,16},{16,0},{1,17},{17,1},{2,18},{18,2},{3,19},{19,3},{4,20},{20... | collective-permute-start | bytes 1671176 | tf_op jit(solution)/shard_map/ppermute | solution.py:31
  284.5 65.5 %collective-permute-start.106 = (bf16[272,1024]{1,0:T(8,128)(2,1)S(1)}, bf16[272,1024]{1,0:T(8,128)(2,1)S(1)}, u32[]{:S(2)}, u32[]{:S(2)}) collective-permute-start(bf16[272,1024]{1,0:T(8,128)(2,1)S(1)} %shard_map.293.own_ref), channel_id=1, source_target_pairs={{0,16},{16,0},{1,17},{17,1},{2,18},{18,2},{3,19},{19,3},{4,20},{20... | collective-permute-start | bytes 1671176 | tf_op jit(solution)/shard_map/ppermute | solution.py:31
  286.0 65.0 %collective-permute-start.85 = (bf16[272,1024]{1,0:T(8,128)(2,1)S(1)}, bf16[272,1024]{1,0:T(8,128)(2,1)S(1)}, u32[]{:S(2)}, u32[]{:S(2)}) collective-permute-start(bf16[272,1024]{1,0:T(8,128)(2,1)S(1)} %shard_map.288.own_ref), channel_id=1, source_target_pairs={{0,16},{16,0},{1,17},{17,1},{2,18},{18,2},{3,19},{19,3},{4,20},{20... | collective-permute-start | bytes 1671176 | tf_op jit(solution)/shard_map/ppermute | solution.py:31
  287.0 65.1 %collective-permute-start.99 = (bf16[272,1024]{1,0:T(8,128)(2,1)S(1)}, bf16[272,1024]{1,0:T(8,128)(2,1)S(1)}, u32[]{:S(2)}, u32[]{:S(2)}) collective-permute-start(bf16[272,1024]{1,0:T(8,128)(2,1)S(1)} %shard_map.292.own_ref), channel_id=1, source_target_pairs={{0,16},{16,0},{1,17},{17,1},{2,18},{18,2},{3,19},{19,3},{4,20},{20... | collective-permute-start | bytes 1671176 | tf_op jit(solution)/shard_map/ppermute | solution.py:31
  289.1 56.5 %collective-permute-start.114 = (bf16[256,1024]{1,0:T(8,128)(2,1)S(1)}, bf16[256,1024]{1,0:T(8,128)(2,1)S(1)}, u32[]{:S(2)}, u32[]{:S(2)}) collective-permute-start(bf16[256,1024]{1,0:T(8,128)(2,1)S(1)} %shard_map.298.own_ref), channel_id=1, source_target_pairs={{0,16},{16,0},{1,17},{17,1},{2,18},{18,2},{3,19},{19,3},{4,20},{20... | collective-permute-start | bytes 1572872 | tf_op jit(solution)/shard_map/ppermute | solution.py:31
  (67 other events, 354.6 us)

commit v2 on v1

--- a/solution.py
+++ b/solution.py
@@ -166,40 +166,6 @@
         )
         at += columns
     return copies
-
-
-def start_blocks(block_input, cotangent, joined, output, size):
-    rows = block_input.shape[0] // size
-    width = block_input.shape[1]
-    pieces = weight_pieces(joined.shape[2], output.shape[2], 0, joined.shape[1], True)
-    total = sum(piece[2] for piece in pieces)
-
-    def kernel(input_ref, cotangent_ref, joined_ref, output_ref, *refs):
-        outs, pack_ref, sems, pack_sems = refs[:size], *refs[size:]
-        copies = []
-        for step in range(size):
-            here = slice(step * rows, (step + 1) * rows)
-            copies.append(
-                pltpu.make_async_copy(
-                    input_ref.at[here], outs[step].at[:, :width], sems.at[2 * step]
-                )
-            )
-            copies.append(
-                pltpu.make_async_copy(
-                    cotangent_ref.at[here], outs[step].at[:, width:], sems.at[2 * step + 1]
-                )
-            )
-        copies += pack_copies((joined_ref, output_ref), pack_ref, pack_sems, pieces)
-        start_copies(copies)
-
-    outs = run(
-        kernel,
-        [in_hbm(array) for array in (block_input, cotangent, joined, output)],
-        [shaped((rows, 2 * width), BF)] * size + [shaped((joined.shape[1], total), BF)],
-        [pltpu.SemaphoreType.DMA((2 * size,)), pltpu.SemaphoreType.DMA((len(pieces),))],
-        HBM,
-    )
-    return outs[:size], outs[size]
 
 
 def start_vectors(vectors, biases):
@@ -243,11 +209,11 @@
         for at in range(size):
             turn[at] = block_refs[at][:rows, :]
         if extra:
-            total = tree_sum([ref[rows:, :] for ref in block_refs])
+            total = tree_sum([wide(ref[rows:, :]) for ref in block_refs])
         for at in range(size):
             out_refs[at][:rows, :] = turn[at ^ shift]
             if extra:
-                out_refs[at][rows:, :] = total
+                out_refs[at][rows:, :] = total.astype(out_refs[at].dtype)
 
     shape, dtype = blocks[0].shape, blocks[0].dtype
     return run(
@@ -276,37 +242,54 @@
     )(in_hbm(one), in_hbm(two))
 
 
-def first_norm(got, vecs):
-    size = len(got)
-    rows, width = got[0].shape[0], got[0].shape[1] // 2
-
-    def kernel(*refs):
-        got_refs = refs[:size]
-        vec_refs = refs[size : size + len(vecs)]
-        resid_ref, cotangent_ref, input_ref, stats_ref = refs[size + len(vecs) :]
-        whole = [ref[...] for ref in got_refs]
-        resid = jnp.concatenate([wide(part[:, :width]) for part in whole], axis=1)
-        cotangent_ref[...] = jnp.concatenate([part[:, width:] for part in whole], axis=1)
-        resid_ref[...] = resid
-        norm_into(
-            resid,
-            vector_row(vec_refs, GAIN_ONE * LAYERS),
-            vector_row(vec_refs, SHIFT_ONE * LAYERS),
-            input_ref,
-            stats_ref,
-        )
-
-    full = size * width
-    return run(
+def own_rows(blocks, step, rows):
+    at = pl.multiple_of((lax.axis_index(ROW) ^ step) * rows, rows)
+    return jnp.concatenate([ref[pl.ds(at, rows), :] for ref in blocks], axis=1)
+
+
+def first_norm(got, vecs, size):
+    cols = len(got)
+    length, width = got[0].shape
+    rows, full = length // size, width * cols
+
+    def kernel(*refs):
+        got_refs = refs[:cols]
+        vec_refs = refs[cols : 2 * cols]
+        resid_ref, normed_ref, scale_ref = refs[2 * cols : 2 * cols + 3]
+        input_refs = refs[2 * cols + 3 :]
+        gain = vector_row(vec_refs, GAIN_ONE * LAYERS)
+        shift = vector_row(vec_refs, SHIFT_ONE * LAYERS)
+        for step in range(size):
+            here = slice(step * rows, (step + 1) * rows)
+            resid = wide(own_rows(got_refs, step, rows))
+            if not step:
+                resid_ref[...] = resid
+            mean = jnp.mean(resid, axis=1, keepdims=True)
+            spread_out = jnp.mean(resid * resid, axis=1, keepdims=True) - mean * mean
+            scale = lax.rsqrt(spread_out + norm_epsilon)
+            normed = (resid - mean) * scale
+            normed_ref[here, :] = normed
+            scale_ref[here, :] = jnp.broadcast_to(scale, (rows, 128))
+            input_refs[step][...] = low(normed * gain + shift)
+
+    outs = run(
         kernel,
         [*got, *vecs],
-        [
-            shaped((rows, full), F32),
-            shaped((rows, full), BF),
-            shaped((rows, full), BF),
-            shaped((rows, 256), F32),
-        ],
-    )
+        [shaped((rows, full), F32), shaped((length, full), F32), shaped((length, 128), F32)]
+        + [shaped((rows, full), BF)] * size,
+    )
+    return outs[0], (outs[1], outs[2]), outs[3:]
+
+
+def row_blocks(got, size):
+    length, width = got[0].shape
+    rows = length // size
+
+    def kernel(*refs):
+        for step in range(size):
+            refs[len(got) + step][...] = own_rows(refs[: len(got)], step, rows)
+
+    return run(kernel, list(got), [shaped((rows, width * len(got)), BF)] * size)
 
 
 def next_norm(resid, parts, vecs, layer, bias_at, gain_at, shift_at):
@@ -342,6 +325,17 @@
         ref[...] = value[at * rows : (at + 1) * rows]
 
 
+def cut_turned(partial, ours, refs):
+    rows, width = ours.shape[0], refs[0].shape[1]
+    for step in range(partial.shape[0] // rows):
+        block = partial[step * rows : (step + 1) * rows]
+        if not step:
+            block = block + ours
+        at = pl.multiple_of((lax.axis_index(ROW) ^ step) * rows, rows)
+        for place, ref in enumerate(refs):
+            ref[pl.ds(at, rows), :] = low(block[:, place * width : (place + 1) * width])
+
+
 def gathered(refs):
     return jnp.concatenate([ref[...] for ref in refs], axis=0)
 
@@ -372,11 +366,10 @@
             ]
         )
         row = lax.axis_index(ROW)
-        turn = row ^ lax.axis_index(COL)
 
         def where_is(axis):
             index = lax.broadcasted_iota(jnp.int32, (length, length), axis)
-            return ((lax.shift_right_logical(index, shift) ^ turn) << shift) + (index & (rows - 1))
+            return ((lax.shift_right_logical(index, shift) ^ row) << shift) + (index & (rows - 1))
 
         offset = wide(where_is(1) - where_is(0))
         allowed = offset <= 0.0
@@ -486,14 +479,7 @@
         )
         if vecs:
             bias = vector_row(more[1:], BIAS_DOWN * LAYERS + layer)
-            shift = lax.axis_index(ROW) ^ lax.axis_index(COL)
-            for step in range(size):
-                block = partial[step * rows : (step + 1) * rows]
-                if not step:
-                    block = block + more[0][...] + bias
-                at = pl.multiple_of((step ^ shift) * rows, rows)
-                for place, ref in enumerate(part_refs):
-                    ref[pl.ds(at, rows), :] = low(block[:, place * width : (place + 1) * width])
+            cut_turned(partial, more[0][...] + bias, part_refs)
         else:
             cut_rows(low(partial), part_refs)
         bundle_into(send_refs, steps, [hidden], [full_second], width)
@@ -557,6 +543,17 @@
     return outs[:size], outs[size], outs[size + 1 :]
 
 
+def bundle_blocks(blocks, cols):
+    rows, full = blocks[0].shape
+    width = full // cols
+    steps = sends_of(cols)
+
+    def kernel(*refs):
+        bundle_into(refs[len(blocks) :], steps, [], [gathered(refs[: len(blocks)])], width)
+
+    return run(kernel, list(blocks), bundle_shapes(len(blocks) * rows, steps, 0, 1, width))
+
+
 def norm_back_math(grad_in, part_refs, resid_ref, stats_ref, gain):
     grad_out = tree_sum([wide(ref[...]) for ref in part_refs])
     half = stats_ref.shape[1] // 2
@@ -604,38 +601,7 @@
     )
 
 
-def last_backward(grad_resid, parts, resid, stats, vecs, other_sums, extra):
-    count = len(parts)
-    rows, full = grad_resid.shape
-    cols = len(vecs)
-    width = full // cols
-
-    def kernel(grad_ref, resid_ref, stats_ref, *refs):
-        part_refs = refs[:count]
-        vec_refs = refs[count : count + cols]
-        sums_refs = refs[count + cols : count + cols + len(other_sums)]
-        out_refs = refs[count + cols + len(other_sums) :]
-        total, sums = norm_back_math(
-            grad_ref[...], part_refs, resid_ref, stats_ref, vector_row(vec_refs, GAIN_ONE * LAYERS)
-        )
-        lines = list(sums)
-        for ref in sums_refs:
-            lines += [ref[at : at + 1, :] for at in range(ref.shape[0])]
-        for place in range(cols):
-            here = slice(place * width, (place + 1) * width)
-            out_refs[place][:rows, :] = total[:, here]
-            out_refs[place][rows:, :] = jnp.zeros((extra, width), F32)
-            for at, line in enumerate(lines):
-                out_refs[place][rows + at : rows + at + 1, :] = line[:, here]
-
-    return run(
-        kernel,
-        [grad_resid, resid, stats, *parts, *vecs, *other_sums],
-        [shaped((rows + extra, width), F32)] * cols,
-    )
-
-
-def attention_backward(blocks, packs, qkv, probs, mixed, across):
+def attention_backward(blocks, packs, qkv, probs, mixed, across, last=None):
     size, cols = len(blocks), len(packs)
     rows, full = blocks[0].shape
     length = size * rows
@@ -643,12 +609,22 @@
     heads = across // HD
     factor = 1.0 / math.sqrt(HD)
 
+    extra = []
+    parts = [shaped((rows, full), BF)] * size
+    sends = bundle_shapes(length, sends_of(cols), 3 * across, 1, width)
+    if last:
+        sends = [shaped((length, 3 * across), BF)]
+        kept, grad_middle, vecs, other_sums = last
+        extra = [*kept, grad_middle, *vecs, *other_sums]
+        parts = [shaped((length + 16, width), BF)] * cols
+
     def kernel(*refs):
         block_refs = refs[:size]
         pack_refs = refs[size : size + cols]
         qkv_ref, probs_ref, mixed_ref = refs[size + cols : size + cols + 3]
-        part_refs = refs[size + cols + 3 : 2 * size + cols + 3]
-        send_refs = refs[2 * size + cols + 3 :]
+        more = refs[size + cols + 3 : size + cols + 3 + len(extra)]
+        part_refs = refs[size + cols + 3 + len(extra) :][: len(parts)]
+        send_refs = refs[size + cols + 3 + len(extra) + len(parts) :]
         joined_ref = send_refs[0]
         full_middle = gathered(block_refs)
         grad_mixed = low(
@@ -679,19 +655,38 @@
             joined_ref[:, at + 2 * HD : at + 3 * HD] = low(value_sum)
         grad_joined = joined_ref[:, : 3 * across]
         partial = jnp.concatenate(
-            [low(dot_right(grad_joined, pack_ref[:, : 3 * across])) for pack_ref in pack_refs],
+            [dot_right(grad_joined, pack_ref[:, : 3 * across]) for pack_ref in pack_refs],
             axis=1,
         )
-        cut_rows(partial, part_refs)
-        bundle_into(send_refs, sends_of(cols), [grad_joined], [full_middle], width)
+        if last:
+            normed, scale = more[0][...], more[1][:, :1]
+            grad_normed = partial * vector_row(more[3 : 3 + cols], GAIN_ONE * LAYERS)
+            first = jnp.mean(grad_normed, axis=1, keepdims=True)
+            second = jnp.mean(grad_normed * normed, axis=1, keepdims=True)
+            cut_turned(
+                scale * (grad_normed - first - normed * second), more[2][...], part_refs
+            )
+            lines = [
+                jnp.sum(partial * normed, axis=0, keepdims=True),
+                jnp.sum(partial, axis=0, keepdims=True),
+            ]
+            for ref in more[3 + cols :]:
+                lines += [ref[at : at + 1, :] for at in range(ref.shape[0])]
+            lines.append(jnp.zeros((16 - len(lines), full), F32))
+            lines = low(jnp.concatenate(lines, axis=0))
+            for place, ref in enumerate(part_refs):
+                ref[length:, :] = lines[:, place * width : (place + 1) * width]
+        else:
+            cut_rows(low(partial), part_refs)
+        if not last:
+            bundle_into(send_refs, sends_of(cols), [grad_joined], [full_middle], width)
 
     outs = run(
         kernel,
-        [*blocks, *packs, qkv, probs, mixed],
-        [shaped((rows, full), BF)] * size
-        + bundle_shapes(length, sends_of(cols), 3 * across, 1, width),
-    )
-    return outs[:size], outs[size:]
+        [*blocks, *packs, qkv, probs, mixed, *extra],
+        parts + sends,
+    )
+    return outs[: len(parts)], outs[len(parts) :]
 
 
 def rows_of(refs, pick):
@@ -732,29 +727,42 @@
     return run(kernel, [*ahead, *pres], [shaped((width + 16, units), BF)])[0]
 
 
-def attention_changes(ahead, joined, across, width):
+def attention_changes(ahead, joined, across, width, middles=None):
     cols = len(ahead)
 
     def kernel(*refs):
-        ahead_refs, joined_refs, out_ref = refs[:cols], refs[cols : 2 * cols], refs[2 * cols]
+        ahead_refs, joined_refs, out_refs = refs[:cols], refs[cols : 2 * cols], refs[2 * cols :]
+        out_ref = out_refs[0]
         joined_all = rows_of(joined_refs, lambda _: slice(0, 3 * across))
         out_ref[:width, : 3 * across] = low(
             dot_left(slices_of(ahead_refs, across, width), joined_all)
         )
         total = jnp.sum(wide(joined_all), axis=0, keepdims=True)
         out_ref[width:, : 3 * across] = low(jnp.broadcast_to(total, (16, 3 * across)))
+        if middles is None:
+            output_part(ahead_refs, joined_refs, 3 * across, out_ref, 3 * across)
+            out_ref[width:, 3 * across :] = jnp.zeros((16, out_ref.shape[1] - 3 * across), BF)
+
+    def output_part(ahead_refs, middle_refs, shared, out_ref, column):
         mixed_all = rows_of(ahead_refs, lambda _: slice(0, across))
-        change = low(dot_left(mixed_all, slices_of(joined_refs, 3 * across, width)))
+        change = low(dot_left(mixed_all, slices_of(middle_refs, shared, width)))
         for at in range(0, across, width):
-            column = 3 * across + at // width * width
-            out_ref[:width, column : column + width] = change[at : at + width]
-        out_ref[width:, 3 * across :] = jnp.zeros((16, out_ref.shape[1] - 3 * across), BF)
-
-    return run(
-        kernel,
-        [*ahead, *joined],
-        [shaped((width + 16, 4 * across), BF)],
-    )[0]
+            out_ref[:width, column + at : column + at + width] = change[at : at + width]
+
+    columns = 3 * across if middles else 4 * across
+    return run(kernel, [*ahead, *joined], [shaped((width + 16, columns), BF)])[0]
+
+
+def output_changes(ahead, middles, across, width):
+    cols = len(ahead)
+
+    def kernel(*refs):
+        mixed_all = rows_of(refs[:cols], lambda _: slice(0, across))
+        change = low(dot_left(mixed_all, slices_of(refs[cols : 2 * cols], 0, width)))
+        for at in range(0, across, width):
+            refs[-1][:, at : at + width] = change[at : at + width]
+
+    return run(kernel, [*ahead, *middles], [shaped((width, across), BF)])[0]
 
 
 def finish(own, other, layer, cuts, shapes, kept, line):
@@ -821,42 +829,30 @@
     )
 
 
-def end_place(got, extra=0):
-    size = len(got)
+def turn(blocks):
+    got = turn_blocks(spread(blocks, ROW))
+    return trade(got, COL)
+
+
+def turn_sum(blocks, dtype, extra=0):
+    got = turn_blocks(trade(blocks, COL), extra)
+    return sum_blocks(trade(got, ROW), dtype, extra)
+
+
+def sum_blocks(got, dtype, extra):
     rows, width = got[0].shape[0] - extra, got[0].shape[1]
 
     def kernel(*refs):
-        for at in range(size):
-            refs[size][at * rows : (at + 1) * rows, :] = refs[at][:rows, :]
+        parts = refs[: len(got)]
+        total = tree_sum([wide(ref[:rows, :]) for ref in parts])
+        refs[len(got)][...] = total.astype(dtype)
         if extra:
-            refs[size + 1][...] = tree_sum([ref[rows:, :] for ref in refs[:size]])
-
-    outs = [shaped((rows * size, width), got[0].dtype)]
+            refs[len(got) + 1][...] = tree_sum([wide(ref[rows:, :]) for ref in parts])
+
+    outs = [shaped((rows, width), dtype)]
     if extra:
-        outs.append(shaped((extra, width), got[0].dtype))
+        outs.append(shaped((extra, width), F32))
     return run(kernel, list(got), outs)
-
-
-def turn_in(blocks):
-    got = turn_blocks(trade(blocks, ROW))
-    return trade(got, COL)
-
-
-def turn_out(blocks, extra=0):
-    got = turn_blocks(trade(blocks, COL), extra)
-    return end_place(trade(got, ROW), extra)
-
-
-def turn_sum(blocks):
-    got = turn_blocks(trade(blocks, COL))
-    return sum_blocks(trade(got, ROW))
-
-
-def sum_blocks(got):
-    def kernel(*refs):
-        refs[-1][...] = low(tree_sum([wide(ref[...]) for ref in refs[:-1]]))
-
-    return run(kernel, list(got), [shaped(got[0].shape, BF)])[0]
 
 
 def shards(
@@ -881,35 +877,36 @@
     width = block_input.shape[1]
     size, cols = lax.axis_size(ROW), lax.axis_size(COL)
     steps = sends_of(cols)
-    extra = -(-6 * LAYERS // 8) * 8
 
     def exchange(sends):
         return [sends[0]] + relay(dict(zip(steps, sends[1:])), COL)
 
-    blocks, first_pack = start_blocks(block_input, cotangent, joined_weight, output_weight, size)
     vectors, (query_bias, value_bias, upward_bias) = start_vectors(
         [first_gain, first_shift, output_bias, second_gain, second_shift, downward_bias],
         [query_bias, value_bias, upward_bias],
     )
-    got = turn_in(blocks)
     vecs = relay_all(vectors, COL)
     weights = []
     for layer in range(LAYERS):
         weights.append([])
         for first in (True, False):
-            if layer or not first:
-                pair = (joined_weight, output_weight) if first else (upward_weight, downward_weight)
-                pack = pack_weights(*pair, layer, width, first)
-            else:
-                pack = first_pack
+            pair = (joined_weight, output_weight) if first else (upward_weight, downward_weight)
+            pack = pack_weights(*pair, layer, width, first)
             weights[layer].append(relay_all(pack, COL))
-    resid, grad_resid, norm_input, stats = first_norm(got, vecs)
+    got = turn(block_input)
+    grad_blocks = row_blocks(turn(cotangent), size)
+    resid, last_kept, input_blocks = first_norm(got, vecs, size)
+    stats = None
     saved = []
     for layer in range(LAYERS):
         attention_packs, feed_packs = weights[layer]
         first_kept = (resid, stats)
         (qkv, probs), parts, sends = attention_forward(
-            spread(norm_input, ROW), attention_packs, query_bias, value_bias, layer
+            spread(norm_input, ROW) if layer else input_blocks,
+            attention_packs,
+            query_bias,
+            value_bias,
+            layer,
         )
         attention_ahead = exchange(sends)
         middle, norm_input, stats = next_norm(
@@ -930,35 +927,43 @@
                 middle, trade(parts, ROW), vecs, layer, BIAS_DOWN, GAIN_ONE, SHIFT_ONE
             )
         else:
-            block_output = turn_sum(parts)
-
-    grad_low = grad_resid
+            (block_output,) = turn_sum(parts, BF)
+
+    grad_resid = grad_blocks[0]
     sums = []
-    down_outs = up_outs = attention_outs = None
+    down_outs = up_outs = joined_out = output_out = None
     up_lines, joined_lines = [None] * LAYERS, [None] * LAYERS
     for layer in reversed(range(LAYERS)):
         attention_packs, feed_packs = weights[layer]
         first_kept, second_kept, qkv, probs, slope, attention_ahead, feed_ahead = saved[layer]
-        parts, grad_pre, sends = feed_backward(spread(grad_low, ROW), feed_packs, slope)
+        parts, grad_pre, sends = feed_backward(grad_blocks, feed_packs, slope)
         grads = exchange(sends)
         pres = relay_all(grad_pre, COL)
         grad_middle, middle_low, second_sums = norm_backward(
             grad_resid, trade(parts, ROW), *second_kept, vecs, layer, GAIN_TWO, True
         )
+        blocks = spread(middle_low, ROW)
+        middles = None
+        if not layer:
+            middles = exchange(bundle_blocks(blocks, cols))
         parts, sends = attention_backward(
-            spread(middle_low, ROW), attention_packs, qkv, probs, attention_ahead[0], across
-        )
-        joined = exchange(sends)
-        parts = trade(parts, ROW)
+            blocks,
+            attention_packs,
+            qkv,
+            probs,
+            attention_ahead[0],
+            across,
+            None if layer else (last_kept, grad_middle, vecs, [second_sums] + sums),
+        )
+        joined = exchange(sends) if layer else relay_all(sends[0], COL)
         if layer:
             grad_resid, grad_low, first_sums = norm_backward(
-                grad_middle, parts, *first_kept, vecs, layer, GAIN_ONE, False
+                grad_middle, trade(parts, ROW), *first_kept, vecs, layer, GAIN_ONE, False
             )
+            grad_blocks = spread(grad_low, ROW)
             sums = [first_sums, second_sums] + sums
         else:
-            blocks = last_backward(
-                grad_middle, parts, *first_kept, vecs, [second_sums] + sums, extra
-            )
+            input_gradient, totals = turn_sum(parts, F32, 16)
         change = down_changes(feed_ahead, grads, units, width)
         down_outs = finish(
             change,
@@ -979,28 +984,48 @@
             up_outs,
             True,
         )
-        change = attention_changes(attention_ahead, joined, across, width)
-        chunk = range(3 * across, 3 * across + across // width * width, width)
-        *attention_outs, joined_lines[layer] = finish(
-            change,
-            axis_swap(change, DP, 1),
-            layer,
-            [[(0, 3 * across)], [(at, at + width) for at in chunk]],
-            [joined_weight.shape, output_weight.shape],
-            attention_outs,
-            True,
-        )
-    input_gradient, totals = turn_out(blocks, extra)
+        change = attention_changes(attention_ahead, joined, across, width, middles)
+        output_cut = [(at, at + width) for at in range(0, across, width)]
+        if layer:
+            joined_out, output_out, joined_lines[layer] = finish(
+                change,
+                axis_swap(change, DP, 1),
+                layer,
+                [[(0, 3 * across)], [(3 * across + one, 3 * across + two) for one, two in output_cut]],
+                [joined_weight.shape, output_weight.shape],
+                None,
+                True,
+            )
+        else:
+            joined_out, joined_lines[layer] = finish(
+                change,
+                axis_swap(change, DP, 1),
+                layer,
+                [[(0, 3 * across)]],
+                [joined_weight.shape],
+                [joined_out],
+                True,
+            )
+            change = output_changes(attention_ahead, middles, across, width)
+            (output_out,) = finish(
+                change,
+                axis_swap(change, DP, 1),
+                layer,
+                [output_cut],
+                [output_weight.shape],
+                [output_out],
+                False,
+            )
     vector_sums = finish_vectors(totals, axis_swap(totals, DP, 1), up_lines, joined_lines, across)
     return (
         block_output,
         input_gradient,
         vector_sums[0],
         vector_sums[1],
-        attention_outs[0],
+        joined_out,
         vector_sums[7],
         vector_sums[8],
-        attention_outs[1],
+        output_out,
         vector_sums[4],
         vector_sums[2],
         vector_sums[3],

time: 354 us -> 346 us (0.977)
  starting transfers between devices: 119 us -> 97.9 us
  waiting for transfers between devices: 202 us -> 214 us
    ppermute x115 -> x116, starting transfers between devices: 119 us -> 97.9 us  [axis_swap(): lax.ppermute(local, axis, [(place, place ^ step) for place in range(size)])]
    ppermute x115 -> x116, waiting for transfers between devices: 202 us -> 214 us  [axis_swap(): lax.ppermute(local, axis, [(place, place ^ step) for place in range(size)])]
    pallas_call x30 -> x32, Pallas kernels: 21.4 us -> 20.7 us  [run(): pl.pallas_call(kernel, in_specs=[spec or VMEM] * len(arrays), out_specs=[...]
  transfers between devices with their start and end apart: 115 -> 116, of which waited for: 48 -> 54; matrix products, arithmetic and copies ran while one was open for 0% -> 0% of each run, Pallas kernels for 8% -> 9%
where the time goes in v2:
time: 346 us
  waiting for transfers between devices  214 us (62%)
  starting transfers between devices  97.9 us (28%)
  Pallas kernels  32.4 us (9%)
    ppermute x116, waiting for transfers between devices, axis_swap(): lax.ppermute(local, axis, [(place, place ^ step) for place in range(size)])  214 us
    ppermute x116, starting transfers between devices, axis_swap(): lax.ppermute(local, axis, [(place, place ^ step) for place in range(size)])  97.9 us
    pallas_call x32, Pallas kernels, run(): pl.pallas_call(kernel, in_specs=[spec or VMEM] * len(arrays), out_specs=[...  20.7 us
    pallas_call x7, Pallas kernels, finish(): pl.pallas_call(kernel, grid=(1,), in_specs=[whole(own), whole(other)] + [...  7.05 us
  transfers between devices with their start and end apart: 116, of which 54 were waited for; matrix products, arithmetic and copies ran while one was open for 0% of the time, Pallas kernels for 9%

profile of v2, /device:TPU:0, one launch (start us, length us, event | category | flops | bytes accessed | tf_op | source)
XLA Modules:
  0.0 345.6 jit_solution(10156365197591490168)
XLA Ops:
  1.9 3.0 collective-permute-start.19
  8.2 2.6 collective-permute-start.1
  14.4 25.3 %collective-permute-done.7.refs_6_.refs_12_.refs_16_ = f32[12,256]{1,0:T(8,128)S(1)} collective-permute-done((f32[12,256]{1,0:T(8,128)S(1)}, f32[12,256]{1,0:T(8,128)S(1)}, u32[]{:S(2)}, u32[]{:S(2)}) %collective-permute-start.7) | collective-permute-done | bytes 12320 | tf_op jit(solution)/shard_map/ppermute | solution.py:31
  39.7 3.9 %collective-permute-start.2 = (bf16[128,256]{1,0:T(8,128)(2,1)S(1)}, bf16[128,256]{1,0:T(8,128)(2,1)S(1)}, u32[]{:S(2)}, u32[]{:S(2)}) collective-permute-start(bf16[128,256]{1,0:T(8,128)(2,1)S(1)} %copy-done), channel_id=1, source_target_pairs={{0,12},{4,8},{8,4},{12,0},{1,13},{5,9},{9,5},{13,1},{2,14},{6,10},... | collective-permute-start | bytes 196616 | tf_op jit(solution)/shard_map/ppermute | solution.py:31
  47.8 2.8 collective-permute-done.45.refs_1_
  51.2 19.6 %collective-permute-done.4.refs_2_ = bf16[128,256]{1,0:T(8,128)(2,1)S(1)} collective-permute-done((bf16[128,256]{1,0:T(8,128)(2,1)S(1)}, bf16[128,256]{1,0:T(8,128)(2,1)S(1)}, u32[]{:S(2)}, u32[]{:S(2)}) %collective-permute-start.4) | collective-permute-done | bytes 65568 | tf_op jit(solution)/shard_map/ppermute | solution.py:31
  78.7 3.3 collective-permute-done.46.refs_2_
  83.8 3.0 collective-permute-done.12.refs_1_
  88.9 4.0 %collective-permute-done.14.refs_3_ = bf16[32,1024]{1,0:T(8,128)(2,1)S(1)} collective-permute-done((bf16[32,1024]{1,0:T(8,128)(2,1)S(1)}, bf16[32,1024]{1,0:T(8,128)(2,1)S(1)}, u32[]{:S(2)}, u32[]{:S(2)}) %collective-permute-start.14) | collective-permute-done | bytes 65568 | tf_op jit(solution)/shard_map/ppermute | solution.py:31
  93.1 2.1 collective-permute-start.16
  95.2 3.5 %collective-permute-done.15.refs_1_ = bf16[32,1024]{1,0:T(8,128)(2,1)S(1)} collective-permute-done((bf16[32,1024]{1,0:T(8,128)(2,1)S(1)}, bf16[32,1024]{1,0:T(8,128)(2,1)S(1)}, u32[]{:S(2)}, u32[]{:S(2)}) %collective-permute-start.15) | collective-permute-done | bytes 65568 | tf_op jit(solution)/shard_map/ppermute | solution.py:31
  100.3 4.5 %collective-permute-done.17.refs_3_ = bf16[32,1024]{1,0:T(8,128)(2,1)S(1)} collective-permute-done((bf16[32,1024]{1,0:T(8,128)(2,1)S(1)}, bf16[32,1024]{1,0:T(8,128)(2,1)S(1)}, u32[]{:S(2)}, u32[]{:S(2)}) %collective-permute-start.17) | collective-permute-done | bytes 65568 | tf_op jit(solution)/shard_map/ppermute | solution.py:31
  107.5 3.6 %collective-permute-done.47.refs_3_ = bf16[128,256]{1,0:T(8,128)(2,1)S(1)} collective-permute-done((bf16[128,256]{1,0:T(8,128)(2,1)S(1)}, bf16[128,256]{1,0:T(8,128)(2,1)S(1)}, u32[]{:S(2)}, u32[]{:S(2)}) %collective-permute-start.47) | collective-permute-done | bytes 65568 | tf_op jit(solution)/shard_map/ppermute | solution.py:31
  111.1 4.3 %collective-permute-done.21.refs_1_ = bf16[32,1024]{1,0:T(8,128)(2,1)S(1)} collective-permute-done((bf16[32,1024]{1,0:T(8,128)(2,1)S(1)}, bf16[32,1024]{1,0:T(8,128)(2,1)S(1)}, u32[]{:S(2)}, u32[]{:S(2)}) %collective-permute-start.21) | collective-permute-done | bytes 65568 | tf_op jit(solution)/shard_map/ppermute | solution.py:31
  115.5 5.6 %collective-permute-done.22.refs_2_ = bf16[32,1024]{1,0:T(8,128)(2,1)S(1)} collective-permute-done((bf16[32,1024]{1,0:T(8,128)(2,1)S(1)}, bf16[32,1024]{1,0:T(8,128)(2,1)S(1)}, u32[]{:S(2)}, u32[]{:S(2)}) %collective-permute-start.22) | collective-permute-done | bytes 65568 | tf_op jit(solution)/shard_map/ppermute | solution.py:31
  122.7 4.4 %collective-permute-done.23.refs_3_ = bf16[32,1024]{1,0:T(8,128)(2,1)S(1)} collective-permute-done((bf16[32,1024]{1,0:T(8,128)(2,1)S(1)}, bf16[32,1024]{1,0:T(8,128)(2,1)S(1)}, u32[]{:S(2)}, u32[]{:S(2)}) %collective-permute-start.23) | collective-permute-done | bytes 65568 | tf_op jit(solution)/shard_map/ppermute | solution.py:31
  129.9 2.1 collective-permute-start.25
  134.3 3.5 %collective-permute-done.25.refs_2_ = bf16[32,1024]{1,0:T(8,128)(2,1)S(1)} collective-permute-done((bf16[32,1024]{1,0:T(8,128)(2,1)S(1)}, bf16[32,1024]{1,0:T(8,128)(2,1)S(1)}, u32[]{:S(2)}, u32[]{:S(2)}) %collective-permute-start.25) | collective-permute-done | bytes 65568 | tf_op jit(solution)/shard_map/ppermute | solution.py:31
  144.8 3.5 %collective-permute-done.30.refs_1_ = bf16[32,1024]{1,0:T(8,128)(2,1)S(1)} collective-permute-done((bf16[32,1024]{1,0:T(8,128)(2,1)S(1)}, bf16[32,1024]{1,0:T(8,128)(2,1)S(1)}, u32[]{:S(2)}, u32[]{:S(2)}) %collective-permute-start.30) | collective-permute-done | bytes 65568 | tf_op jit(solution)/shard_map/ppermute | solution.py:31
  151.2 4.5 %collective-permute-done.32.refs_3_ = bf16[32,1024]{1,0:T(8,128)(2,1)S(1)} collective-permute-done((bf16[32,1024]{1,0:T(8,128)(2,1)S(1)}, bf16[32,1024]{1,0:T(8,128)(2,1)S(1)}, u32[]{:S(2)}, u32[]{:S(2)}) %collective-permute-start.32) | collective-permute-done | bytes 65568 | tf_op jit(solution)/shard_map/ppermute | solution.py:31
  156.0 2.1 collective-permute-start.34
  158.8 2.8 collective-permute-done.33.refs_1_
  164.5 4.5 %collective-permute-done.35.refs_3_ = bf16[32,1024]{1,0:T(8,128)(2,1)S(1)} collective-permute-done((bf16[32,1024]{1,0:T(8,128)(2,1)S(1)}, bf16[32,1024]{1,0:T(8,128)(2,1)S(1)}, u32[]{:S(2)}, u32[]{:S(2)}) %collective-permute-start.35) | collective-permute-done | bytes 65568 | tf_op jit(solution)/shard_map/ppermute | solution.py:31
  174.7 2.2 collective-permute-start.53
  183.1 2.5 collective-permute-done.41.refs_3_
  189.2 3.7 %collective-permute-done.55.refs_2_ = bf16[32,1024]{1,0:T(8,128)(2,1)S(1)} collective-permute-done((bf16[32,1024]{1,0:T(8,128)(2,1)S(1)}, bf16[32,1024]{1,0:T(8,128)(2,1)S(1)}, u32[]{:S(2)}, u32[]{:S(2)}) %collective-permute-start.55) | collective-permute-done | bytes 65568 | tf_op jit(solution)/shard_map/ppermute | solution.py:31
  192.9 2.2 collective-permute-start.44
  201.5 2.2 collective-permute-start.59
  203.6 3.2 collective-permute-done.58.refs_2_
  212.4 2.2 collective-permute-start.62
  215.9 2.6 collective-permute-done.62.refs_3_
  221.4 2.2 collective-permute-start.64
  223.6 2.1 collective-permute-start.65
  227.1 2.6 collective-permute-done.65.refs_3_
  230.0 2.7 collective-permute-start.67
  232.6 3.0 collective-permute-done.66.refs_1_
  235.6 2.1 collective-permute-start.68
  237.7 3.9 %collective-permute-done.68.refs_3_ = bf16[32,1024]{1,0:T(8,128)(2,1)S(1)} collective-permute-done((bf16[32,1024]{1,0:T(8,128)(2,1)S(1)}, bf16[32,1024]{1,0:T(8,128)(2,1)S(1)}, u32[]{:S(2)}, u32[]{:S(2)}) %collective-permute-start.68) | collective-permute-done | bytes 65568 | tf_op jit(solution)/shard_map/ppermute | solution.py:31
  249.2 3.0 collective-permute-done.70.refs_2_
  252.2 5.8 %collective-permute-done.71.refs_3_ = bf16[144,256]{1,0:T(8,128)(2,1)S(1)} collective-permute-done((bf16[144,256]{1,0:T(8,128)(2,1)S(1)}, bf16[144,256]{1,0:T(8,128)(2,1)S(1)}, u32[]{:S(2)}, u32[]{:S(2)}) %collective-permute-start.71) | collective-permute-done | bytes 73760 | tf_op jit(solution)/shard_map/ppermute | solution.py:31
  260.1 3.9 %collective-permute-done.105.refs_6_ = bf16[128,512]{1,0:T(8,128)(2,1)S(1)} collective-permute-done((bf16[128,512]{1,0:T(8,128)(2,1)S(1)}, bf16[128,512]{1,0:T(8,128)(2,1)S(1)}, u32[]{:S(2)}, u32[]{:S(2)}) %collective-permute-start.105) | collective-permute-done | bytes 131104 | tf_op jit(solution)/shard_map/ppermute | solution.py:31
  267.4 4.1 %collective-permute-done.73.refs_2_ = bf16[144,256]{1,0:T(8,128)(2,1)S(1)} collective-permute-done((bf16[144,256]{1,0:T(8,128)(2,1)S(1)}, bf16[144,256]{1,0:T(8,128)(2,1)S(1)}, u32[]{:S(2)}, u32[]{:S(2)}) %collective-permute-start.73) | collective-permute-done | bytes 73760 | tf_op jit(solution)/shard_map/ppermute | solution.py:31
  280.7 5.6 %collective-permute-done.111.other_ref = bf16[256,1024]{1,0:T(8,128)(2,1)S(1)} collective-permute-done((bf16[256,1024]{1,0:T(8,128)(2,1)S(1)}, bf16[256,1024]{1,0:T(8,128)(2,1)S(1)}, u32[]{:S(2)}, u32[]{:S(2)}) %collective-permute-start.111) | collective-permute-done | bytes 524320 | tf_op jit(solution)/shard_map/ppermute | solution.py:31
  288.1 9.4 %collective-permute-done.115.other_ref = bf16[256,1024]{1,0:T(8,128)(2,1)S(1)} collective-permute-done((bf16[256,1024]{1,0:T(8,128)(2,1)S(1)}, bf16[256,1024]{1,0:T(8,128)(2,1)S(1)}, u32[]{:S(2)}, u32[]{:S(2)}) %collective-permute-start.115) | collective-permute-done | bytes 524320 | tf_op jit(solution)/shard_map/ppermute | solution.py:31
  299.7 9.7 %collective-permute-done.89.other_ref = bf16[272,1024]{1,0:T(8,128)(2,1)S(1)} collective-permute-done((bf16[272,1024]{1,0:T(8,128)(2,1)S(1)}, bf16[272,1024]{1,0:T(8,128)(2,1)S(1)}, u32[]{:S(2)}, u32[]{:S(2)}) %collective-permute-start.89) | collective-permute-done | bytes 557088 | tf_op jit(solution)/shard_map/ppermute | solution.py:31
  314.9 6.5 %collective-permute-done.103.other_ref = bf16[272,1024]{1,0:T(8,128)(2,1)S(1)} collective-permute-done((bf16[272,1024]{1,0:T(8,128)(2,1)S(1)}, bf16[272,1024]{1,0:T(8,128)(2,1)S(1)}, u32[]{:S(2)}, u32[]{:S(2)}) %collective-permute-start.103) | collective-permute-done | bytes 557088 | tf_op jit(solution)/shard_map/ppermute | solution.py:31
  322.4 10.9 %collective-permute-done.82.other_ref = bf16[272,1024]{1,0:T(8,128)(2,1)S(1)} collective-permute-done((bf16[272,1024]{1,0:T(8,128)(2,1)S(1)}, bf16[272,1024]{1,0:T(8,128)(2,1)S(1)}, u32[]{:S(2)}, u32[]{:S(2)}) %collective-permute-start.82) | collective-permute-done | bytes 557088 | tf_op jit(solution)/shard_map/ppermute | solution.py:31
  334.4 7.9 %collective-permute-done.96.other_ref = bf16[272,768]{1,0:T(8,128)(2,1)S(1)} collective-permute-done((bf16[272,768]{1,0:T(8,128)(2,1)S(1)}, bf16[272,768]{1,0:T(8,128)(2,1)S(1)}, u32[]{:S(2)}, u32[]{:S(2)}) %collective-permute-start.96) | collective-permute-done | bytes 417824 | tf_op jit(solution)/shard_map/ppermute | solution.py:31
  (231 shorter events, 119.7 us)
Async XLA Ops:
  1.9 69.3 %collective-permute-start.19 = (bf16[256,2048]{1,0:T(8,128)(2,1)S(1)}, bf16[256,2048]{1,0:T(8,128)(2,1)S(1)}, u32[]{:S(2)}, u32[]{:S(2)}) collective-permute-start(bf16[256,2048]{1,0:T(8,128)(2,1)S(1)} %shard_map.268.refs_4_), channel_id=1, source_target_pairs={{0,2},{1,3},{2,0},{3,1},{4,6},{5,7},{6,4},{7,5},{8,10},{9,11},{10,... | collective-permute-start | bytes 3145736 | tf_op jit(solution)/shard_map/ppermute | solution.py:31
  6.0 65.3 %collective-permute-start.10 = (bf16[256,1024]{1,0:T(8,128)(2,1)S(1)}, bf16[256,1024]{1,0:T(8,128)(2,1)S(1)}, u32[]{:S(2)}, u32[]{:S(2)}) collective-permute-start(bf16[256,1024]{1,0:T(8,128)(2,1)S(1)} %shard_map.265.refs_4_), channel_id=1, source_target_pairs={{0,2},{1,3},{2,0},{3,1},{4,6},{5,7},{6,4},{7,5},{8,10},{9,11},{10,... | collective-permute-start | bytes 1572872 | tf_op jit(solution)/shard_map/ppermute | solution.py:31
  6.1 38.7 %collective-permute-start = (bf16[128,256]{1,0:T(8,128)(2,1)S(1)}, bf16[128,256]{1,0:T(8,128)(2,1)S(1)}, u32[]{:S(2)}, u32[]{:S(2)}) collective-permute-start(bf16[128,256]{1,0:T(8,128)(2,1)S(1)} %copy-done), channel_id=1, source_target_pairs={{0,4},{4,0},{8,12},{12,8},{1,5},{5,1},{9,13},{13,9},{2,6},{6,2},{1... | collective-permute-start | bytes 196616 | tf_op jit(solution)/shard_map/ppermute | solution.py:31
  8.2 38.2 %collective-permute-start.1 = (bf16[128,256]{1,0:T(8,128)(2,1)S(1)}, bf16[128,256]{1,0:T(8,128)(2,1)S(1)}, u32[]{:S(2)}, u32[]{:S(2)}) collective-permute-start(bf16[128,256]{1,0:T(8,128)(2,1)S(1)} %copy-done), channel_id=1, source_target_pairs={{0,8},{4,12},{8,0},{12,4},{1,9},{5,13},{9,1},{13,5},{2,10},{6,14},... | collective-permute-start | bytes 196616 | tf_op jit(solution)/shard_map/ppermute | solution.py:31
  12.9 26.8 %collective-permute-start.7 = (f32[12,256]{1,0:T(8,128)S(1)}, f32[12,256]{1,0:T(8,128)S(1)}, u32[]{:S(2)}, u32[]{:S(2)}) collective-permute-start(f32[12,256]{1,0:T(8,128)S(1)} %get-tuple-element.153.refs_4_.refs_10_.refs_14_), channel_id=1, source_target_pairs={{0,2},{1,3},{2,0},{3,1},{4,6},{5,7},{6,4},{7,5},{8,10},{9,11},{10,... | collective-permute-start | bytes 36872 | tf_op jit(solution)/shard_map/ppermute | solution.py:31
  44.8 37.2 %collective-permute-start.37 = (bf16[256,2048]{1,0:T(8,128)(2,1)S(1)}, bf16[256,2048]{1,0:T(8,128)(2,1)S(1)}, u32[]{:S(2)}, u32[]{:S(2)}) collective-permute-start(bf16[256,2048]{1,0:T(8,128)(2,1)S(1)} %shard_map.274.refs_4_), channel_id=1, source_target_pairs={{0,2},{1,3},{2,0},{3,1},{4,6},{5,7},{6,4},{7,5},{8,10},{9,11},{10,... | collective-permute-start | bytes 3145736 | tf_op jit(solution)/shard_map/ppermute | solution.py:31
  50.6 20.1 %collective-permute-start.4 = (bf16[128,256]{1,0:T(8,128)(2,1)S(1)}, bf16[128,256]{1,0:T(8,128)(2,1)S(1)}, u32[]{:S(2)}, u32[]{:S(2)}) collective-permute-start(bf16[128,256]{1,0:T(8,128)(2,1)S(1)} %get-tuple-element.151), channel_id=1, source_target_pairs={{0,2},{1,3},{2,0},{3,1},{4,6},{5,7},{6,4},{7,5},{8,10},{9,11},{10,... | collective-permute-start | bytes 196616 | tf_op jit(solution)/shard_map/ppermute | solution.py:31
  51.2 19.6 %collective-permute-start.5 = (bf16[128,256]{1,0:T(8,128)(2,1)S(1)}, bf16[128,256]{1,0:T(8,128)(2,1)S(1)}, u32[]{:S(2)}, u32[]{:S(2)}) collective-permute-start(bf16[128,256]{1,0:T(8,128)(2,1)S(1)} %get-tuple-element.152), channel_id=1, source_target_pairs={{0,3},{1,2},{2,1},{3,0},{4,7},{5,6},{6,5},{7,4},{8,11},{9,10},{10,... | collective-permute-start | bytes 196616 | tf_op jit(solution)/shard_map/ppermute | solution.py:31
  70.7 22.4 %collective-permute-start.18 = (bf16[256,2048]{1,0:T(8,128)(2,1)S(1)}, bf16[256,2048]{1,0:T(8,128)(2,1)S(1)}, u32[]{:S(2)}, u32[]{:S(2)}) collective-permute-start(bf16[256,2048]{1,0:T(8,128)(2,1)S(1)} %shard_map.268.refs_4_), channel_id=1, source_target_pairs={{0,1},{1,0},{2,3},{3,2},{4,5},{5,4},{6,7},{7,6},{8,9},{9,8},{10,11... | collective-permute-start | bytes 3145736 | tf_op jit(solution)/shard_map/ppermute | solution.py:31
  71.3 33.5 %collective-permute-start.20 = (bf16[256,2048]{1,0:T(8,128)(2,1)S(1)}, bf16[256,2048]{1,0:T(8,128)(2,1)S(1)}, u32[]{:S(2)}, u32[]{:S(2)}) collective-permute-start(bf16[256,2048]{1,0:T(8,128)(2,1)S(1)} %collective-permute-done.19.refs_6_), channel_id=1, source_target_pairs={{0,1},{1,0},{2,3},{3,2},{4,5},{5,4},{6,7},{7,6},{8,9},{9,8},{10,11... | collective-permute-start | bytes 3145736 | tf_op jit(solution)/shard_map/ppermute | solution.py:31
  72.8 20.2 %collective-permute-start.28 = (bf16[256,1024]{1,0:T(8,128)(2,1)S(1)}, bf16[256,1024]{1,0:T(8,128)(2,1)S(1)}, u32[]{:S(2)}, u32[]{:S(2)}) collective-permute-start(bf16[256,1024]{1,0:T(8,128)(2,1)S(1)} %shard_map.271.refs_4_), channel_id=1, source_target_pairs={{0,2},{1,3},{2,0},{3,1},{4,6},{5,7},{6,4},{7,5},{8,10},{9,11},{10,... | collective-permute-start | bytes 1572872 | tf_op jit(solution)/shard_map/ppermute | solution.py:31
  88.9 67.0 %collective-permute-start.36 = (bf16[256,2048]{1,0:T(8,128)(2,1)S(1)}, bf16[256,2048]{1,0:T(8,128)(2,1)S(1)}, u32[]{:S(2)}, u32[]{:S(2)}) collective-permute-start(bf16[256,2048]{1,0:T(8,128)(2,1)S(1)} %shard_map.274.refs_4_), channel_id=1, source_target_pairs={{0,1},{1,0},{2,3},{3,2},{4,5},{5,4},{6,7},{7,6},{8,9},{9,8},{10,11... | collective-permute-start | bytes 3145736 | tf_op jit(solution)/shard_map/ppermute | solution.py:31
  92.8 65.3 %collective-permute-start.38 = (bf16[256,2048]{1,0:T(8,128)(2,1)S(1)}, bf16[256,2048]{1,0:T(8,128)(2,1)S(1)}, u32[]{:S(2)}, u32[]{:S(2)}) collective-permute-start(bf16[256,2048]{1,0:T(8,128)(2,1)S(1)} %collective-permute-done.37.refs_6_), channel_id=1, source_target_pairs={{0,1},{1,0},{2,3},{3,2},{4,5},{5,4},{6,7},{7,6},{8,9},{9,8},{10,11... | collective-permute-start | bytes 3145736 | tf_op jit(solution)/shard_map/ppermute | solution.py:31
  100.3 28.1 %collective-permute-start.27 = (bf16[256,1024]{1,0:T(8,128)(2,1)S(1)}, bf16[256,1024]{1,0:T(8,128)(2,1)S(1)}, u32[]{:S(2)}, u32[]{:S(2)}) collective-permute-start(bf16[256,1024]{1,0:T(8,128)(2,1)S(1)} %shard_map.271.refs_4_), channel_id=1, source_target_pairs={{0,1},{1,0},{2,3},{3,2},{4,5},{5,4},{6,7},{7,6},{8,9},{9,8},{10,11... | collective-permute-start | bytes 1572872 | tf_op jit(solution)/shard_map/ppermute | solution.py:31
  104.8 25.1 %collective-permute-start.29 = (bf16[256,1024]{1,0:T(8,128)(2,1)S(1)}, bf16[256,1024]{1,0:T(8,128)(2,1)S(1)}, u32[]{:S(2)}, u32[]{:S(2)}) collective-permute-start(bf16[256,1024]{1,0:T(8,128)(2,1)S(1)} %collective-permute-done.28.refs_6_), channel_id=1, source_target_pairs={{0,1},{1,0},{2,3},{3,2},{4,5},{5,4},{6,7},{7,6},{8,9},{9,8},{10,11... | collective-permute-start | bytes 1572872 | tf_op jit(solution)/shard_map/ppermute | solution.py:31
  128.4 16.0 %collective-permute-start.91 = (bf16[128,768]{1,0:T(8,128)(2,1)S(1)}, bf16[128,768]{1,0:T(8,128)(2,1)S(1)}, u32[]{:S(2)}, u32[]{:S(2)}) collective-permute-start(bf16[128,768]{1,0:T(8,128)(2,1)S(1)} %get-tuple-element.252), channel_id=1, source_target_pairs={{0,2},{1,3},{2,0},{3,1},{4,6},{5,7},{6,4},{7,5},{8,10},{9,11},{10,... | collective-permute-start | bytes 589832 | tf_op jit(solution)/shard_map/ppermute | solution.py:31
  129.9 7.9 %collective-permute-start.25 = (bf16[32,1024]{1,0:T(8,128)(2,1)S(1)}, bf16[32,1024]{1,0:T(8,128)(2,1)S(1)}, u32[]{:S(2)}, u32[]{:S(2)}) collective-permute-start(bf16[32,1024]{1,0:T(8,128)(2,1)S(1)} %get-tuple-element.173.refs_0_), channel_id=1, source_target_pairs={{0,8},{4,12},{8,0},{12,4},{1,9},{5,13},{9,1},{13,5},{2,10},{6,14},... | collective-permute-start | bytes 196616 | tf_op jit(solution)/shard_map/ppermute | solution.py:31
  144.4 28.1 %collective-permute-start.76 = (bf16[128,1280]{1,0:T(8,128)(2,1)S(1)}, bf16[128,1280]{1,0:T(8,128)(2,1)S(1)}, u32[]{:S(2)}, u32[]{:S(2)}) collective-permute-start(bf16[128,1280]{1,0:T(8,128)(2,1)S(1)} %get-tuple-element.241), channel_id=1, source_target_pairs={{0,1},{1,0},{2,3},{3,2},{4,5},{5,4},{6,7},{7,6},{8,9},{9,8},{10,11... | collective-permute-start | bytes 983048 | tf_op jit(solution)/shard_map/ppermute | solution.py:31
  155.7 15.1 %collective-permute-start.92 = (bf16[128,768]{1,0:T(8,128)(2,1)S(1)}, bf16[128,768]{1,0:T(8,128)(2,1)S(1)}, u32[]{:S(2)}, u32[]{:S(2)}) collective-permute-start(bf16[128,768]{1,0:T(8,128)(2,1)S(1)} %collective-permute-done.91.refs_2_), channel_id=1, source_target_pairs={{0,1},{1,0},{2,3},{3,2},{4,5},{5,4},{6,7},{7,6},{8,9},{9,8},{10,11... | collective-permute-start | bytes 589832 | tf_op jit(solution)/shard_map/ppermute | solution.py:31
  158.1 39.0 %collective-permute-start.77 = (bf16[128,1536]{1,0:T(8,128)(2,1)S(1)}, bf16[128,1536]{1,0:T(8,128)(2,1)S(1)}, u32[]{:S(2)}, u32[]{:S(2)}) collective-permute-start(bf16[128,1536]{1,0:T(8,128)(2,1)S(1)} %get-tuple-element.242), channel_id=1, source_target_pairs={{0,2},{1,3},{2,0},{3,1},{4,6},{5,7},{6,4},{7,5},{8,10},{9,11},{10,... | collective-permute-start | bytes 1179656 | tf_op jit(solution)/shard_map/ppermute | solution.py:31
  161.6 10.8 %collective-permute-start.97 = (bf16[128,512]{1,0:T(8,128)(2,1)S(1)}, bf16[128,512]{1,0:T(8,128)(2,1)S(1)}, u32[]{:S(2)}, u32[]{:S(2)}) collective-permute-start(bf16[128,512]{1,0:T(8,128)(2,1)S(1)} %get-tuple-element.254), channel_id=1, source_target_pairs={{0,1},{1,0},{2,3},{3,2},{4,5},{5,4},{6,7},{7,6},{8,9},{9,8},{10,11... | collective-permute-start | bytes 393224 | tf_op jit(solution)/shard_map/ppermute | solution.py:31
  169.0 16.6 %collective-permute-start.98 = (bf16[128,768]{1,0:T(8,128)(2,1)S(1)}, bf16[128,768]{1,0:T(8,128)(2,1)S(1)}, u32[]{:S(2)}, u32[]{:S(2)}) collective-permute-start(bf16[128,768]{1,0:T(8,128)(2,1)S(1)} %get-tuple-element.255), channel_id=1, source_target_pairs={{0,2},{1,3},{2,0},{3,1},{4,6},{5,7},{6,4},{7,5},{8,10},{9,11},{10,... | collective-permute-start | bytes 589832 | tf_op jit(solution)/shard_map/ppermute | solution.py:31
  172.6 8.7 %collective-permute-start.52 = (bf16[32,1024]{1,0:T(8,128)(2,1)S(1)}, bf16[32,1024]{1,0:T(8,128)(2,1)S(1)}, u32[]{:S(2)}, u32[]{:S(2)}) collective-permute-start(bf16[32,1024]{1,0:T(8,128)(2,1)S(1)} %get-tuple-element.200), channel_id=1, source_target_pairs={{0,8},{4,12},{8,0},{12,4},{1,9},{5,13},{9,1},{13,5},{2,10},{6,14},... | collective-permute-start | bytes 196616 | tf_op jit(solution)/shard_map/ppermute | solution.py:31
  185.5 23.5 %collective-permute-start.86 = (bf16[128,1024]{1,0:T(8,128)(2,1)S(1)}, bf16[128,1024]{1,0:T(8,128)(2,1)S(1)}, u32[]{:S(2)}, u32[]{:S(2)}) collective-permute-start(bf16[128,1024]{1,0:T(8,128)(2,1)S(1)} %get-tuple-element.247.refs_4_), channel_id=1, source_target_pairs={{0,1},{1,0},{2,3},{3,2},{4,5},{5,4},{6,7},{7,6},{8,9},{9,8},{10,11... | collective-permute-start | bytes 786440 | tf_op jit(solution)/shard_map/ppermute | solution.py:31
  187.5 11.0 %collective-permute-start.42 = (bf16[128,256]{1,0:T(8,128)(2,1)S(1)}, bf16[128,256]{1,0:T(8,128)(2,1)S(1)}, u32[]{:S(2)}, u32[]{:S(2)}) collective-permute-start(bf16[128,256]{1,0:T(8,128)(2,1)S(1)} %get-tuple-element.185), channel_id=1, source_target_pairs={{0,4},{4,0},{8,12},{12,8},{1,5},{5,1},{9,13},{13,9},{2,6},{6,2},{1... | collective-permute-start | bytes 196616 | tf_op jit(solution)/shard_map/ppermute | solution.py:31
  198.5 9.3 %collective-permute-start.113 = (bf16[128,512]{1,0:T(8,128)(2,1)S(1)}, bf16[128,512]{1,0:T(8,128)(2,1)S(1)}, u32[]{:S(2)}, u32[]{:S(2)}) collective-permute-start(bf16[128,512]{1,0:T(8,128)(2,1)S(1)} %get-tuple-element.281), channel_id=1, source_target_pairs={{0,2},{1,3},{2,0},{3,1},{4,6},{5,7},{6,4},{7,5},{8,10},{9,11},{10,... | collective-permute-start | bytes 393224 | tf_op jit(solution)/shard_map/ppermute | solution.py:31
  200.2 21.0 %collective-permute-start.87 = (bf16[128,1024]{1,0:T(8,128)(2,1)S(1)}, bf16[128,1024]{1,0:T(8,128)(2,1)S(1)}, u32[]{:S(2)}, u32[]{:S(2)}) collective-permute-start(bf16[128,1024]{1,0:T(8,128)(2,1)S(1)} %get-tuple-element.247.refs_4_), channel_id=1, source_target_pairs={{0,2},{1,3},{2,0},{3,1},{4,6},{5,7},{6,4},{7,5},{8,10},{9,11},{10,... | collective-permute-start | bytes 786440 | tf_op jit(solution)/shard_map/ppermute | solution.py:31
  206.8 23.1 %collective-permute-start.83 = (bf16[128,1280]{1,0:T(8,128)(2,1)S(1)}, bf16[128,1280]{1,0:T(8,128)(2,1)S(1)}, u32[]{:S(2)}, u32[]{:S(2)}) collective-permute-start(bf16[128,1280]{1,0:T(8,128)(2,1)S(1)} %get-tuple-element.245), channel_id=1, source_target_pairs={{0,1},{1,0},{2,3},{3,2},{4,5},{5,4},{6,7},{7,6},{8,9},{9,8},{10,11... | collective-permute-start | bytes 983048 | tf_op jit(solution)/shard_map/ppermute | solution.py:31
  207.6 13.7 %collective-permute-start.99 = (bf16[128,768]{1,0:T(8,128)(2,1)S(1)}, bf16[128,768]{1,0:T(8,128)(2,1)S(1)}, u32[]{:S(2)}, u32[]{:S(2)}) collective-permute-start(bf16[128,768]{1,0:T(8,128)(2,1)S(1)} %collective-permute-done.98.refs_2_), channel_id=1, source_target_pairs={{0,1},{1,0},{2,3},{3,2},{4,5},{5,4},{6,7},{7,6},{8,9},{9,8},{10,11... | collective-permute-start | bytes 589832 | tf_op jit(solution)/shard_map/ppermute | solution.py:31
  218.5 26.5 %collective-permute-start.84 = (bf16[128,1536]{1,0:T(8,128)(2,1)S(1)}, bf16[128,1536]{1,0:T(8,128)(2,1)S(1)}, u32[]{:S(2)}, u32[]{:S(2)}) collective-permute-start(bf16[128,1536]{1,0:T(8,128)(2,1)S(1)} %get-tuple-element.246), channel_id=1, source_target_pairs={{0,2},{1,3},{2,0},{3,1},{4,6},{5,7},{6,4},{7,5},{8,10},{9,11},{10,... | collective-permute-start | bytes 1179656 | tf_op jit(solution)/shard_map/ppermute | solution.py:31
  225.7 20.9 %collective-permute-start.101 = (bf16[128,1280]{1,0:T(8,128)(2,1)S(1)}, bf16[128,1280]{1,0:T(8,128)(2,1)S(1)}, u32[]{:S(2)}, u32[]{:S(2)}) collective-permute-start(bf16[128,1280]{1,0:T(8,128)(2,1)S(1)} %get-tuple-element.258), channel_id=1, source_target_pairs={{0,2},{1,3},{2,0},{3,1},{4,6},{5,7},{6,4},{7,5},{8,10},{9,11},{10,... | collective-permute-start | bytes 983048 | tf_op jit(solution)/shard_map/ppermute | solution.py:31
  229.7 15.4 %collective-permute-start.100 = (bf16[128,1024]{1,0:T(8,128)(2,1)S(1)}, bf16[128,1024]{1,0:T(8,128)(2,1)S(1)}, u32[]{:S(2)}, u32[]{:S(2)}) collective-permute-start(bf16[128,1024]{1,0:T(8,128)(2,1)S(1)} %get-tuple-element.257), channel_id=1, source_target_pairs={{0,1},{1,0},{2,3},{3,2},{4,5},{5,4},{6,7},{7,6},{8,9},{9,8},{10,11... | collective-permute-start | bytes 786440 | tf_op jit(solution)/shard_map/ppermute | solution.py:31
  230.0 7.8 %collective-permute-start.67 = (bf16[32,1024]{1,0:T(8,128)(2,1)S(1)}, bf16[32,1024]{1,0:T(8,128)(2,1)S(1)}, u32[]{:S(2)}, u32[]{:S(2)}) collective-permute-start(bf16[32,1024]{1,0:T(8,128)(2,1)S(1)} %get-tuple-element.220.refs_0_), channel_id=1, source_target_pairs={{0,8},{4,12},{8,0},{12,4},{1,9},{5,13},{9,1},{13,5},{2,10},{6,14},... | collective-permute-start | bytes 196616 | tf_op jit(solution)/shard_map/ppermute | solution.py:31
  237.7 21.2 %collective-permute-start.78 = (bf16[128,1536]{1,0:T(8,128)(2,1)S(1)}, bf16[128,1536]{1,0:T(8,128)(2,1)S(1)}, u32[]{:S(2)}, u32[]{:S(2)}) collective-permute-start(bf16[128,1536]{1,0:T(8,128)(2,1)S(1)} %collective-permute-done.77.refs_2_), channel_id=1, source_target_pairs={{0,1},{1,0},{2,3},{3,2},{4,5},{5,4},{6,7},{7,6},{8,9},{9,8},{10,11... | collective-permute-start | bytes 1179656 | tf_op jit(solution)/shard_map/ppermute | solution.py:31
  246.6 12.8 %collective-permute-start.88 = (bf16[128,1024]{1,0:T(8,128)(2,1)S(1)}, bf16[128,1024]{1,0:T(8,128)(2,1)S(1)}, u32[]{:S(2)}, u32[]{:S(2)}) collective-permute-start(bf16[128,1024]{1,0:T(8,128)(2,1)S(1)} %collective-permute-done.87.refs_6_), channel_id=1, source_target_pairs={{0,1},{1,0},{2,3},{3,2},{4,5},{5,4},{6,7},{7,6},{8,9},{9,8},{10,11... | collective-permute-start | bytes 786440 | tf_op jit(solution)/shard_map/ppermute | solution.py:31
  246.6 12.9 %collective-permute-start.79 = (bf16[128,1024]{1,0:T(8,128)(2,1)S(1)}, bf16[128,1024]{1,0:T(8,128)(2,1)S(1)}, u32[]{:S(2)}, u32[]{:S(2)}) collective-permute-start(bf16[128,1024]{1,0:T(8,128)(2,1)S(1)} %get-tuple-element.243.refs_4_), channel_id=1, source_target_pairs={{0,1},{1,0},{2,3},{3,2},{4,5},{5,4},{6,7},{7,6},{8,9},{9,8},{10,11... | collective-permute-start | bytes 786440 | tf_op jit(solution)/shard_map/ppermute | solution.py:31
  248.4 11.5 %collective-permute-start.80 = (bf16[128,1024]{1,0:T(8,128)(2,1)S(1)}, bf16[128,1024]{1,0:T(8,128)(2,1)S(1)}, u32[]{:S(2)}, u32[]{:S(2)}) collective-permute-start(bf16[128,1024]{1,0:T(8,128)(2,1)S(1)} %get-tuple-element.243.refs_4_), channel_id=1, source_target_pairs={{0,2},{1,3},{2,0},{3,1},{4,6},{5,7},{6,4},{7,5},{8,10},{9,11},{10,... | collective-permute-start | bytes 786440 | tf_op jit(solution)/shard_map/ppermute | solution.py:31
  259.4 13.6 %collective-permute-start.93 = (bf16[128,768]{1,0:T(8,128)(2,1)S(1)}, bf16[128,768]{1,0:T(8,128)(2,1)S(1)}, u32[]{:S(2)}, u32[]{:S(2)}) collective-permute-start(bf16[128,768]{1,0:T(8,128)(2,1)S(1)} %get-tuple-element.253.refs_4_), channel_id=1, source_target_pairs={{0,1},{1,0},{2,3},{3,2},{4,5},{5,4},{6,7},{7,6},{8,9},{9,8},{10,11... | collective-permute-start | bytes 589832 | tf_op jit(solution)/shard_map/ppermute | solution.py:31
  259.5 14.1 %collective-permute-start.85 = (bf16[128,1536]{1,0:T(8,128)(2,1)S(1)}, bf16[128,1536]{1,0:T(8,128)(2,1)S(1)}, u32[]{:S(2)}, u32[]{:S(2)}) collective-permute-start(bf16[128,1536]{1,0:T(8,128)(2,1)S(1)} %collective-permute-done.84.refs_2_), channel_id=1, source_target_pairs={{0,1},{1,0},{2,3},{3,2},{4,5},{5,4},{6,7},{7,6},{8,9},{9,8},{10,11... | collective-permute-start | bytes 1179656 | tf_op jit(solution)/shard_map/ppermute | solution.py:31
  263.9 9.1 %collective-permute-start.74 = (bf16[144,256]{1,0:T(8,128)(2,1)S(1)}, bf16[144,256]{1,0:T(8,128)(2,1)S(1)}, u32[]{:S(2)}, u32[]{:S(2)}) collective-permute-start(bf16[144,256]{1,0:T(8,128)(2,1)S(1)} %get-tuple-element.237), channel_id=1, source_target_pairs={{0,12},{4,8},{8,4},{12,0},{1,13},{5,9},{9,5},{13,1},{2,14},{6,10},... | collective-permute-start | bytes 221192 | tf_op jit(solution)/shard_map/ppermute | solution.py:31
  271.5 14.8 %collective-permute-start.111 = (bf16[256,1024]{1,0:T(8,128)(2,1)S(1)}, bf16[256,1024]{1,0:T(8,128)(2,1)S(1)}, u32[]{:S(2)}, u32[]{:S(2)}) collective-permute-start(bf16[256,1024]{1,0:T(8,128)(2,1)S(1)} %shard_map.301.own_ref), channel_id=1, source_target_pairs={{0,16},{16,0},{1,17},{17,1},{2,18},{18,2},{3,19},{19,3},{4,20},{20... | collective-permute-start | bytes 1572872 | tf_op jit(solution)/shard_map/ppermute | solution.py:31
  274.6 23.0 %collective-permute-start.115 = (bf16[256,1024]{1,0:T(8,128)(2,1)S(1)}, bf16[256,1024]{1,0:T(8,128)(2,1)S(1)}, u32[]{:S(2)}, u32[]{:S(2)}) collective-permute-start(bf16[256,1024]{1,0:T(8,128)(2,1)S(1)} %shard_map.302.own_ref), channel_id=1, source_target_pairs={{0,16},{16,0},{1,17},{17,1},{2,18},{18,2},{3,19},{19,3},{4,20},{20... | collective-permute-start | bytes 1572872 | tf_op jit(solution)/shard_map/ppermute | solution.py:31
  275.6 33.8 %collective-permute-start.89 = (bf16[272,1024]{1,0:T(8,128)(2,1)S(1)}, bf16[272,1024]{1,0:T(8,128)(2,1)S(1)}, u32[]{:S(2)}, u32[]{:S(2)}) collective-permute-start(bf16[272,1024]{1,0:T(8,128)(2,1)S(1)} %shard_map.290.own_ref), channel_id=1, source_target_pairs={{0,16},{16,0},{1,17},{17,1},{2,18},{18,2},{3,19},{19,3},{4,20},{20... | collective-permute-start | bytes 1671176 | tf_op jit(solution)/shard_map/ppermute | solution.py:31
  278.2 43.2 %collective-permute-start.103 = (bf16[272,1024]{1,0:T(8,128)(2,1)S(1)}, bf16[272,1024]{1,0:T(8,128)(2,1)S(1)}, u32[]{:S(2)}, u32[]{:S(2)}) collective-permute-start(bf16[272,1024]{1,0:T(8,128)(2,1)S(1)} %shard_map.294.own_ref), channel_id=1, source_target_pairs={{0,16},{16,0},{1,17},{17,1},{2,18},{18,2},{3,19},{19,3},{4,20},{20... | collective-permute-start | bytes 1671176 | tf_op jit(solution)/shard_map/ppermute | solution.py:31
  278.7 54.6 %collective-permute-start.82 = (bf16[272,1024]{1,0:T(8,128)(2,1)S(1)}, bf16[272,1024]{1,0:T(8,128)(2,1)S(1)}, u32[]{:S(2)}, u32[]{:S(2)}) collective-permute-start(bf16[272,1024]{1,0:T(8,128)(2,1)S(1)} %shard_map.289.own_ref), channel_id=1, source_target_pairs={{0,16},{16,0},{1,17},{17,1},{2,18},{18,2},{3,19},{19,3},{4,20},{20... | collective-permute-start | bytes 1671176 | tf_op jit(solution)/shard_map/ppermute | solution.py:31
  286.3 56.0 %collective-permute-start.96 = (bf16[272,768]{1,0:T(8,128)(2,1)S(1)}, bf16[272,768]{1,0:T(8,128)(2,1)S(1)}, u32[]{:S(2)}, u32[]{:S(2)}) collective-permute-start(bf16[272,768]{1,0:T(8,128)(2,1)S(1)} %shard_map.293.own_ref), channel_id=1, source_target_pairs={{0,16},{16,0},{1,17},{17,1},{2,18},{18,2},{3,19},{19,3},{4,20},{20... | collective-permute-start | bytes 1253384 | tf_op jit(solution)/shard_map/ppermute | solution.py:31
  297.5 46.7 %collective-permute-start.107 = (bf16[256,256]{1,0:T(8,128)(2,1)S(1)}, bf16[256,256]{1,0:T(8,128)(2,1)S(1)}, u32[]{:S(2)}, u32[]{:S(2)}) collective-permute-start(bf16[256,256]{1,0:T(8,128)(2,1)S(1)} %shard_map.299.own_ref), channel_id=1, source_target_pairs={{0,16},{16,0},{1,17},{17,1},{2,18},{18,2},{3,19},{19,3},{4,20},{20... | collective-permute-start | bytes 393224 | tf_op jit(solution)/shard_map/ppermute | solution.py:31
  309.5 35.5 %collective-permute-start.75 = (f32[16,256]{1,0:T(8,128)S(1)}, f32[16,256]{1,0:T(8,128)S(1)}, u32[]{:S(2)}, u32[]{:S(2)}) collective-permute-start(f32[16,256]{1,0:T(8,128)S(1)} %get-tuple-element.239.refs_0_), channel_id=1, source_target_pairs={{0,16},{16,0},{1,17},{17,1},{2,18},{18,2},{3,19},{19,3},{4,20},{20... | collective-permute-start | bytes 49160 | tf_op jit(solution)/shard_map/ppermute | solution.py:31
  (70 other events, 407.8 us)

commit v3 on v2

--- a/solution.py
+++ b/solution.py
@@ -283,13 +283,22 @@
 
 def row_blocks(got, size):
     length, width = got[0].shape
-    rows = length // size
-
-    def kernel(*refs):
-        for step in range(size):
-            refs[len(got) + step][...] = own_rows(refs[: len(got)], step, rows)
-
-    return run(kernel, list(got), [shaped((rows, width * len(got)), BF)] * size)
+    rows, cols = length // size, len(got)
+    steps = sends_of(cols)
+
+    def kernel(*refs):
+        whole = [own_rows(refs[:cols], step, rows) for step in range(size)]
+        for step, value in enumerate(whole):
+            refs[cols + step][...] = value
+        whole = jnp.concatenate(whole, axis=0)
+        bundle_into(refs[cols + size :], steps, [], [whole], width)
+
+    outs = run(
+        kernel,
+        list(got),
+        [shaped((rows, width * cols), BF)] * size + bundle_shapes(length, steps, 0, 1, width),
+    )
+    return outs[:size], outs[size:]
 
 
 def next_norm(resid, parts, vecs, layer, bias_at, gain_at, shift_at):
@@ -500,7 +509,6 @@
     length = size * rows
     width = full // cols
     units = slope.shape[1]
-    steps = sends_of(cols)
 
     def kernel(*refs):
         block_refs = refs[:size]
@@ -508,7 +516,6 @@
         slope_ref = refs[size + cols]
         part_refs = refs[size + cols + 1 : 2 * size + cols + 1]
         pre_ref = refs[2 * size + cols + 1]
-        send_refs = refs[2 * size + cols + 2 :]
         full_grad = gathered(block_refs)
         grad_hidden = jnp.concatenate(
             [
@@ -531,16 +538,14 @@
             [low(dot_right(grad_pre, pack_ref[:, :units])) for pack_ref in pack_refs], axis=1
         )
         cut_rows(partial, part_refs)
-        bundle_into(send_refs, steps, [], [full_grad], width)
 
     outs = run(
         kernel,
         [*blocks, *packs, slope],
         [shaped((rows, full), BF)] * size
-        + [shaped((length, units), BF)]
-        + bundle_shapes(length, steps, 0, 1, width),
-    )
-    return outs[:size], outs[size], outs[size + 1 :]
+        + [shaped((length, units), BF)],
+    )
+    return outs[:size], outs[size]
 
 
 def bundle_blocks(blocks, cols):
@@ -718,13 +723,12 @@
     cols = len(ahead)
 
     def kernel(*refs):
-        ahead_refs, pre_refs, out_ref = refs[:cols], refs[cols : 2 * cols], refs[2 * cols]
+        ahead_refs, pre_refs = refs[:cols], refs[cols : 2 * cols]
         pre_all = gathered(pre_refs)
-        out_ref[:width, :] = low(dot_left(slices_of(ahead_refs, units, width), pre_all))
-        total = jnp.sum(wide(pre_all), axis=0, keepdims=True)
-        out_ref[width:, :] = low(jnp.broadcast_to(total, (16, units)))
-
-    return run(kernel, [*ahead, *pres], [shaped((width + 16, units), BF)])[0]
+        refs[-2][...] = low(dot_left(slices_of(ahead_refs, units, width), pre_all))
+        refs[-1][...] = jnp.sum(wide(pre_all), axis=0, keepdims=True)
+
+    return run(kernel, [*ahead, *pres], [shaped((width, units), BF), shaped((1, units), F32)])
 
 
 def attention_changes(ahead, joined, across, width, middles=None):
@@ -734,23 +738,21 @@
         ahead_refs, joined_refs, out_refs = refs[:cols], refs[cols : 2 * cols], refs[2 * cols :]
         out_ref = out_refs[0]
         joined_all = rows_of(joined_refs, lambda _: slice(0, 3 * across))
-        out_ref[:width, : 3 * across] = low(
-            dot_left(slices_of(ahead_refs, across, width), joined_all)
-        )
-        total = jnp.sum(wide(joined_all), axis=0, keepdims=True)
-        out_ref[width:, : 3 * across] = low(jnp.broadcast_to(total, (16, 3 * across)))
+        out_ref[:, : 3 * across] = low(dot_left(slices_of(ahead_refs, across, width), joined_all))
+        out_refs[1][...] = jnp.sum(wide(joined_all), axis=0, keepdims=True)
         if middles is None:
             output_part(ahead_refs, joined_refs, 3 * across, out_ref, 3 * across)
-            out_ref[width:, 3 * across :] = jnp.zeros((16, out_ref.shape[1] - 3 * across), BF)
 
     def output_part(ahead_refs, middle_refs, shared, out_ref, column):
         mixed_all = rows_of(ahead_refs, lambda _: slice(0, across))
         change = low(dot_left(mixed_all, slices_of(middle_refs, shared, width)))
         for at in range(0, across, width):
-            out_ref[:width, column + at : column + at + width] = change[at : at + width]
+            out_ref[:, column + at : column + at + width] = change[at : at + width]
 
     columns = 3 * across if middles else 4 * across
-    return run(kernel, [*ahead, *joined], [shaped((width + 16, columns), BF)])[0]
+    return run(
+        kernel, [*ahead, *joined], [shaped((width, columns), BF), shaped((1, 3 * across), F32)]
+    )
 
 
 def output_changes(ahead, middles, across, width):
@@ -765,64 +767,61 @@
     return run(kernel, [*ahead, *middles], [shaped((width, across), BF)])[0]
 
 
-def finish(own, other, layer, cuts, shapes, kept, line):
-    width = own.shape[0] - (16 if line else 0)
+def finish(own, other, layer, cuts, shapes, kept):
+    width = own.shape[0]
+    kept = kept or ()
 
     def kernel(own_ref, other_ref, *refs):
-        out_refs = refs[len(kept or ()) :]
-        for out_ref, pieces in zip(out_refs, cuts):
-            row = 0
-            for start, stop in pieces:
-                out_ref[0, row : row + width, :] = wide(own_ref[:width, start:stop]) + wide(
-                    other_ref[:width, start:stop]
+        for out_ref, pieces in zip(refs[len(kept) :], cuts):
+            for at, (start, stop) in enumerate(pieces):
+                out_ref[0, at * width : (at + 1) * width, :] = wide(own_ref[:, start:stop]) + wide(
+                    other_ref[:, start:stop]
                 )
-                row += width
-        if line:
-            out_refs[-1][...] = wide(own_ref[width : width + 8, :]) + wide(
-                other_ref[width : width + 8, :]
-            )
 
     def whole(array):
         return pl.BlockSpec(array.shape, lambda at: (0, 0))
 
-    lines = [shaped((8, own.shape[1]), F32)] if line else []
     return pl.pallas_call(
         kernel,
         grid=(1,),
-        in_specs=[whole(own), whole(other)] + [ANY] * len(kept or ()),
-        out_specs=[pl.BlockSpec((1,) + shape[1:], lambda at: (layer, 0, 0)) for shape in shapes]
-        + [whole(array) for array in lines],
-        out_shape=[shaped(shape, F32) for shape in shapes] + lines,
-        input_output_aliases={2 + at: at for at in range(len(kept or ()))},
+        in_specs=[whole(own), whole(other)] + [ANY] * len(kept),
+        out_specs=[pl.BlockSpec((1,) + shape[1:], lambda at: (layer, 0, 0)) for shape in shapes],
+        out_shape=[shaped(shape, F32) for shape in shapes],
+        input_output_aliases={2 + at: at for at in range(len(kept))},
         compiler_params=pltpu.CompilerParams(vmem_limit_bytes=VMEM_LIMIT),
-    )(own, other, *(kept or ()))
-
-
-def finish_vectors(own, other, up_lines, joined_lines, across):
+    )(own, other, *kept)
+
+
+def finish_vectors(own, other, units, across):
     width = own.shape[1]
-    units = up_lines[0].shape[1]
     heads = across // HD
 
-    def kernel(*refs):
-        own_ref, other_ref = refs[:2]
-        up_refs = refs[2 : 2 + LAYERS]
-        joined_refs = refs[2 + LAYERS : 2 + 2 * LAYERS]
-        outs = refs[2 + 2 * LAYERS :]
+    def kernel(own_ref, other_ref, *outs):
         total = own_ref[...] + other_ref[...]
+        row = 16
+
+        def line(columns):
+            nonlocal row
+            rows = columns // width
+            parts = [total[row + at : row + at + 1, :] for at in range(rows)]
+            row += rows
+            return jnp.concatenate(parts, axis=1)
+
         for layer in range(LAYERS):
             here = slice(layer, layer + 1)
             for slot in range(6):
                 outs[slot][here, :] = total[6 * layer + slot : 6 * layer + slot + 1, :]
-            outs[6][here, :] = up_refs[layer][:1, :]
+            outs[6][here, :] = line(units)
+            joined = line(3 * across)
             for head in range(heads):
                 at = head * 3 * HD
                 there = slice(head * HD, (head + 1) * HD)
-                outs[7][here, there] = joined_refs[layer][:1, at : at + HD]
-                outs[8][here, there] = joined_refs[layer][:1, at + 2 * HD : at + 3 * HD]
+                outs[7][here, there] = joined[:, at : at + HD]
+                outs[8][here, there] = joined[:, at + 2 * HD : at + 3 * HD]
 
     return run(
         kernel,
-        [own, other, *up_lines, *joined_lines],
+        [own, other],
         [shaped((LAYERS, width), F32)] * 6
         + [shaped((LAYERS, units), F32)]
         + [shaped((LAYERS, across), F32)] * 2,
@@ -834,25 +833,34 @@
     return trade(got, COL)
 
 
-def turn_sum(blocks, dtype, extra=0):
-    got = turn_blocks(trade(blocks, COL), extra)
-    return sum_blocks(trade(got, ROW), dtype, extra)
-
-
-def sum_blocks(got, dtype, extra):
+def turn_sum(blocks, dtype):
+    got = turn_blocks(trade(blocks, COL))
+    return sum_blocks(trade(got, ROW), dtype)
+
+
+def sum_blocks(got, dtype, extra=0, lines=()):
     rows, width = got[0].shape[0] - extra, got[0].shape[1]
+    below = sum(line.shape[1] for line in lines) // width
+    padded = -(-(extra + below) // 8) * 8
 
     def kernel(*refs):
         parts = refs[: len(got)]
+        line_refs = refs[len(got) : len(got) + len(lines)]
+        outs = refs[len(got) + len(lines) :]
         total = tree_sum([wide(ref[:rows, :]) for ref in parts])
-        refs[len(got)][...] = total.astype(dtype)
+        outs[0][...] = total.astype(dtype)
         if extra:
-            refs[len(got) + 1][...] = tree_sum([wide(ref[rows:, :]) for ref in parts])
+            values = [tree_sum([wide(ref[rows:, :]) for ref in parts])]
+            for ref in line_refs:
+                values += [ref[:, at : at + width] for at in range(0, ref.shape[1], width)]
+            if padded > extra + below:
+                values.append(jnp.zeros((padded - extra - below, width), F32))
+            outs[1][...] = jnp.concatenate(values, axis=0)
 
     outs = [shaped((rows, width), dtype)]
     if extra:
-        outs.append(shaped((extra, width), F32))
-    return run(kernel, list(got), outs)
+        outs.append(shaped((padded, width), F32))
+    return run(kernel, [*got, *lines], outs)
 
 
 def shards(
@@ -894,7 +902,8 @@
             pack = pack_weights(*pair, layer, width, first)
             weights[layer].append(relay_all(pack, COL))
     got = turn(block_input)
-    grad_blocks = row_blocks(turn(cotangent), size)
+    grad_blocks, sends = row_blocks(turn(cotangent), size)
+    grads = exchange(sends)
     resid, last_kept, input_blocks = first_norm(got, vecs, size)
     stats = None
     saved = []
@@ -936,8 +945,9 @@
     for layer in reversed(range(LAYERS)):
         attention_packs, feed_packs = weights[layer]
         first_kept, second_kept, qkv, probs, slope, attention_ahead, feed_ahead = saved[layer]
-        parts, grad_pre, sends = feed_backward(grad_blocks, feed_packs, slope)
-        grads = exchange(sends)
+        if not layer:
+            grads = exchange(bundle_blocks(grad_blocks, cols))
+        parts, grad_pre = feed_backward(grad_blocks, feed_packs, slope)
         pres = relay_all(grad_pre, COL)
         grad_middle, middle_low, second_sums = norm_backward(
             grad_resid, trade(parts, ROW), *second_kept, vecs, layer, GAIN_TWO, True
@@ -963,7 +973,7 @@
             grad_blocks = spread(grad_low, ROW)
             sums = [first_sums, second_sums] + sums
         else:
-            input_gradient, totals = turn_sum(parts, F32, 16)
+            parts = trade(turn_blocks(trade(parts, COL), 16), ROW)
         change = down_changes(feed_ahead, grads, units, width)
         down_outs = finish(
             change,
@@ -972,39 +982,32 @@
             [[(at, at + width) for at in range(0, units, width)]],
             [downward_weight.shape],
             down_outs,
-            False,
-        )
-        change = up_changes(feed_ahead, pres, units, width)
-        *up_outs, up_lines[layer] = finish(
-            change,
-            axis_swap(change, DP, 1),
-            layer,
-            [[(0, units)]],
-            [upward_weight.shape],
-            up_outs,
-            True,
-        )
-        change = attention_changes(attention_ahead, joined, across, width, middles)
+        )
+        change, up_lines[layer] = up_changes(feed_ahead, pres, units, width)
+        up_outs = finish(
+            change, axis_swap(change, DP, 1), layer, [[(0, units)]], [upward_weight.shape], up_outs
+        )
+        change, joined_lines[layer] = attention_changes(
+            attention_ahead, joined, across, width, middles
+        )
         output_cut = [(at, at + width) for at in range(0, across, width)]
         if layer:
-            joined_out, output_out, joined_lines[layer] = finish(
+            joined_out, output_out = finish(
                 change,
                 axis_swap(change, DP, 1),
                 layer,
                 [[(0, 3 * across)], [(3 * across + one, 3 * across + two) for one, two in output_cut]],
                 [joined_weight.shape, output_weight.shape],
                 None,
-                True,
             )
         else:
-            joined_out, joined_lines[layer] = finish(
+            (joined_out,) = finish(
                 change,
                 axis_swap(change, DP, 1),
                 layer,
                 [[(0, 3 * across)]],
                 [joined_weight.shape],
                 [joined_out],
-                True,
             )
             change = output_changes(attention_ahead, middles, across, width)
             (output_out,) = finish(
@@ -1014,9 +1017,10 @@
                 [output_cut],
                 [output_weight.shape],
                 [output_out],
-                False,
             )
-    vector_sums = finish_vectors(totals, axis_swap(totals, DP, 1), up_lines, joined_lines, across)
+    lines = [line for pair in zip(up_lines, joined_lines) for line in pair]
+    input_gradient, totals = sum_blocks(parts, F32, 16, lines)
+    vector_sums = finish_vectors(totals, axis_swap(totals, DP, 1), units, across)
     return (
         block_output,
         input_gradient,

time: 346 us -> 338 us (0.977)
  waiting for transfers between devices: 214 us -> 196 us
  starting transfers between devices: 97.9 us -> 108 us
    ppermute x116, waiting for transfers between devices: 214 us -> 196 us  [axis_swap(): lax.ppermute(local, axis, [(place, place ^ step) for place in range(size)])]
    ppermute x116, starting transfers between devices: 97.9 us -> 108 us  [axis_swap(): lax.ppermute(local, axis, [(place, place ^ step) for place in range(size)])]
    pallas_call x32 -> x33, Pallas kernels: 20.7 us -> 20.5 us  [run(): pl.pallas_call(kernel, in_specs=[spec or VMEM] * len(arrays), out_specs=[...]
  transfers between devices with their start and end apart: 116 -> 116, of which waited for: 54 -> 53; matrix products, arithmetic and copies ran while one was open for 0% -> 0% of each run, Pallas kernels for 9% -> 9%
where the time goes in v3:
time: 338 us
  waiting for transfers between devices  196 us (58%)
  starting transfers between devices  108 us (32%)
  Pallas kernels  32.2 us (10%)
    ppermute x116, waiting for transfers between devices, axis_swap(): lax.ppermute(local, axis, [(place, place ^ step) for place in range(size)])  196 us
    ppermute x116, starting transfers between devices, axis_swap(): lax.ppermute(local, axis, [(place, place ^ step) for place in range(size)])  108 us
    pallas_call x33, Pallas kernels, run(): pl.pallas_call(kernel, in_specs=[spec or VMEM] * len(arrays), out_specs=[...  20.5 us
    pallas_call x7, Pallas kernels, finish(): pl.pallas_call(kernel, grid=(1,), in_specs=[whole(own), whole(other)] + [...  7.07 us
  transfers between devices with their start and end apart: 116, of which 53 were waited for; matrix products, arithmetic and copies ran while one was open for 0% of the time, Pallas kernels for 9%

profile of v3, /device:TPU:0, one launch (start us, length us, event | category | flops | bytes accessed | tf_op | source)
XLA Modules:
  0.0 337.7 jit_solution(10287262607084878265)
XLA Ops:
  1.9 3.0 collective-permute-start.19
  6.1 2.1 collective-permute-start
  11.0 2.6 collective-permute-start.1
  15.4 2.0 collective-permute-done.1.refs_2_
  17.4 2.2 collective-permute-done.2.refs_3_
  20.3 41.9 %collective-permute-done.7.refs_6_.refs_12_.refs_16_ = f32[12,256]{1,0:T(8,128)S(1)} collective-permute-done((f32[12,256]{1,0:T(8,128)S(1)}, f32[12,256]{1,0:T(8,128)S(1)}, u32[]{:S(2)}, u32[]{:S(2)}) %collective-permute-start.7) | collective-permute-done | bytes 12320 | tf_op jit(solution)/shard_map/ppermute | solution.py:31
  65.1 2.5 collective-permute-done.4.refs_2_
  74.6 2.0 shard_map.266
  78.7 2.6 collective-permute-start.13
  82.1 3.2 collective-permute-start.14
  85.7 2.5 collective-permute-done.14.refs_3_
  88.4 3.7 %collective-permute-start.16 = (bf16[32,1024]{1,0:T(8,128)(2,1)S(1)}, bf16[32,1024]{1,0:T(8,128)(2,1)S(1)}, u32[]{:S(2)}, u32[]{:S(2)}) collective-permute-start(bf16[32,1024]{1,0:T(8,128)(2,1)S(1)} %get-tuple-element.167.refs_0_), channel_id=1, source_target_pairs={{0,8},{4,12},{8,0},{12,4},{1,9},{5,13},{9,1},{13,5},{2,10},{6,14},... | collective-permute-start | bytes 196616 | tf_op jit(solution)/shard_map/ppermute | solution.py:31
  92.9 4.4 %collective-permute-start.17 = (bf16[32,1024]{1,0:T(8,128)(2,1)S(1)}, bf16[32,1024]{1,0:T(8,128)(2,1)S(1)}, u32[]{:S(2)}, u32[]{:S(2)}) collective-permute-start(bf16[32,1024]{1,0:T(8,128)(2,1)S(1)} %get-tuple-element.167.refs_0_), channel_id=1, source_target_pairs={{0,12},{4,8},{8,4},{12,0},{1,13},{5,9},{9,5},{13,1},{2,14},{6,10},... | collective-permute-start | bytes 196616 | tf_op jit(solution)/shard_map/ppermute | solution.py:31
  97.2 2.2 collective-permute-done.17.refs_3_
  101.5 4.8 %collective-permute-done.46.refs_2_ = bf16[128,256]{1,0:T(8,128)(2,1)S(1)} collective-permute-done((bf16[128,256]{1,0:T(8,128)(2,1)S(1)}, bf16[128,256]{1,0:T(8,128)(2,1)S(1)}, u32[]{:S(2)}, u32[]{:S(2)}) %collective-permute-start.46) | collective-permute-done | bytes 65568 | tf_op jit(solution)/shard_map/ppermute | solution.py:31
  106.7 3.8 %collective-permute-done.21.refs_1_ = bf16[32,1024]{1,0:T(8,128)(2,1)S(1)} collective-permute-done((bf16[32,1024]{1,0:T(8,128)(2,1)S(1)}, bf16[32,1024]{1,0:T(8,128)(2,1)S(1)}, u32[]{:S(2)}, u32[]{:S(2)}) %collective-permute-start.21) | collective-permute-done | bytes 65568 | tf_op jit(solution)/shard_map/ppermute | solution.py:31
  111.5 5.3 %collective-permute-done.22.refs_2_ = bf16[32,1024]{1,0:T(8,128)(2,1)S(1)} collective-permute-done((bf16[32,1024]{1,0:T(8,128)(2,1)S(1)}, bf16[32,1024]{1,0:T(8,128)(2,1)S(1)}, u32[]{:S(2)}, u32[]{:S(2)}) %collective-permute-start.22) | collective-permute-done | bytes 65568 | tf_op jit(solution)/shard_map/ppermute | solution.py:31
  118.7 4.5 %collective-permute-done.23.refs_3_ = bf16[32,1024]{1,0:T(8,128)(2,1)S(1)} collective-permute-done((bf16[32,1024]{1,0:T(8,128)(2,1)S(1)}, bf16[32,1024]{1,0:T(8,128)(2,1)S(1)}, u32[]{:S(2)}, u32[]{:S(2)}) %collective-permute-start.23) | collective-permute-done | bytes 65568 | tf_op jit(solution)/shard_map/ppermute | solution.py:31
  124.9 4.3 %collective-permute-done.47.refs_3_ = bf16[128,256]{1,0:T(8,128)(2,1)S(1)} collective-permute-done((bf16[128,256]{1,0:T(8,128)(2,1)S(1)}, bf16[128,256]{1,0:T(8,128)(2,1)S(1)}, u32[]{:S(2)}, u32[]{:S(2)}) %collective-permute-start.47) | collective-permute-done | bytes 65568 | tf_op jit(solution)/shard_map/ppermute | solution.py:31
  129.3 2.7 collective-permute-start.25
  135.8 2.2 collective-permute-done.26.refs_3_
  138.0 2.0 shard_map.272
  146.2 2.5 collective-permute-done.31.refs_2_
  150.5 5.2 %collective-permute-done.32.refs_3_ = bf16[32,1024]{1,0:T(8,128)(2,1)S(1)} collective-permute-done((bf16[32,1024]{1,0:T(8,128)(2,1)S(1)}, bf16[32,1024]{1,0:T(8,128)(2,1)S(1)}, u32[]{:S(2)}, u32[]{:S(2)}) %collective-permute-start.32) | collective-permute-done | bytes 65568 | tf_op jit(solution)/shard_map/ppermute | solution.py:31
  158.2 2.5 collective-permute-start.35
  161.6 2.7 collective-permute-done.35.refs_3_
  167.9 2.2 collective-permute-start.52
  171.5 2.9 collective-permute-done.52.refs_2_
  174.4 2.1 collective-permute-start.53
  176.5 4.0 %collective-permute-done.53.refs_3_ = bf16[32,1024]{1,0:T(8,128)(2,1)S(1)} collective-permute-done((bf16[32,1024]{1,0:T(8,128)(2,1)S(1)}, bf16[32,1024]{1,0:T(8,128)(2,1)S(1)}, u32[]{:S(2)}, u32[]{:S(2)}) %collective-permute-start.53) | collective-permute-done | bytes 65568 | tf_op jit(solution)/shard_map/ppermute | solution.py:31
  180.9 2.7 collective-permute-start.55
  193.8 2.1 collective-permute-start.59
  197.3 4.7 %collective-permute-start.91 = (bf16[128,1024]{1,0:T(8,128)(2,1)S(1)}, bf16[128,1024]{1,0:T(8,128)(2,1)S(1)}, u32[]{:S(2)}, u32[]{:S(2)}) collective-permute-start(bf16[128,1024]{1,0:T(8,128)(2,1)S(1)} %get-tuple-element.251.refs_4_), channel_id=1, source_target_pairs={{0,2},{1,3},{2,0},{3,1},{4,6},{5,7},{6,4},{7,5},{8,10},{9,11},{10,... | collective-permute-start | bytes 786440 | tf_op jit(solution)/shard_map/ppermute | solution.py:31
  204.5 3.3 collective-permute-done.43.refs_2_
  210.6 5.7 %collective-permute-done.61.refs_2_ = bf16[32,1024]{1,0:T(8,128)(2,1)S(1)} collective-permute-done((bf16[32,1024]{1,0:T(8,128)(2,1)S(1)}, bf16[32,1024]{1,0:T(8,128)(2,1)S(1)}, u32[]{:S(2)}, u32[]{:S(2)}) %collective-permute-start.61) | collective-permute-done | bytes 65568 | tf_op jit(solution)/shard_map/ppermute | solution.py:31
  217.7 4.6 %collective-permute-done.44.refs_3_ = bf16[128,256]{1,0:T(8,128)(2,1)S(1)} collective-permute-done((bf16[128,256]{1,0:T(8,128)(2,1)S(1)}, bf16[128,256]{1,0:T(8,128)(2,1)S(1)}, u32[]{:S(2)}, u32[]{:S(2)}) %collective-permute-start.44) | collective-permute-done | bytes 65568 | tf_op jit(solution)/shard_map/ppermute | solution.py:31
  222.8 2.5 collective-permute-start.64
  228.2 4.4 %collective-permute-done.65.refs_3_ = bf16[32,1024]{1,0:T(8,128)(2,1)S(1)} collective-permute-done((bf16[32,1024]{1,0:T(8,128)(2,1)S(1)}, bf16[32,1024]{1,0:T(8,128)(2,1)S(1)}, u32[]{:S(2)}, u32[]{:S(2)}) %collective-permute-start.65) | collective-permute-done | bytes 65568 | tf_op jit(solution)/shard_map/ppermute | solution.py:31
  233.6 2.5 collective-permute-start.67
  236.0 3.1 collective-permute-done.66.refs_1_
  241.1 4.1 %collective-permute-done.68.refs_3_ = bf16[32,1024]{1,0:T(8,128)(2,1)S(1)} collective-permute-done((bf16[32,1024]{1,0:T(8,128)(2,1)S(1)}, bf16[32,1024]{1,0:T(8,128)(2,1)S(1)}, u32[]{:S(2)}, u32[]{:S(2)}) %collective-permute-start.68) | collective-permute-done | bytes 65568 | tf_op jit(solution)/shard_map/ppermute | solution.py:31
  246.7 2.0 shard_map.286
  251.9 2.0 collective-permute-done.70.refs_2_
  257.2 5.9 %collective-permute-done.79.refs_6_ = bf16[128,1024]{1,0:T(8,128)(2,1)S(1)} collective-permute-done((bf16[128,1024]{1,0:T(8,128)(2,1)S(1)}, bf16[128,1024]{1,0:T(8,128)(2,1)S(1)}, u32[]{:S(2)}, u32[]{:S(2)}) %collective-permute-start.79) | collective-permute-done | bytes 262176 | tf_op jit(solution)/shard_map/ppermute | solution.py:31
  263.0 2.8 collective-permute-done.103.refs_6_
  280.8 10.7 %collective-permute-done.99.other_ref = f32[32,256]{1,0:T(8,128)S(1)} collective-permute-done((f32[32,256]{1,0:T(8,128)S(1)}, f32[32,256]{1,0:T(8,128)S(1)}, u32[]{:S(2)}, u32[]{:S(2)}) %collective-permute-start.99) | collective-permute-done | bytes 32800 | tf_op jit(solution)/shard_map/ppermute | solution.py:31
  298.8 3.9 %collective-permute-done.115.other_ref = bf16[256,1024]{1,0:T(8,128)(2,1)S(1)} collective-permute-done((bf16[256,1024]{1,0:T(8,128)(2,1)S(1)}, bf16[256,1024]{1,0:T(8,128)(2,1)S(1)}, u32[]{:S(2)}, u32[]{:S(2)}) %collective-permute-start.115) | collective-permute-done | bytes 524320 | tf_op jit(solution)/shard_map/ppermute | solution.py:31
  303.9 29.5 %collective-permute-done.100.other_ref = bf16[256,768]{1,0:T(8,128)(2,1)S(1)} collective-permute-done((bf16[256,768]{1,0:T(8,128)(2,1)S(1)}, bf16[256,768]{1,0:T(8,128)(2,1)S(1)}, u32[]{:S(2)}, u32[]{:S(2)}) %collective-permute-start.100) | collective-permute-done | bytes 393248 | tf_op jit(solution)/shard_map/ppermute | solution.py:31
  (232 shorter events, 109.2 us)
Async XLA Ops:
  1.9 68.0 %collective-permute-start.19 = (bf16[256,2048]{1,0:T(8,128)(2,1)S(1)}, bf16[256,2048]{1,0:T(8,128)(2,1)S(1)}, u32[]{:S(2)}, u32[]{:S(2)}) collective-permute-start(bf16[256,2048]{1,0:T(8,128)(2,1)S(1)} %shard_map.268.refs_4_), channel_id=1, source_target_pairs={{0,2},{1,3},{2,0},{3,1},{4,6},{5,7},{6,4},{7,5},{8,10},{9,11},{10,... | collective-permute-start | bytes 3145736 | tf_op jit(solution)/shard_map/ppermute | solution.py:31
  6.0 63.5 %collective-permute-start.10 = (bf16[256,1024]{1,0:T(8,128)(2,1)S(1)}, bf16[256,1024]{1,0:T(8,128)(2,1)S(1)}, u32[]{:S(2)}, u32[]{:S(2)}) collective-permute-start(bf16[256,1024]{1,0:T(8,128)(2,1)S(1)} %shard_map.265.refs_4_), channel_id=1, source_target_pairs={{0,2},{1,3},{2,0},{3,1},{4,6},{5,7},{6,4},{7,5},{8,10},{9,11},{10,... | collective-permute-start | bytes 1572872 | tf_op jit(solution)/shard_map/ppermute | solution.py:31
  6.1 7.5 %collective-permute-start = (bf16[128,256]{1,0:T(8,128)(2,1)S(1)}, bf16[128,256]{1,0:T(8,128)(2,1)S(1)}, u32[]{:S(2)}, u32[]{:S(2)}) collective-permute-start(bf16[128,256]{1,0:T(8,128)(2,1)S(1)} %copy-done), channel_id=1, source_target_pairs={{0,4},{4,0},{8,12},{12,8},{1,5},{5,1},{9,13},{13,9},{2,6},{6,2},{1... | collective-permute-start | bytes 196616 | tf_op jit(solution)/shard_map/ppermute | solution.py:31
  9.4 69.3 %collective-permute-start.37 = (bf16[256,2048]{1,0:T(8,128)(2,1)S(1)}, bf16[256,2048]{1,0:T(8,128)(2,1)S(1)}, u32[]{:S(2)}, u32[]{:S(2)}) collective-permute-start(bf16[256,2048]{1,0:T(8,128)(2,1)S(1)} %shard_map.274.refs_4_), channel_id=1, source_target_pairs={{0,2},{1,3},{2,0},{3,1},{4,6},{5,7},{6,4},{7,5},{8,10},{9,11},{10,... | collective-permute-start | bytes 3145736 | tf_op jit(solution)/shard_map/ppermute | solution.py:31
  19.6 42.5 %collective-permute-start.7 = (f32[12,256]{1,0:T(8,128)S(1)}, f32[12,256]{1,0:T(8,128)S(1)}, u32[]{:S(2)}, u32[]{:S(2)}) collective-permute-start(f32[12,256]{1,0:T(8,128)S(1)} %get-tuple-element.154.refs_4_.refs_10_.refs_14_), channel_id=1, source_target_pairs={{0,2},{1,3},{2,0},{3,1},{4,6},{5,7},{6,4},{7,5},{8,10},{9,11},{10,... | collective-permute-start | bytes 36872 | tf_op jit(solution)/shard_map/ppermute | solution.py:31
  20.2 44.9 %collective-permute-start.3 = (bf16[128,256]{1,0:T(8,128)(2,1)S(1)}, bf16[128,256]{1,0:T(8,128)(2,1)S(1)}, u32[]{:S(2)}, u32[]{:S(2)}) collective-permute-start(bf16[128,256]{1,0:T(8,128)(2,1)S(1)} %get-tuple-element.151), channel_id=1, source_target_pairs={{0,1},{1,0},{2,3},{3,2},{4,5},{5,4},{6,7},{7,6},{8,9},{9,8},{10,11... | collective-permute-start | bytes 196616 | tf_op jit(solution)/shard_map/ppermute | solution.py:31
  69.4 19.0 %collective-permute-start.18 = (bf16[256,2048]{1,0:T(8,128)(2,1)S(1)}, bf16[256,2048]{1,0:T(8,128)(2,1)S(1)}, u32[]{:S(2)}, u32[]{:S(2)}) collective-permute-start(bf16[256,2048]{1,0:T(8,128)(2,1)S(1)} %shard_map.268.refs_4_), channel_id=1, source_target_pairs={{0,1},{1,0},{2,3},{3,2},{4,5},{5,4},{6,7},{7,6},{8,9},{9,8},{10,11... | collective-permute-start | bytes 3145736 | tf_op jit(solution)/shard_map/ppermute | solution.py:31
  69.9 29.5 %collective-permute-start.20 = (bf16[256,2048]{1,0:T(8,128)(2,1)S(1)}, bf16[256,2048]{1,0:T(8,128)(2,1)S(1)}, u32[]{:S(2)}, u32[]{:S(2)}) collective-permute-start(bf16[256,2048]{1,0:T(8,128)(2,1)S(1)} %collective-permute-done.19.refs_6_), channel_id=1, source_target_pairs={{0,1},{1,0},{2,3},{3,2},{4,5},{5,4},{6,7},{7,6},{8,9},{9,8},{10,11... | collective-permute-start | bytes 3145736 | tf_op jit(solution)/shard_map/ppermute | solution.py:31
  71.1 17.2 %collective-permute-start.28 = (bf16[256,1024]{1,0:T(8,128)(2,1)S(1)}, bf16[256,1024]{1,0:T(8,128)(2,1)S(1)}, u32[]{:S(2)}, u32[]{:S(2)}) collective-permute-start(bf16[256,1024]{1,0:T(8,128)(2,1)S(1)} %shard_map.271.refs_4_), channel_id=1, source_target_pairs={{0,2},{1,3},{2,0},{3,1},{4,6},{5,7},{6,4},{7,5},{8,10},{9,11},{10,... | collective-permute-start | bytes 1572872 | tf_op jit(solution)/shard_map/ppermute | solution.py:31
  85.7 72.0 %collective-permute-start.36 = (bf16[256,2048]{1,0:T(8,128)(2,1)S(1)}, bf16[256,2048]{1,0:T(8,128)(2,1)S(1)}, u32[]{:S(2)}, u32[]{:S(2)}) collective-permute-start(bf16[256,2048]{1,0:T(8,128)(2,1)S(1)} %shard_map.274.refs_4_), channel_id=1, source_target_pairs={{0,1},{1,0},{2,3},{3,2},{4,5},{5,4},{6,7},{7,6},{8,9},{9,8},{10,11... | collective-permute-start | bytes 3145736 | tf_op jit(solution)/shard_map/ppermute | solution.py:31
  88.1 70.1 %collective-permute-start.38 = (bf16[256,2048]{1,0:T(8,128)(2,1)S(1)}, bf16[256,2048]{1,0:T(8,128)(2,1)S(1)}, u32[]{:S(2)}, u32[]{:S(2)}) collective-permute-start(bf16[256,2048]{1,0:T(8,128)(2,1)S(1)} %collective-permute-done.37.refs_6_), channel_id=1, source_target_pairs={{0,1},{1,0},{2,3},{3,2},{4,5},{5,4},{6,7},{7,6},{8,9},{9,8},{10,11... | collective-permute-start | bytes 3145736 | tf_op jit(solution)/shard_map/ppermute | solution.py:31
  88.4 8.8 %collective-permute-start.16 = (bf16[32,1024]{1,0:T(8,128)(2,1)S(1)}, bf16[32,1024]{1,0:T(8,128)(2,1)S(1)}, u32[]{:S(2)}, u32[]{:S(2)}) collective-permute-start(bf16[32,1024]{1,0:T(8,128)(2,1)S(1)} %get-tuple-element.167.refs_0_), channel_id=1, source_target_pairs={{0,8},{4,12},{8,0},{12,4},{1,9},{5,13},{9,1},{13,5},{2,10},{6,14},... | collective-permute-start | bytes 196616 | tf_op jit(solution)/shard_map/ppermute | solution.py:31
  97.2 32.0 %collective-permute-start.27 = (bf16[256,1024]{1,0:T(8,128)(2,1)S(1)}, bf16[256,1024]{1,0:T(8,128)(2,1)S(1)}, u32[]{:S(2)}, u32[]{:S(2)}) collective-permute-start(bf16[256,1024]{1,0:T(8,128)(2,1)S(1)} %shard_map.271.refs_4_), channel_id=1, source_target_pairs={{0,1},{1,0},{2,3},{3,2},{4,5},{5,4},{6,7},{7,6},{8,9},{9,8},{10,11... | collective-permute-start | bytes 1572872 | tf_op jit(solution)/shard_map/ppermute | solution.py:31
  99.5 32.5 %collective-permute-start.29 = (bf16[256,1024]{1,0:T(8,128)(2,1)S(1)}, bf16[256,1024]{1,0:T(8,128)(2,1)S(1)}, u32[]{:S(2)}, u32[]{:S(2)}) collective-permute-start(bf16[256,1024]{1,0:T(8,128)(2,1)S(1)} %collective-permute-done.28.refs_6_), channel_id=1, source_target_pairs={{0,1},{1,0},{2,3},{3,2},{4,5},{5,4},{6,7},{7,6},{8,9},{9,8},{10,11... | collective-permute-start | bytes 1572872 | tf_op jit(solution)/shard_map/ppermute | solution.py:31
  140.1 17.6 %collective-permute-start.82 = (bf16[128,768]{1,0:T(8,128)(2,1)S(1)}, bf16[128,768]{1,0:T(8,128)(2,1)S(1)}, u32[]{:S(2)}, u32[]{:S(2)}) collective-permute-start(bf16[128,768]{1,0:T(8,128)(2,1)S(1)} %get-tuple-element.245), channel_id=1, source_target_pairs={{0,2},{1,3},{2,0},{3,1},{4,6},{5,7},{6,4},{7,5},{8,10},{9,11},{10,... | collective-permute-start | bytes 589832 | tf_op jit(solution)/shard_map/ppermute | solution.py:31
  144.6 11.3 %collective-permute-start.113 = (bf16[128,512]{1,0:T(8,128)(2,1)S(1)}, bf16[128,512]{1,0:T(8,128)(2,1)S(1)}, u32[]{:S(2)}, u32[]{:S(2)}) collective-permute-start(bf16[128,512]{1,0:T(8,128)(2,1)S(1)} %get-tuple-element.283), channel_id=1, source_target_pairs={{0,2},{1,3},{2,0},{3,1},{4,6},{5,7},{6,4},{7,5},{8,10},{9,11},{10,... | collective-permute-start | bytes 393224 | tf_op jit(solution)/shard_map/ppermute | solution.py:31
  157.7 25.8 %collective-permute-start.75 = (bf16[128,1280]{1,0:T(8,128)(2,1)S(1)}, bf16[128,1280]{1,0:T(8,128)(2,1)S(1)}, u32[]{:S(2)}, u32[]{:S(2)}) collective-permute-start(bf16[128,1280]{1,0:T(8,128)(2,1)S(1)} %get-tuple-element.240), channel_id=1, source_target_pairs={{0,1},{1,0},{2,3},{3,2},{4,5},{5,4},{6,7},{7,6},{8,9},{9,8},{10,11... | collective-permute-start | bytes 983048 | tf_op jit(solution)/shard_map/ppermute | solution.py:31
  157.7 10.2 %collective-permute-start.114 = (bf16[128,512]{1,0:T(8,128)(2,1)S(1)}, bf16[128,512]{1,0:T(8,128)(2,1)S(1)}, u32[]{:S(2)}, u32[]{:S(2)}) collective-permute-start(bf16[128,512]{1,0:T(8,128)(2,1)S(1)} %collective-permute-done.113.refs_6_), channel_id=1, source_target_pairs={{0,1},{1,0},{2,3},{3,2},{4,5},{5,4},{6,7},{7,6},{8,9},{9,8},{10,11... | collective-permute-start | bytes 393224 | tf_op jit(solution)/shard_map/ppermute | solution.py:31
  160.8 9.3 %collective-permute-start.81 = (bf16[128,512]{1,0:T(8,128)(2,1)S(1)}, bf16[128,512]{1,0:T(8,128)(2,1)S(1)}, u32[]{:S(2)}, u32[]{:S(2)}) collective-permute-start(bf16[128,512]{1,0:T(8,128)(2,1)S(1)} %get-tuple-element.244), channel_id=1, source_target_pairs={{0,1},{1,0},{2,3},{3,2},{4,5},{5,4},{6,7},{7,6},{8,9},{9,8},{10,11... | collective-permute-start | bytes 393224 | tf_op jit(solution)/shard_map/ppermute | solution.py:31
  164.3 16.5 %collective-permute-start.83 = (bf16[128,768]{1,0:T(8,128)(2,1)S(1)}, bf16[128,768]{1,0:T(8,128)(2,1)S(1)}, u32[]{:S(2)}, u32[]{:S(2)}) collective-permute-start(bf16[128,768]{1,0:T(8,128)(2,1)S(1)} %collective-permute-done.82.refs_2_), channel_id=1, source_target_pairs={{0,1},{1,0},{2,3},{3,2},{4,5},{5,4},{6,7},{7,6},{8,9},{9,8},{10,11... | collective-permute-start | bytes 589832 | tf_op jit(solution)/shard_map/ppermute | solution.py:31
  170.1 32.8 %collective-permute-start.76 = (bf16[128,1536]{1,0:T(8,128)(2,1)S(1)}, bf16[128,1536]{1,0:T(8,128)(2,1)S(1)}, u32[]{:S(2)}, u32[]{:S(2)}) collective-permute-start(bf16[128,1536]{1,0:T(8,128)(2,1)S(1)} %get-tuple-element.241), channel_id=1, source_target_pairs={{0,2},{1,3},{2,0},{3,1},{4,6},{5,7},{6,4},{7,5},{8,10},{9,11},{10,... | collective-permute-start | bytes 1179656 | tf_op jit(solution)/shard_map/ppermute | solution.py:31
  171.5 9.4 %collective-permute-start.93 = (bf16[128,512]{1,0:T(8,128)(2,1)S(1)}, bf16[128,512]{1,0:T(8,128)(2,1)S(1)}, u32[]{:S(2)}, u32[]{:S(2)}) collective-permute-start(bf16[128,512]{1,0:T(8,128)(2,1)S(1)} %get-tuple-element.253), channel_id=1, source_target_pairs={{0,1},{1,0},{2,3},{3,2},{4,5},{5,4},{6,7},{7,6},{8,9},{9,8},{10,11... | collective-permute-start | bytes 393224 | tf_op jit(solution)/shard_map/ppermute | solution.py:31
  180.5 15.5 %collective-permute-start.94 = (bf16[128,768]{1,0:T(8,128)(2,1)S(1)}, bf16[128,768]{1,0:T(8,128)(2,1)S(1)}, u32[]{:S(2)}, u32[]{:S(2)}) collective-permute-start(bf16[128,768]{1,0:T(8,128)(2,1)S(1)} %get-tuple-element.254), channel_id=1, source_target_pairs={{0,2},{1,3},{2,0},{3,1},{4,6},{5,7},{6,4},{7,5},{8,10},{9,11},{10,... | collective-permute-start | bytes 589832 | tf_op jit(solution)/shard_map/ppermute | solution.py:31
  193.8 8.2 %collective-permute-start.59 = (bf16[32,1024]{1,0:T(8,128)(2,1)S(1)}, bf16[32,1024]{1,0:T(8,128)(2,1)S(1)}, u32[]{:S(2)}, u32[]{:S(2)}) collective-permute-start(bf16[32,1024]{1,0:T(8,128)(2,1)S(1)} %get-tuple-element.212), channel_id=1, source_target_pairs={{0,12},{4,8},{8,4},{12,0},{1,13},{5,9},{9,5},{13,1},{2,14},{6,10},... | collective-permute-start | bytes 196616 | tf_op jit(solution)/shard_map/ppermute | solution.py:31
  195.9 26.4 %collective-permute-start.90 = (bf16[128,1024]{1,0:T(8,128)(2,1)S(1)}, bf16[128,1024]{1,0:T(8,128)(2,1)S(1)}, u32[]{:S(2)}, u32[]{:S(2)}) collective-permute-start(bf16[128,1024]{1,0:T(8,128)(2,1)S(1)} %get-tuple-element.251.refs_4_), channel_id=1, source_target_pairs={{0,1},{1,0},{2,3},{3,2},{4,5},{5,4},{6,7},{7,6},{8,9},{9,8},{10,11... | collective-permute-start | bytes 786440 | tf_op jit(solution)/shard_map/ppermute | solution.py:31
  197.3 25.6 %collective-permute-start.91 = (bf16[128,1024]{1,0:T(8,128)(2,1)S(1)}, bf16[128,1024]{1,0:T(8,128)(2,1)S(1)}, u32[]{:S(2)}, u32[]{:S(2)}) collective-permute-start(bf16[128,1024]{1,0:T(8,128)(2,1)S(1)} %get-tuple-element.251.refs_4_), channel_id=1, source_target_pairs={{0,2},{1,3},{2,0},{3,1},{4,6},{5,7},{6,4},{7,5},{8,10},{9,11},{10,... | collective-permute-start | bytes 786440 | tf_op jit(solution)/shard_map/ppermute | solution.py:31
  204.5 29.0 %collective-permute-start.87 = (bf16[128,1280]{1,0:T(8,128)(2,1)S(1)}, bf16[128,1280]{1,0:T(8,128)(2,1)S(1)}, u32[]{:S(2)}, u32[]{:S(2)}) collective-permute-start(bf16[128,1280]{1,0:T(8,128)(2,1)S(1)} %get-tuple-element.249), channel_id=1, source_target_pairs={{0,1},{1,0},{2,3},{3,2},{4,5},{5,4},{6,7},{7,6},{8,9},{9,8},{10,11... | collective-permute-start | bytes 983048 | tf_op jit(solution)/shard_map/ppermute | solution.py:31
  207.8 8.4 %collective-permute-start.61 = (bf16[32,1024]{1,0:T(8,128)(2,1)S(1)}, bf16[32,1024]{1,0:T(8,128)(2,1)S(1)}, u32[]{:S(2)}, u32[]{:S(2)}) collective-permute-start(bf16[32,1024]{1,0:T(8,128)(2,1)S(1)} %get-tuple-element.215.refs_0_), channel_id=1, source_target_pairs={{0,8},{4,12},{8,0},{12,4},{1,9},{5,13},{9,1},{13,5},{2,10},{6,14},... | collective-permute-start | bytes 196616 | tf_op jit(solution)/shard_map/ppermute | solution.py:31
  208.6 7.6 %collective-permute-start.62 = (bf16[32,1024]{1,0:T(8,128)(2,1)S(1)}, bf16[32,1024]{1,0:T(8,128)(2,1)S(1)}, u32[]{:S(2)}, u32[]{:S(2)}) collective-permute-start(bf16[32,1024]{1,0:T(8,128)(2,1)S(1)} %get-tuple-element.215.refs_0_), channel_id=1, source_target_pairs={{0,12},{4,8},{8,4},{12,0},{1,13},{5,9},{9,5},{13,1},{2,14},{6,10},... | collective-permute-start | bytes 196616 | tf_op jit(solution)/shard_map/ppermute | solution.py:31
  216.2 17.2 %collective-permute-start.95 = (bf16[128,768]{1,0:T(8,128)(2,1)S(1)}, bf16[128,768]{1,0:T(8,128)(2,1)S(1)}, u32[]{:S(2)}, u32[]{:S(2)}) collective-permute-start(bf16[128,768]{1,0:T(8,128)(2,1)S(1)} %collective-permute-done.94.refs_2_), channel_id=1, source_target_pairs={{0,1},{1,0},{2,3},{3,2},{4,5},{5,4},{6,7},{7,6},{8,9},{9,8},{10,11... | collective-permute-start | bytes 589832 | tf_op jit(solution)/shard_map/ppermute | solution.py:31
  222.3 26.4 %collective-permute-start.88 = (bf16[128,1536]{1,0:T(8,128)(2,1)S(1)}, bf16[128,1536]{1,0:T(8,128)(2,1)S(1)}, u32[]{:S(2)}, u32[]{:S(2)}) collective-permute-start(bf16[128,1536]{1,0:T(8,128)(2,1)S(1)} %get-tuple-element.250), channel_id=1, source_target_pairs={{0,2},{1,3},{2,0},{3,1},{4,6},{5,7},{6,4},{7,5},{8,10},{9,11},{10,... | collective-permute-start | bytes 1179656 | tf_op jit(solution)/shard_map/ppermute | solution.py:31
  232.7 18.0 %collective-permute-start.97 = (bf16[128,1280]{1,0:T(8,128)(2,1)S(1)}, bf16[128,1280]{1,0:T(8,128)(2,1)S(1)}, u32[]{:S(2)}, u32[]{:S(2)}) collective-permute-start(bf16[128,1280]{1,0:T(8,128)(2,1)S(1)} %get-tuple-element.257), channel_id=1, source_target_pairs={{0,2},{1,3},{2,0},{3,1},{4,6},{5,7},{6,4},{7,5},{8,10},{9,11},{10,... | collective-permute-start | bytes 983048 | tf_op jit(solution)/shard_map/ppermute | solution.py:31
  233.4 15.4 %collective-permute-start.96 = (bf16[128,1024]{1,0:T(8,128)(2,1)S(1)}, bf16[128,1024]{1,0:T(8,128)(2,1)S(1)}, u32[]{:S(2)}, u32[]{:S(2)}) collective-permute-start(bf16[128,1024]{1,0:T(8,128)(2,1)S(1)} %get-tuple-element.256), channel_id=1, source_target_pairs={{0,1},{1,0},{2,3},{3,2},{4,5},{5,4},{6,7},{7,6},{8,9},{9,8},{10,11... | collective-permute-start | bytes 786440 | tf_op jit(solution)/shard_map/ppermute | solution.py:31
  233.6 7.5 %collective-permute-start.67 = (bf16[32,1024]{1,0:T(8,128)(2,1)S(1)}, bf16[32,1024]{1,0:T(8,128)(2,1)S(1)}, u32[]{:S(2)}, u32[]{:S(2)}) collective-permute-start(bf16[32,1024]{1,0:T(8,128)(2,1)S(1)} %get-tuple-element.221.refs_0_), channel_id=1, source_target_pairs={{0,8},{4,12},{8,0},{12,4},{1,9},{5,13},{9,1},{13,5},{2,10},{6,14},... | collective-permute-start | bytes 196616 | tf_op jit(solution)/shard_map/ppermute | solution.py:31
  241.1 13.9 %collective-permute-start.77 = (bf16[128,1536]{1,0:T(8,128)(2,1)S(1)}, bf16[128,1536]{1,0:T(8,128)(2,1)S(1)}, u32[]{:S(2)}, u32[]{:S(2)}) collective-permute-start(bf16[128,1536]{1,0:T(8,128)(2,1)S(1)} %collective-permute-done.76.refs_2_), channel_id=1, source_target_pairs={{0,1},{1,0},{2,3},{3,2},{4,5},{5,4},{6,7},{7,6},{8,9},{9,8},{10,11... | collective-permute-start | bytes 1179656 | tf_op jit(solution)/shard_map/ppermute | solution.py:31
  253.8 9.2 %collective-permute-start.79 = (bf16[128,1024]{1,0:T(8,128)(2,1)S(1)}, bf16[128,1024]{1,0:T(8,128)(2,1)S(1)}, u32[]{:S(2)}, u32[]{:S(2)}) collective-permute-start(bf16[128,1024]{1,0:T(8,128)(2,1)S(1)} %get-tuple-element.242.refs_4_), channel_id=1, source_target_pairs={{0,2},{1,3},{2,0},{3,1},{4,6},{5,7},{6,4},{7,5},{8,10},{9,11},{10,... | collective-permute-start | bytes 786440 | tf_op jit(solution)/shard_map/ppermute | solution.py:31
  254.8 11.1 %collective-permute-start.98 = (bf16[128,1280]{1,0:T(8,128)(2,1)S(1)}, bf16[128,1280]{1,0:T(8,128)(2,1)S(1)}, u32[]{:S(2)}, u32[]{:S(2)}) collective-permute-start(bf16[128,1280]{1,0:T(8,128)(2,1)S(1)} %collective-permute-done.97.refs_6_), channel_id=1, source_target_pairs={{0,1},{1,0},{2,3},{3,2},{4,5},{5,4},{6,7},{7,6},{8,9},{9,8},{10,11... | collective-permute-start | bytes 983048 | tf_op jit(solution)/shard_map/ppermute | solution.py:31
  254.9 10.9 %collective-permute-start.103 = (bf16[128,512]{1,0:T(8,128)(2,1)S(1)}, bf16[128,512]{1,0:T(8,128)(2,1)S(1)}, u32[]{:S(2)}, u32[]{:S(2)}) collective-permute-start(bf16[128,512]{1,0:T(8,128)(2,1)S(1)} %get-tuple-element.270), channel_id=1, source_target_pairs={{0,2},{1,3},{2,0},{3,1},{4,6},{5,7},{6,4},{7,5},{8,10},{9,11},{10,... | collective-permute-start | bytes 393224 | tf_op jit(solution)/shard_map/ppermute | solution.py:31
  256.0 16.6 %collective-permute-start.89 = (bf16[128,1536]{1,0:T(8,128)(2,1)S(1)}, bf16[128,1536]{1,0:T(8,128)(2,1)S(1)}, u32[]{:S(2)}, u32[]{:S(2)}) collective-permute-start(bf16[128,1536]{1,0:T(8,128)(2,1)S(1)} %collective-permute-done.88.refs_2_), channel_id=1, source_target_pairs={{0,1},{1,0},{2,3},{3,2},{4,5},{5,4},{6,7},{7,6},{8,9},{9,8},{10,11... | collective-permute-start | bytes 1179656 | tf_op jit(solution)/shard_map/ppermute | solution.py:31
  256.2 15.9 %collective-permute-start.85 = (bf16[128,768]{1,0:T(8,128)(2,1)S(1)}, bf16[128,768]{1,0:T(8,128)(2,1)S(1)}, u32[]{:S(2)}, u32[]{:S(2)}) collective-permute-start(bf16[128,768]{1,0:T(8,128)(2,1)S(1)} %get-tuple-element.246.refs_4_), channel_id=1, source_target_pairs={{0,2},{1,3},{2,0},{3,1},{4,6},{5,7},{6,4},{7,5},{8,10},{9,11},{10,... | collective-permute-start | bytes 589832 | tf_op jit(solution)/shard_map/ppermute | solution.py:31
  268.3 24.7 %collective-permute-start.101 = (bf16[256,1024]{1,0:T(8,128)(2,1)S(1)}, bf16[256,1024]{1,0:T(8,128)(2,1)S(1)}, u32[]{:S(2)}, u32[]{:S(2)}) collective-permute-start(bf16[256,1024]{1,0:T(8,128)(2,1)S(1)} %get-tuple-element.264.own_ref), channel_id=1, source_target_pairs={{0,16},{16,0},{1,17},{17,1},{2,18},{18,2},{3,19},{19,3},{4,20},{20... | collective-permute-start | bytes 1572872 | tf_op jit(solution)/shard_map/ppermute | solution.py:31
  273.5 20.3 %collective-permute-start.107 = (bf16[256,1024]{1,0:T(8,128)(2,1)S(1)}, bf16[256,1024]{1,0:T(8,128)(2,1)S(1)}, u32[]{:S(2)}, u32[]{:S(2)}) collective-permute-start(bf16[256,1024]{1,0:T(8,128)(2,1)S(1)} %get-tuple-element.276.own_ref), channel_id=1, source_target_pairs={{0,16},{16,0},{1,17},{17,1},{2,18},{18,2},{3,19},{19,3},{4,20},{20... | collective-permute-start | bytes 1572872 | tf_op jit(solution)/shard_map/ppermute | solution.py:31
  277.2 14.3 %collective-permute-start.99 = (f32[32,256]{1,0:T(8,128)S(1)}, f32[32,256]{1,0:T(8,128)S(1)}, u32[]{:S(2)}, u32[]{:S(2)}) collective-permute-start(f32[32,256]{1,0:T(8,128)S(1)} %get-tuple-element.260.own_ref), channel_id=1, source_target_pairs={{0,16},{16,0},{1,17},{17,1},{2,18},{18,2},{3,19},{19,3},{4,20},{20... | collective-permute-start | bytes 98312 | tf_op jit(solution)/shard_map/ppermute | solution.py:31
  278.2 24.6 %collective-permute-start.115 = (bf16[256,1024]{1,0:T(8,128)(2,1)S(1)}, bf16[256,1024]{1,0:T(8,128)(2,1)S(1)}, u32[]{:S(2)}, u32[]{:S(2)}) collective-permute-start(bf16[256,1024]{1,0:T(8,128)(2,1)S(1)} %shard_map.303.own_ref), channel_id=1, source_target_pairs={{0,16},{16,0},{1,17},{17,1},{2,18},{18,2},{3,19},{19,3},{4,20},{20... | collective-permute-start | bytes 1572872 | tf_op jit(solution)/shard_map/ppermute | solution.py:31
  280.3 55.3 %collective-permute-start.106 = (bf16[256,1024]{1,0:T(8,128)(2,1)S(1)}, bf16[256,1024]{1,0:T(8,128)(2,1)S(1)}, u32[]{:S(2)}, u32[]{:S(2)}) collective-permute-start(bf16[256,1024]{1,0:T(8,128)(2,1)S(1)} %get-tuple-element.275.own_ref), channel_id=1, source_target_pairs={{0,16},{16,0},{1,17},{17,1},{2,18},{18,2},{3,19},{19,3},{4,20},{20... | collective-permute-start | bytes 1572872 | tf_op jit(solution)/shard_map/ppermute | solution.py:31
  291.5 45.1 %collective-permute-start.111 = (bf16[256,1024]{1,0:T(8,128)(2,1)S(1)}, bf16[256,1024]{1,0:T(8,128)(2,1)S(1)}, u32[]{:S(2)}, u32[]{:S(2)}) collective-permute-start(bf16[256,1024]{1,0:T(8,128)(2,1)S(1)} %shard_map.302.own_ref), channel_id=1, source_target_pairs={{0,16},{16,0},{1,17},{17,1},{2,18},{18,2},{3,19},{19,3},{4,20},{20... | collective-permute-start | bytes 1572872 | tf_op jit(solution)/shard_map/ppermute | solution.py:31
  293.0 40.4 %collective-permute-start.100 = (bf16[256,768]{1,0:T(8,128)(2,1)S(1)}, bf16[256,768]{1,0:T(8,128)(2,1)S(1)}, u32[]{:S(2)}, u32[]{:S(2)}) collective-permute-start(bf16[256,768]{1,0:T(8,128)(2,1)S(1)} %get-tuple-element.263.own_ref), channel_id=1, source_target_pairs={{0,16},{16,0},{1,17},{17,1},{2,18},{18,2},{3,19},{19,3},{4,20},{20... | collective-permute-start | bytes 1179656 | tf_op jit(solution)/shard_map/ppermute | solution.py:31
  293.8 41.0 %collective-permute-start.105 = (bf16[256,256]{1,0:T(8,128)(2,1)S(1)}, bf16[256,256]{1,0:T(8,128)(2,1)S(1)}, u32[]{:S(2)}, u32[]{:S(2)}) collective-permute-start(bf16[256,256]{1,0:T(8,128)(2,1)S(1)} %shard_map.297.own_ref), channel_id=1, source_target_pairs={{0,16},{16,0},{1,17},{17,1},{2,18},{18,2},{3,19},{19,3},{4,20},{20... | collective-permute-start | bytes 393224 | tf_op jit(solution)/shard_map/ppermute | solution.py:31
  (70 other events, 422.6 us)
